TPU v7x, 32 devices: a whole 2x2x4 slice. The times are simulated.
32 devices in a mesh: pair: 16 (over z, y, x), vtile: 1, irrep: 2 (over core).
Axes of the slice: x: 2, y: 2, z: 4, core: 2. Of those that a mesh axis runs over, the one named last changes fastest.
Arguments:
- amplitudes: bfloat16 [80, 8, 7744], P('pair'), may hold values from -4 to 4
- slabs: bfloat16 [16, 8, 2, 88, 7744], P('pair', 'vtile', 'irrep'), may hold values from -1.5 to 1.5
- couplings: bfloat16 [2, 30, 30, 176], P(None, None, None, 'irrep'), may hold values from -6 to 6
- occ_energy: float32 [30], replicated, may hold values from -2 to -0.3
- vir_energy: float32 [8, 88], replicated, may hold values from 0.2 to 4
- occ_irrep: int32 [30], replicated, may hold values from 0 to 7
- pair_i: int32 [80], P('pair'), may hold values from 0 to 29, as said below
- pair_j: int32 [80], P('pair'), may hold values from 0 to 29, as said below
- window_k: int32 [2], replicated, may hold values from 0 to 29
- owner: int32 [2], replicated, may hold values from 0 to 15
Outputs:
- resid_part: float32 [80, 8, 7744], P('pair', 'vtile', 'irrep')
Inputs may be any that keep to these rules, and one draw needn't show every extreme that they name: Pairs come in groups of 16 that share pair_i; groups have different pair_i. Within a group of pairs sharing pair_i, pair_j values are distinct.
All inputs are finite; a program needn't handle non-finite values.
Results may differ from a plain program's by a relative error of at most 0.0003.
Values may be sent and summed in bfloat16 or wider, within the bound.
No kernel may reach another device: no remote copies, remote signals or barrier semaphores. Data moves between devices by JAX's collectives and lax.ppermute only.
A program may use at most 256 MiB of HBM per device.

v0:
```python
import functools
import math

import jax
import jax.numpy as jnp
from jax import lax
from jax.experimental import pallas as pl
from jax.experimental.pallas import tpu as pltpu
from jax.sharding import PartitionSpec as P


K_WIN = 2


def spread_2(shard, axis, root):
    mine = lax.axis_index(axis) == root
    return lax.psum(jnp.where(mine, shard, jnp.zeros_like(shard)), axis)


def on_device_gather(
    amplitudes, slabs, couplings, occ_energy, vir_energy, occ_irrep, pair_i, pair_j, window_k, owner
):
    tile_blocks = slabs.shape[1]
    block_size = slabs.shape[3]
    block_area = block_size * block_size
    occ_count = occ_irrep.shape[0]
    local_pairs = amplitudes.shape[0]
    tile_index = lax.axis_index("vtile")
    gamma_irrep = lax.axis_index("irrep")
    beta_irreps = tile_index * tile_blocks + jnp.arange(tile_blocks, dtype=jnp.int32)
    pair_sym = jnp.bitwise_xor(occ_irrep[pair_i], occ_irrep[pair_j])
    send_index = jnp.bitwise_xor(beta_irreps[None, :], pair_sym[:, None])
    outgoing = jnp.take_along_axis(amplitudes, send_index[:, :, None], axis=1)
    local_slab = slabs[0, :, 0]
    gamma_energy = jnp.take(vir_energy, gamma_irrep, axis=0)
    beta_energy = vir_energy[beta_irreps]
    occ_keep = jnp.bitwise_xor(occ_irrep, gamma_irrep)

    def pair_term(amp_pair, occ_i, occ_j, hole_part, slab_data, k_irrep, k_energy):
        pair_irrep = jnp.bitwise_xor(occ_irrep[occ_i], occ_irrep[occ_j])
        alpha_irrep = jnp.bitwise_xor(
            jnp.bitwise_xor(pair_irrep, k_irrep), jnp.bitwise_xor(beta_irreps, gamma_irrep)
        )
        amp_sel = amp_pair[alpha_irrep].reshape(tile_blocks, block_size, block_size)
        particle = jnp.einsum(
            "mad,mdx->max", amp_sel, slab_data, preferred_element_type=jnp.float32
        )
        energy_a = vir_energy[alpha_irrep]
        base = occ_energy[occ_i] + occ_energy[occ_j] + k_energy
        denominator = (
            energy_a[:, :, None, None]
            + beta_energy[:, None, :, None]
            + gamma_energy[None, None, None, :]
            - base
        )
        triples = (
            (particle - hole_part) / denominator.reshape(tile_blocks, block_size, block_area)
        ).astype(jnp.bfloat16)
        contrib = jnp.einsum("max,mdx->mad", triples, slab_data, preferred_element_type=jnp.float32)
        return (
            jnp.zeros((8, block_area), jnp.float32)
            .at[alpha_irrep]
            .add(contrib.reshape(tile_blocks, block_area))
        )

    def coupling_rows(window, occ_j, k_irrep):
        y_column = jnp.take(couplings[window], occ_j, axis=1)
        keep_mask = jnp.bitwise_xor(occ_keep, jnp.bitwise_xor(occ_irrep[occ_j], k_irrep)) == 0
        return y_column.astype(jnp.float32) * keep_mask[:, None].astype(jnp.float32)

    empty_stash = jnp.zeros((local_pairs, occ_count, tile_blocks, block_area), jnp.bfloat16)
    empty_seen = jnp.zeros((local_pairs, occ_count), jnp.float32)
    stash = empty_stash
    seen = empty_seen
    piece_amp = lax.all_gather(outgoing, "pair", axis=0, tiled=True)
    piece_first = lax.all_gather(pair_i, "pair", axis=0, tiled=True)
    piece_second = lax.all_gather(pair_j, "pair", axis=0, tiled=True)
    match = piece_first[None, :] == pair_i[:, None]
    slot = jnp.where(match, piece_second[None, :], occ_count).astype(jnp.int32)
    row_index = jnp.broadcast_to(jnp.arange(local_pairs, dtype=jnp.int32)[:, None], slot.shape)
    spread = jnp.broadcast_to(piece_amp[None], (local_pairs,) + piece_amp.shape)
    stash = stash.at[row_index, slot].add(spread, mode="drop")
    seen = seen.at[row_index, slot].add(jnp.ones(slot.shape, jnp.float32), mode="drop")
    accumulated = jnp.zeros((local_pairs, 8, block_area), jnp.float32)
    for window in range(K_WIN):
        slab_data = spread_2(local_slab, "pair", owner[window])
        k_index = window_k[window]
        k_irrep = occ_irrep[k_index]
        k_energy = occ_energy[k_index]

        def folded_step(packed):
            amp_pair, occ_i, occ_j, slot_amp, slot_seen = packed
            coef_rows = coupling_rows(window, occ_j, k_irrep)
            coupling = (coef_rows * slot_seen[:, None]).astype(jnp.bfloat16)
            hole_part = jnp.einsum(
                "qmx,qc->mxc", slot_amp, coupling, preferred_element_type=jnp.float32
            )
            hole_part = hole_part.reshape(tile_blocks, block_size, block_area)
            return pair_term(amp_pair, occ_i, occ_j, hole_part, slab_data, k_irrep, k_energy)

        contrib_all = lax.map(folded_step, (amplitudes, pair_i, pair_j, stash, seen))
        accumulated = accumulated + contrib_all
    summed = lax.psum(accumulated, ("vtile", "irrep"))
    irrep_count = lax.axis_size("irrep")
    share = block_area // irrep_count
    summed = lax.dynamic_slice_in_dim(summed, tile_index * tile_blocks, tile_blocks, 1)
    return lax.dynamic_slice_in_dim(summed, gamma_irrep * share, share, 2)


GROUP = 16
LANE = 128
TILE = 256
STEP = 8


def tile_plan(rows):
    lanes = -(-GROUP * rows // TILE) * TILE
    depth = LANE // GROUP
    starts = []
    for first in range(0, lanes, TILE):
        lowest = min(first // rows, GROUP - depth)
        highest = min((first + TILE - 1) // rows, GROUP - 1)
        assert lowest >= 0 and highest < lowest + depth
        starts.append(lowest)
    return lanes, depth, starts


def b_chunks(block):
    unit = LANE // math.gcd(LANE, block)
    size = 2 * unit
    return [(first, min(size, block - first)) for first in range(0, block, size)]


def triples_kernel(last, *refs):
    eb_ref, vt_ref, v_ref, at_ref, arep_ref, ct_ref, mask_ref, ecol_ref, lrow_ref = refs[:9]
    o_ref, t_ref = refs[-2:]
    count, block = vt_ref.shape[1], vt_ref.shape[2]
    unroll = math.gcd(count, STEP)
    depth = mask_ref.shape[1] // GROUP
    tiles = mask_ref.shape[0]

    def some_b(step, carry):
        for tile in range(tiles):
            lanes = slice(tile * TILE, (tile + 1) * TILE)
            top = at_ref[0, :, lanes]
            for first in range(0, unroll, 2):
                results = []
                for b in (unroll * step + first, unroll * step + first + 1):
                    lhs = jnp.concatenate([vt_ref[0, b], ct_ref[0, 0, tile]], axis=1)
                    hole_amp = arep_ref[0, 0, b, :, lanes]
                    bottom = jnp.concatenate([hole_amp] * depth, axis=0) * mask_ref[tile]
                    rhs = jnp.concatenate([top, bottom], axis=0)
                    numer = jnp.dot(lhs, rhs, preferred_element_type=jnp.float32)
                    denom = (ecol_ref[...] + eb_ref[0, b]) + lrow_ref[0, 0, :, lanes]
                    results.append(numer / denom)
                start = pl.multiple_of((unroll * step + first) * block, 2 * block)
                t_ref[pl.ds(start, 2 * block), lanes] = jnp.concatenate(results, axis=0).astype(jnp.bfloat16)
        return carry

    lax.fori_loop(0, count // unroll, some_b, 0)

    def finish(tile, carry):
        lanes = pl.ds(pl.multiple_of(tile * TILE, TILE), TILE)
        contrib = jnp.dot(v_ref[0], t_ref[:, lanes], preferred_element_type=jnp.float32)
        if len(refs) == 12:
            contrib = contrib + refs[9][0, :, lanes]
        if last:
            o_ref[0, lanes, :] = contrib.T
        else:
            o_ref[0, :, lanes] = contrib
        return carry

    lax.fori_loop(0, tiles, finish, 0)


def triples_call(window, last, eb, vt, v, at, arep, ct, mask, ecol, lrow, total=None):
    _, count, block, _ = vt.shape
    groups, depth_rows, lanes = at.shape
    w = window
    tall, wide = pl.BlockSpec((1, lanes, block), lambda g: (g, 0, 0)), pl.BlockSpec((1, block, lanes), lambda g: (g, 0, 0))
    in_specs = [
        pl.BlockSpec(memory_space=pltpu.SMEM),
        pl.BlockSpec((1, count, block, LANE), lambda g: (w, 0, 0, 0)),
        pl.BlockSpec((1, block, count * block), lambda g: (w, 0, 0)),
        pl.BlockSpec((1, depth_rows, lanes), lambda g: (g, 0, 0)),
        pl.BlockSpec((1, 1, count, GROUP, lanes), lambda g: (w, g, 0, 0, 0)),
        pl.BlockSpec((1, 1) + ct.shape[2:], lambda g: (w, g, 0, 0, 0)),
        pl.BlockSpec(mask.shape, lambda g: (0, 0, 0)),
        pl.BlockSpec(ecol.shape, lambda g: (0, 0)),
        pl.BlockSpec((1, 1, 1, lanes), lambda g: (w, g, 0, 0)),
    ]
    operands = [eb[w : w + 1], vt, v, at, arep, ct, mask, ecol, lrow]
    if total is not None:
        in_specs.append(wide)
        operands.append(total)
    shape = (groups, lanes, block) if last else (groups, block, lanes)
    return pl.pallas_call(
        functools.partial(triples_kernel, last),
        grid=(groups,),
        in_specs=in_specs,
        out_specs=tall if last else wide,
        out_shape=jax.ShapeDtypeStruct(shape, jnp.float32),
        scratch_shapes=[pltpu.VMEM((count * block, lanes), jnp.bfloat16)],
        compiler_params=pltpu.CompilerParams(
            dimension_semantics=("arbitrary",), vmem_limit_bytes=40 * 1024 * 1024
        ),
        cost_estimate=pl.CostEstimate(
            flops=groups * count * block * lanes * 2 * (TILE + block) * 4,
            bytes_accessed=(arep.size + vt.size + v.size) * 2,
            transcendentals=groups * count * block * lanes,
        ),
        name="triples",
    )(*operands)


def swap_cores(x):
    return lax.ppermute(x, "irrep", [(0, 1), (1, 0)])


def across(x, bit):
    count = lax.axis_size("pair")
    return lax.ppermute(x, "pair", [(t, t ^ bit) for t in range(count)])


def pick(x, index):
    return lax.dynamic_index_in_dim(x, index, 0, keepdims=False)


def after(x, *others):
    return lax.optimization_barrier((x,) + others)[0]


class SlabPath:
    def __init__(self, owner, k_irrep, me, core):
        self.owner, self.k_irrep, self.core = owner, k_irrep, core
        self.windows = owner.shape[0]
        self.bits = [(me >> n) & 1 for n in range(4)]

    def from_here(self, bit):
        return ((self.owner >> bit) & 1) == self.bits[bit]

    def split_cores(self, slab):
        halves = slab.reshape((2, slab.shape[0] // 2) + slab.shape[1:])
        mine, theirs = pick(halves, self.core), swap_cores(pick(halves, 1 - self.core))
        same = self.bits[0] == self.core
        return jnp.where(same, mine, theirs), jnp.where(same, theirs, mine)

    def split_low(self, kept, came):
        def block(w, high, low):
            beta = (2 * high + low) ^ (self.k_irrep[w] & 3) ^ self.bits[0]
            return jnp.where(self.from_here(0)[w], pick(kept, beta), pick(came, beta))

        def blocks(low):
            return jnp.stack(
                [jnp.stack([block(w, high, low) for w in range(self.windows)]) for high in range(2)]
            )

        return blocks(self.bits[1]), blocks(1 - self.bits[1])

    def split_high(self, kept, came):
        here = self.from_here(1)[:, None, None]
        kept, leaving = [
            jnp.where(here, pick(kept, high), pick(came, high)) for high in (self.bits[2], 1 - self.bits[2])
        ]
        return kept, leaving

    def split_top(self, kept, came):
        blocks = jnp.where(self.from_here(2)[:, None, None], kept, came)
        mine, theirs = pick(blocks, self.core), swap_cores(pick(blocks, 1 - self.core))
        stays = (self.bits[3] ^ ((self.k_irrep[self.core] >> 2) & 1)) == self.core
        return jnp.where(stays, mine, theirs), jnp.where(stays, theirs, mine)

    def join(self, kept, came):
        block = jnp.where(self.from_here(3)[self.core], kept, came)
        other = swap_cores(block)
        first = self.core == 0
        return jnp.stack([jnp.where(first, block, other), jnp.where(first, other, block)])


def on_device_scatter(
    amplitudes, slabs, couplings, occ_energy, vir_energy, occ_irrep, pair_i, pair_j, window_k, owner
):
    betas, block = slabs.shape[1], slabs.shape[3]
    windows = window_k.shape[0]
    rows = block // lax.axis_size("irrep")
    share = rows * block
    chips = lax.axis_size("pair")
    local_pairs = pair_i.shape[0]
    pairs = chips * local_pairs
    groups = pairs // GROUP
    lanes, depth, starts = tile_plan(rows)
    me, core = lax.axis_index("pair"), lax.axis_index("irrep")
    gamma, m = me & 1, me >> 1
    k_irrep = occ_irrep[window_k]
    bf16 = jnp.bfloat16

    chunks = b_chunks(block)
    local = slabs[0, :, 0]
    path = SlabPath(owner, k_irrep, me, core)
    kept_x, sent_x = zip(
        *[path.split_cores(local[:, :, first * block : (first + size) * block]) for first, size in chunks]
    )
    x, leaving_x = [], []
    for leaving in sent_x:
        leaving_x.append(after(leaving, x[-1]) if x else leaving)
        x.append(across(leaving_x[-1], 1))
    kept_y, sent_y = [], []
    for kept, came in zip(kept_x, x):
        kept, leaving = path.split_low(kept, after(came, sent_y[-1]) if sent_y else came)
        kept_y.append(kept)
        sent_y.append(leaving)
    y = [across(leaving, 2) for leaving in sent_y]

    pair_sym = occ_irrep[pair_i] ^ occ_irrep[pair_j]
    mine = lax.dynamic_slice_in_dim(after(amplitudes, sent_x[0]), core * share, share, 2)
    target = jnp.arange(chips, dtype=jnp.int32)
    wanted = jnp.stack([target >> 1] + [(target >> 1) ^ (target & 1) ^ k_irrep[w] for w in range(windows)], 1)
    index = wanted[:, :, None] ^ pair_sym[None, None, :]
    kinds = 1 + windows
    labels = jnp.concatenate([pair_i, pair_j]).astype(bf16)
    labels = jnp.pad(labels, (0, share - labels.shape[0]))[None]
    stored = jnp.concatenate([mine.reshape(local_pairs * betas, share), labels], 0)
    index = index + betas * jnp.arange(local_pairs, dtype=jnp.int32)
    index = index.reshape(chips, kinds * local_pairs)
    index = jnp.pad(index, ((0, 0), (0, 1)), constant_values=local_pairs * betas).reshape(-1)
    chosen = (index[:, None] == jnp.arange(stored.shape[0], dtype=jnp.int32)[None, :]).astype(bf16)
    sent = jnp.einsum("rh,hx->rx", chosen, stored)
    sent = sent.reshape(chips, kinds * local_pairs + 1, share)
    came = lax.all_to_all(sent, "pair", 0, 0, tiled=True)
    came = after(came, sent_y[0], leaving_x[1])
    came = came.reshape(chips * (kinds * local_pairs + 1), share)
    label_rows = after(target, leaving_x[1]) * (kinds * local_pairs + 1) + kinds * local_pairs
    both = came[label_rows][:, : 2 * local_pairs].astype(jnp.int32).reshape(chips, 2, local_pairs)
    both = both.transpose(1, 0, 2).reshape(2, pairs)

    numbers = jnp.arange(pairs, dtype=jnp.int32)
    ahead = both[0][None, :] < both[0][:, None]
    tied = (both[0][None, :] == both[0][:, None]) & (numbers[None, :] < numbers[:, None])
    rank = jnp.sum((ahead | tied).astype(jnp.int32), axis=1)
    placed = (rank[None, :] == numbers[:, None]).astype(jnp.int32)
    order = jnp.sum(placed * numbers[None, :], axis=1)
    first = jnp.sum(placed * both[0][None, :], axis=1)
    second = jnp.sum(placed * both[1][None, :], axis=1)

    source = (order // local_pairs) * (kinds * local_pairs + 1) + order % local_pairs
    source = source[None, :] + local_pairs * jnp.arange(kinds, dtype=jnp.int32)[:, None]
    amps = came[source]
    amps = amps.reshape(kinds, groups, GROUP, rows, block)
    holes = amps[1:]
    used = GROUP * rows
    at = amps[0].transpose(0, 3, 1, 2).reshape(groups, block, used)
    at = jnp.pad(at, ((0, 0), (0, LANE - block), (0, lanes - used)))
    lane = jnp.arange(lanes, dtype=jnp.int32)
    spread = ((lane[None, :] % rows == jnp.arange(rows)[:, None]) & (lane < used)[None, :]).astype(bf16)
    lane_pair = lane // rows
    mask = jnp.stack([
        (jnp.repeat(start + jnp.arange(depth), GROUP)[:, None] == lane_pair[None, n * TILE : (n + 1) * TILE])
        for n, start in enumerate(starts)
    ]).astype(bf16)

    coupled = jnp.where(gamma == core, couplings, swap_cores(couplings))
    chosen = (second.reshape(groups, GROUP)[:, :, None] == jnp.arange(occ_irrep.shape[0])).astype(bf16)
    coupled = jnp.einsum("gql,wljc->wgqjc", chosen, coupled)
    coupled = jnp.einsum("gpj,wgqjc->wgcpq", chosen, coupled)
    sym_j = occ_irrep[second].reshape(groups, GROUP)
    keep = (sym_j[None, :, :, None] ^ sym_j[None, :, None, :] ^ gamma ^ k_irrep[:, None, None, None]) == 0
    coupled = -(coupled * keep[:, :, None].astype(bf16))
    ct = jnp.stack(
        [coupled[:, :, :, s : s + depth].reshape(windows, groups, block, depth * GROUP) for s in starts], 2
    )

    alpha = occ_irrep[first] ^ occ_irrep[second] ^ m
    energy_a = lax.dynamic_slice_in_dim(vir_energy, core * rows, rows, 1)[alpha]
    base = occ_energy[first] + occ_energy[second]
    lrow = energy_a[None] - (base[None] + occ_energy[window_k][:, None])[:, :, None]
    lrow = lrow.reshape(windows, groups, 1, used)
    lrow = jnp.pad(lrow, ((0, 0), (0, 0), (0, 0), (0, lanes - used)), constant_values=1.0)
    ecol = jnp.broadcast_to(pick(vir_energy, gamma)[:, None], (block, TILE))
    energy_b = vir_energy[m ^ gamma ^ k_irrep]

    eye = (jnp.arange(block)[:, None] == jnp.arange(LANE)[None, :]).astype(bf16)

    def spread_holes(chunk, *tokens):
        start, size = chunks[chunk]
        hole = after(holes[:, :, :, :, start : start + size], *tokens)
        return jnp.einsum("wgqab,ae->wgbqe", hole, spread)

    def run(chunk, w, v, total):
        start, size = chunks[chunk]
        vt = jnp.einsum("wdx,de->wxe", v, eye).reshape(windows, size, block, LANE)
        last = start + size == block and w == windows - 1
        energies = energy_b[:, start : start + size]
        return triples_call(w, last, energies, vt, v, at, areps[chunk], ct, mask, ecol, lrow, total)

    calls = [(chunk, w) for chunk in range(len(chunks)) for w in range(windows)]
    kept_z, sent_z, kept_h, sent_h, z, h, ready = {}, {}, {}, {}, {}, {}, {}

    def to_high(chunk, token=None):
        came_y = y[chunk] if token is None else after(y[chunk], token)
        kept_z[chunk], sent_z[chunk] = path.split_high(kept_y[chunk], came_y)
        z[chunk] = across(sent_z[chunk], 4)
        return sent_z[chunk]

    def to_top(chunk, token=None):
        came_z = z[chunk] if token is None else after(z[chunk], token)
        kept_h[chunk], sent_h[chunk] = path.split_top(kept_z[chunk], came_z)
        h[chunk] = across(sent_h[chunk], 8)
        return sent_h[chunk]

    def arrive(chunk, token=None):
        came_h = h[chunk] if token is None else after(h[chunk], token)
        ready[chunk] = path.join(kept_h[chunk], came_h)
        return ready[chunk]

    plan = {0: [(to_top, 1), (to_high, 2)], 1: [(arrive, 1), (to_top, 2)], 2: [(arrive, 2)]}
    to_high(0, amps)
    at = after(at, sent_z[0], sent_y[1], leaving_x[2])
    areps = [spread_holes(0, at)]
    to_top(0, areps[0])
    ct = after(ct, sent_h[0])
    arrive(0, ct)
    ready[0] = after(ready[0], to_high(1, sent_h[0]), sent_y[2])
    total = None
    for n, (chunk, w) in enumerate(calls):
        total = run(chunk, w, ready[chunk], total)
        issued = [move(number, total) for move, number in plan.get(n, [])]
        if n == 0:
            areps += [spread_holes(number, total) for number in range(1, len(chunks))]
        if issued:
            total = after(total, *issued)
    total = total[:, :used].reshape(pairs, share)[rank]
    cut = 8 if share % 8 == 0 else 1
    total = total.reshape(chips, local_pairs * cut, share // cut)
    came = lax.all_to_all(total, "pair", 0, 0, tiled=True)
    came = came.reshape(betas, 2, local_pairs, cut, share // cut)
    came = (came[:, 0] + came[:, 1]).reshape(betas, local_pairs, share)
    back = jnp.arange(betas, dtype=jnp.int32)[None, :] ^ pair_sym[:, None]
    return came[back, jnp.arange(local_pairs, dtype=jnp.int32)[:, None]]


def on_device(*args):
    betas, block = args[1].shape[1], args[1].shape[3]
    chips, cores = lax.axis_size("pair"), lax.axis_size("irrep")
    fits = lax.axis_size("vtile") == 1 and cores == 2 and betas == 8 and chips == betas * cores
    fits = fits and args[8].shape[0] == 2 and block % 2 == 0 and block < LANE
    if fits and args[5].shape[0] <= 256:
        return on_device_scatter(*args)
    return on_device_gather(*args)


def solution(mesh):
    placed = (
        P("pair", None, None),
        P("pair", "vtile", "irrep", None, None),
        P(None, None, None, "irrep"),
        P(),
        P(),
        P(),
        P("pair"),
        P("pair"),
        P(),
        P(),
    )
    return jax.shard_map(
        on_device,
        mesh=mesh,
        in_specs=placed,
        out_specs=P("pair", "vtile", "irrep"),
        check_vma=False,
    )
```

profile of v0, /device:TPU:12, one launch (start us, length us, event | category | flops | bytes accessed | tf_op | source)
XLA Modules:
  0.0 408.6 jit_solution(12004696114503428983)
XLA Ops:
  0.0 5.7 %fusion.88 = (bf16[8,88,2816]{2,1,0:T(8,128)(2,1)}, bf16[8,88,2816]{2,1,0:T(8,128)(2,1)}) fusion(bf16[8,88,7744]{2,1,0:T(8,128)(2,1)} %bitcast.227), kind=kLoop, calls=%fused_computation.239 | loop fusion | bytes 15859712 | tf_op jit(solution)/shard_map/slice | solution.py:301
  5.7 1.8 dynamic-slice_bitcast_fusion
  8.5 1.4 dynamic-slice_bitcast_fusion.1
  9.9 3.7 slice.219
  13.6 2.7 dynamic-slice_bitcast_fusion.2
  29.5 4.3 %bitcast_select_fusion = (bf16[4,88,2816]{2,1,0:T(8,128)(2,1)}, bf16[4,88,2816]{2,1,0:T(8,128)(2,1)}) fusion(bf16[4,88,2816]{2,1,0:T(8,128)(2,1)} %collective-permute-done.2, pred[]{:T(512)S(6)} %eq.290, bf16[2,4,88,2816]{3,2,1,0:T(8,128)(2,1)} %bitcast.226, s32[]{:T(128)S(6)} %select_n.527), kind=kLoop, calls=%fused_computation.27 | loop fusion | flops 1982464 | bytes 7929861 | tf_op jit(solution)/shard_map/jit(_where)/select_n | solution.py:246
  33.9 1.5 collective-permute-start.3
  35.5 2.1 fusion.37
  37.6 6.6 %all-to-all-start = ((bf16[16,16,3872]{2,1,0:T(8,128)(2,1)}), bf16[16,16,3872]{2,1,0:T(8,128)(2,1)S(1)}, u32[]{:S(2)}, u32[]{:S(2)}) async-start(bf16[16,16,3872]{2,1,0:T(8,128)(2,1)} %bitcast.229), calls=%async_computation | async-start | bytes 4063232 | tf_op jit(solution)/shard_map/all_to_all | solution.py:329
  44.2 1.3 fusion.35
  45.5 4.0 bitcast_select_fusion.5
  49.5 3.9 bitcast_select_fusion.2
  53.4 43.2 %collective-permute-done.3 = bf16[4,88,2816]{2,1,0:T(8,128)(2,1)} collective-permute-done((bf16[4,88,2816]{2,1,0:T(8,128)(2,1)}, bf16[4,88,2816]{2,1,0:T(8,128)(2,1)}, u32[]{:S(2)}, u32[]{:S(2)}) %collective-permute-start.3) | collective-permute-done | bytes 1982496 | tf_op jit(solution)/shard_map/ppermute | solution.py:222
  96.6 1.5 collective-permute-start.4
  98.1 4.1 %dynamic-slice_select_fusion.5 = (bf16[1,88,2816]{2,1,0:T(8,128)(2,1)S(1)}, bf16[1,88,2816]{2,1,0:T(8,128)(2,1)S(1)}, bf16[1,88,2816]{2,1,0:T(8,128)(2,1)S(1)}, ...) fusion(bf16[4,88,2816]{2,1,0:T(8,128)(2,1)} %collective-permute, ...), kind=kLoop, calls=%fused_computation.103 | loop fusion | flops 1982464 | bytes 11894818 | tf_op jit(solution)/shard_map/jit(_where)/select_n | solution.py:251
  102.4 1.6 pad_maximum_fusion
  104.3 1.5 maximum_bitcast_fusion.4
  107.2 1.2 gather_fusion.6
  108.5 1.2 gather_fusion.10
  112.4 3.0 gather_fusion.5
  116.6 1.7 squeeze.221
  118.7 1.4 copy.72
  120.1 4.0 slice.84
  124.3 1.5 convolution_bitcast_fusion.3
  129.4 1.9 slice.232
  133.0 2.9 fusion.89
  135.9 8.1 %collective-permute-done.4 = bf16[4,88,2816]{2,1,0:T(8,128)(2,1)} collective-permute-done((bf16[4,88,2816]{2,1,0:T(8,128)(2,1)}, bf16[4,88,2816]{2,1,0:T(8,128)(2,1)}, u32[]{:S(2)}, u32[]{:S(2)}) %collective-permute-start.4) | collective-permute-done | bytes 1982496 | tf_op jit(solution)/shard_map/ppermute | solution.py:222
  144.0 4.2 %collective-permute-done.7 = bf16[2,2,88,2816]{3,2,1,0:T(8,128)(2,1)} collective-permute-done((bf16[2,2,88,2816]{3,2,1,0:T(8,128)(2,1)}, bf16[2,2,88,2816]{3,2,1,0:T(8,128)(2,1)}, u32[]{:S(2)}, u32[]{:S(2)}) %collective-permute-start.7) | collective-permute-done | bytes 1982496 | tf_op jit(solution)/shard_map/ppermute | solution.py:222
  148.1 2.7 fusion.20
  151.3 5.2 %dynamic-slice_select_fusion.1 = (bf16[1,88,2816]{2,1,0:T(8,128)(2,1)}, bf16[1,88,2816]{2,1,0:T(8,128)(2,1)}, bf16[1,88,2816]{2,1,0:T(8,128)(2,1)}, bf16[1,88,28...) fusion(bf16[4,88,2816]{2,1,0:T(8,128)(2,1)} %collective-permute, ...), kind=kLoop, calls=%fused_computation.96 | loop fusion | flops 1982464 | bytes 11894818 | tf_op jit(solution)/shard_map/jit(_where)/select_n | solution.py:251
  156.7 1.6 pad_maximum_fusion.1
  159.3 3.0 copy.93
  162.4 3.6 convolution_bitcast_fusion.1.refs_4_
  166.0 6.9 %collective-permute-done.8 = bf16[2,88,2816]{2,1,0:T(8,128)(2,1)} collective-permute-done((bf16[2,88,2816]{2,1,0:T(8,128)(2,1)}, bf16[2,88,2816]{2,1,0:T(8,128)(2,1)}, u32[]{:S(2)}, u32[]{:S(2)}) %collective-permute-start.8) | collective-permute-done | bytes 991264 | tf_op jit(solution)/shard_map/ppermute | solution.py:222
  172.9 2.1 fusion.24
  177.1 2.7 collective-permute-start.10
  179.7 11.9 %collective-permute-done.5 = bf16[4,88,2112]{2,1,0:T(8,128)(2,1)} collective-permute-done((bf16[4,88,2112]{2,1,0:T(8,128)(2,1)}, bf16[4,88,2112]{2,1,0:T(8,128)(2,1)}, u32[]{:S(2)}, u32[]{:S(2)}) %collective-permute-start.5) | collective-permute-done | bytes 1486880 | tf_op jit(solution)/shard_map/ppermute | solution.py:222
  191.7 3.7 dynamic-slice_select_fusion.19
  195.5 1.4 pad_maximum_fusion.2
  196.9 1.8 collective-permute-start.6
  200.7 3.9 collective-permute-done.13
  205.4 2.6 fusion.17
  208.0 1.6 collective-permute-start.15
  210.8 20.1 %triples.6.refs_9_ = f32[5,88,768]{2,1,0:T(8,128)S(1)} custom-call(f32[1,32]{1,0:T(1,128)S(1)} %copy-done.7, bf16[2,32,88,128]{3,2,1,0:T(8,128)(2,1)S(1)} %bitcast.215, bf16[2,88,2816]{2,1,0:T(8,128)(2,1)S(1)} %pad_maximum_fusion.3.refs_2_, bf16[5,128,768]{2,1,0:T(8,128)(2,1)S(1)} %pad.18.refs_3_, ...), custom_call_target="tpu_custom_call" | custom-call | flops 29758586880 | bytes 10297344 | tf_op jit(solution)/shard_map/triples/pallas_call | solution.py:197
  232.0 4.3 %copy.98 = bf16[2,5,16,44,32]{3,2,4,1,0:T(8,128)(2,1)} copy(bf16[2,5,16,44,32]{4,3,2,1,0:T(8,128)(2,1)} %get-tuple-element.48) | data formatting | bytes 901120 | tf_op jit(solution)/shard_map/optimization_barrier | solution.py:230
  236.4 3.3 copy.100
  239.6 6.7 %convolution_bitcast_fusion.refs_4_ = bf16[2,5,32,16,768]{4,3,2,1,0:T(8,128)(2,1)} fusion(bf16[2,5,16,44,32]{3,2,4,1,0:T(8,128)(2,1)} %copy.98, s32[768]{0:T(1024)} %copy-done.44, pred[768]{0:T(1024)(128)(4,1)} %iota_compare_fusion.8), kind=kOutput, calls=%fused_computation.14 | convolution fusion | flops 346097664 | bytes 8318720 | tf_op jit(solution)/shard_map/wgqab,ae->wgbqe/dot_general | solution.py:386
  246.4 2.1 fusion.14
  248.9 1.7 fusion.27
  251.1 2.7 collective-permute-start.19
  253.8 20.5 %triples.7.refs_9_ = f32[5,88,768]{2,1,0:T(8,128)S(1)} custom-call(f32[1,32]{1,0:T(1,128)S(1)} %copy-done.6, bf16[2,32,88,128]{3,2,1,0:T(8,128)(2,1)S(1)} %bitcast.216, bf16[2,88,2816]{2,1,0:T(8,128)(2,1)S(1)} %pad_maximum_fusion.3.refs_2_, bf16[5,128,768]{2,1,0:T(8,128)(2,1)S(1)} %pad.18.refs_3_, bf16[2,5,32,16,768]{4,3,2,1,0:T(8,128)(2,1)} %copy-done.8, ...), custom_call_target="tpu_custom_call" | custom-call | flops 29758586880 | bytes 10297344 | tf_op jit(solution)/shard_map/triples/pallas_call | solution.py:197
  274.3 4.3 %collective-permute-done.14 = bf16[2,88,2112]{2,1,0:T(8,128)(2,1)S(1)} collective-permute-done((bf16[2,88,2112]{2,1,0:T(8,128)(2,1)S(1)}, bf16[2,88,2112]{2,1,0:T(8,128)(2,1)S(1)}, u32[]{:S(2)}, u32[]{:S(2)}) %collective-permute-start.14) | collective-permute-done | bytes 743456 | tf_op jit(solution)/shard_map/ppermute | solution.py:222
  278.6 1.5 fusion.31
  280.2 1.4 collective-permute-done.19
  282.4 4.3 %collective-permute-start.18 = (bf16[88,2112]{1,0:T(8,128)(2,1)S(1)}, bf16[88,2112]{1,0:T(8,128)(2,1)S(1)}, u32[]{:S(2)}, u32[]{:S(2)}) collective-permute-start(bf16[88,2112]{1,0:T(8,128)(2,1)S(1)} %bitcast_select_fusion.10), channel_id=1, source_target_pairs={{0,16},{2,18},{4,20},{6,22},{8,24},{10,26},{12,28},{14,30},{16,0},... | collective-permute-start | bytes 1115144 | tf_op jit(solution)/shard_map/ppermute | solution.py:222
  287.5 20.6 %triples.8.refs_9_ = f32[5,88,768]{2,1,0:T(8,128)S(1)} custom-call(f32[1,32]{1,0:T(1,128)S(1)} %get-tuple-element.107.refs_0_, bf16[2,32,88,128]{3,2,1,0:T(8,128)(2,1)S(1)} %bitcast.217, bf16[2,88,2816]{2,1,0:T(8,128)(2,1)S(1)} %pad_maximum_fusion.4.refs_2_, bf16[5,128,768]{2,1,0:T(8,128)(2,1)S(1)} %pad.18.refs_3_, ...), custom_call_target="tpu_custom_call" | custom-call | flops 29758586880 | bytes 10297344 | tf_op jit(solution)/shard_map/triples/pallas_call | solution.py:197
  308.9 1.7 convolution_bitcast_fusion.2.refs_4_
  311.2 20.5 %triples.9.refs_9_ = f32[5,88,768]{2,1,0:T(8,128)S(1)} custom-call(f32[1,32]{1,0:T(1,128)S(1)} %get-tuple-element.106.refs_0_, bf16[2,32,88,128]{3,2,1,0:T(8,128)(2,1)S(1)} %bitcast.218, bf16[2,88,2816]{2,1,0:T(8,128)(2,1)S(1)} %pad_maximum_fusion.4.refs_2_, bf16[5,128,768]{2,1,0:T(8,128)(2,1)S(1)} %pad.18.refs_3_, ...), custom_call_target="tpu_custom_call" | custom-call | flops 29758586880 | bytes 10297344 | tf_op jit(solution)/shard_map/triples/pallas_call | solution.py:197
  331.7 15.7 %triples.10.refs_9_ = f32[5,88,768]{2,1,0:T(8,128)S(1)} custom-call(f32[1,24]{1,0:T(1,128)S(1)} %get-tuple-element.110.refs_0_, bf16[2,24,88,128]{3,2,1,0:T(8,128)(2,1)S(1)} %bitcast.219, bf16[2,88,2112]{2,1,0:T(8,128)(2,1)S(1)} %pad_maximum_fusion.5.refs_2_, bf16[5,128,768]{2,1,0:T(8,128)(2,1)S(1)} %pad.18.refs_3_, ...), custom_call_target="tpu_custom_call" | custom-call | flops 22318940160 | bytes 7723008 | tf_op jit(solution)/shard_map/triples/pallas_call | solution.py:197
  347.5 17.2 %triples.11 = f32[5,768,88]{2,1,0:T(8,128)S(1)} custom-call(f32[1,24]{1,0:T(1,128)S(1)} %get-tuple-element.111.refs_0_, bf16[2,24,88,128]{3,2,1,0:T(8,128)(2,1)S(1)} %bitcast.220, bf16[2,88,2112]{2,1,0:T(8,128)(2,1)S(1)} %pad_maximum_fusion.5.refs_2_, bf16[5,128,768]{2,1,0:T(8,128)(2,1)S(1)} %pad.18.refs_3_, ...), custom_call_target="tpu_custom_call" | custom-call | flops 22318940160 | bytes 7723008 | tf_op jit(solution)/shard_map/triples/pallas_call | solution.py:197
  366.5 2.4 reshape.569
  368.9 4.9 %all-to-all-start.1 = ((f32[16,40,484]{2,1,0:T(8,128)}), f32[16,40,484]{2,1,0:T(8,128)S(1)}, u32[]{:S(2)}, u32[]{:S(2)}) async-start(f32[16,40,484]{2,1,0:T(8,128)} %reshape.569), calls=%async_computation.1 | async-start | bytes 2621440 | tf_op jit(solution)/shard_map/all_to_all | solution.py:434
  374.0 31.4 %all-to-all-done.1 = f32[16,40,484]{2,1,0:T(8,128)S(1)} async-done(((f32[16,40,484]{2,1,0:T(8,128)}), f32[16,40,484]{2,1,0:T(8,128)S(1)}, u32[]{:S(2)}, u32[]{:S(2)}) %all-to-all-start.1) | async-done | bytes 1239072 | tf_op jit(solution)/shard_map/all_to_all | solution.py:434
  406.0 2.4 gather_fusion.13
  (285 shorter events, 39.0 us)
Async XLA Ops:
  0.0 35.4 %copy-start = (bf16[5,8,7744]{2,1,0:T(8,128)(2,1)S(1)}, bf16[5,8,7744]{2,1,0:T(8,128)(2,1)}, u32[]{:S(2)}) copy-start(bf16[5,8,7744]{2,1,0:T(8,128)(2,1)} %param.10) | copy-start | bytes 1858564
  5.7 2.7 copy-start.15
  7.6 22.0 %collective-permute-start.2 = (bf16[4,88,2816]{2,1,0:T(8,128)(2,1)S(1)}, bf16[4,88,2816]{2,1,0:T(8,128)(2,1)}, u32[]{:S(2)}, u32[]{:S(2)}) collective-permute-start(bf16[4,88,2816]{2,1,0:T(8,128)(2,1)S(1)} %dynamic-slice_bitcast_fusion), channel_id=1, source_target_pairs={{0,1},{1,0},{2,3},{3,2},{4,5},{5,4},{6,7},{7,6},{8,9},{9,8},{10,11... | collective-permute-start | bytes 5947400 | tf_op jit(solution)/shard_map/ppermute | solution.py:217
  9.9 39.6 %collective-permute-start.1 = (bf16[4,88,2816]{2,1,0:T(8,128)(2,1)}, bf16[4,88,2816]{2,1,0:T(8,128)(2,1)}, u32[]{:S(2)}, u32[]{:S(2)}) collective-permute-start(bf16[4,88,2816]{2,1,0:T(8,128)(2,1)} %dynamic-slice_bitcast_fusion.1), channel_id=1, source_target_pairs={{0,1},{1,0},{2,3},{3,2},{4,5},{5,4},{6,7},{7,6},{8,9},{9,8},{10,11... | collective-permute-start | bytes 5947400 | tf_op jit(solution)/shard_map/ppermute | solution.py:217
  13.6 3.3 copy-start.38
  13.6 3.3 copy-start.52
  13.6 3.4 copy-start.11
  13.6 7.2 %copy-start.50 = (s32[5]{0:T(128)S(1)}, s32[5]{0:T(128)}, u32[]{:S(2)}) copy-start(s32[5]{0:T(128)} %param.17) | copy-start | bytes 64
  13.6 7.2 %copy-start.51 = (s32[5]{0:T(128)S(1)}, s32[5]{0:T(128)}, u32[]{:S(2)}) copy-start(s32[5]{0:T(128)} %param.16) | copy-start | bytes 64
  13.6 9.6 %copy-start.12 = (f32[30]{0:T(128)S(1)}, f32[30]{0:T(128)}, u32[]{:S(2)}) copy-start(f32[30]{0:T(128)} %param.13) | copy-start | bytes 364
  16.3 7.5 %copy-start.49 = (s32[2]{0:T(128)S(1)}, s32[2]{0:T(128)}, u32[]{:S(2)}) copy-start(s32[2]{0:T(128)} %param.19) | copy-start | bytes 28
  16.3 9.1 %copy-start.39 = (f32[8,88]{1,0:T(8,128)S(1)}, f32[8,88]{1,0:T(8,128)}, u32[]{:S(2)}) copy-start(f32[8,88]{1,0:T(8,128)} %param.14) | copy-start | bytes 8452
  16.3 29.2 %collective-permute-start = (bf16[4,88,2112]{2,1,0:T(8,128)(2,1)}, bf16[4,88,2112]{2,1,0:T(8,128)(2,1)}, u32[]{:S(2)}, u32[]{:S(2)}) collective-permute-start(bf16[4,88,2112]{2,1,0:T(8,128)(2,1)} %dynamic-slice_bitcast_fusion.2), channel_id=1, source_target_pairs={{0,1},{1,0},{2,3},{3,2},{4,5},{5,4},{6,7},{7,6},{8,9},{9,8},{10,11... | collective-permute-start | bytes 4460552 | tf_op jit(solution)/shard_map/ppermute | solution.py:217
  16.8 27.4 %collective-permute-start.11 = (bf16[2,30,30,88]{3,0,2,1:T(2,128)(2,1)S(1)}, bf16[2,30,30,88]{3,0,2,1:T(2,128)(2,1)}, u32[]{:S(2)}, u32[]{:S(2)}) collective-permute-start(bf16[2,30,30,88]{3,0,2,1:T(2,128)(2,1)S(1)} %copy-done.38), channel_id=1, source_target_pairs={{0,1},{1,0},{2,3},{3,2},{4,5},{5,4},{6,7},{7,6},{8,9},{9,8},{10,11... | collective-permute-start | bytes 950408 | tf_op jit(solution)/shard_map/ppermute | solution.py:217
  23.8 149.1 %copy-start.42 = (pred[2]{0:T(512)(128)(4,1)}, pred[2]{0:T(512)(128)(4,1)S(1)}, u32[]{:S(2)}) copy-start(pred[2]{0:T(512)(128)(4,1)S(1)} %get-tuple-element.113) | copy-start | bytes 10
  23.8 181.6 %copy-start.40 = (pred[2]{0:T(512)(128)(4,1)}, pred[2]{0:T(512)(128)(4,1)S(1)}, u32[]{:S(2)}) copy-start(pred[2]{0:T(512)(128)(4,1)S(1)} %get-tuple-element.115) | copy-start | bytes 10
  27.2 135.1 %copy-start.44 = (s32[768]{0:T(1024)}, s32[768]{0:T(1024)S(1)}, u32[]{:S(2)}) copy-start(s32[768]{0:T(1024)S(1)} %add_select_fusion.1) | copy-start | bytes 9220
  33.9 62.7 %collective-permute-start.3 = (bf16[4,88,2816]{2,1,0:T(8,128)(2,1)}, bf16[4,88,2816]{2,1,0:T(8,128)(2,1)}, u32[]{:S(2)}, u32[]{:S(2)}) collective-permute-start(bf16[4,88,2816]{2,1,0:T(8,128)(2,1)} %get-tuple-element.61), channel_id=1, source_target_pairs={{0,2},{2,0},{4,6},{6,4},{8,10},{10,8},{12,14},{14,12},{16,18},{18,... | collective-permute-start | bytes 5947400 | tf_op jit(solution)/shard_map/ppermute | solution.py:222
  37.6 68.2 %all-to-all-start = ((bf16[16,16,3872]{2,1,0:T(8,128)(2,1)}), bf16[16,16,3872]{2,1,0:T(8,128)(2,1)S(1)}, u32[]{:S(2)}, u32[]{:S(2)}) async-start(bf16[16,16,3872]{2,1,0:T(8,128)(2,1)} %bitcast.229), calls=%async_computation | async-start | bytes 4063232 | tf_op jit(solution)/shard_map/all_to_all | solution.py:329
  45.5 4.0 copy-start.16
  49.5 48.6 %copy-start.14 = (bf16[4,88,2816]{2,1,0:T(8,128)(2,1)S(1)}, bf16[4,88,2816]{2,1,0:T(8,128)(2,1)}, u32[]{:S(2)}) copy-start(bf16[4,88,2816]{2,1,0:T(8,128)(2,1)} %get-tuple-element.60) | copy-start | bytes 5947396
  96.6 47.4 %collective-permute-start.4 = (bf16[4,88,2816]{2,1,0:T(8,128)(2,1)}, bf16[4,88,2816]{2,1,0:T(8,128)(2,1)}, u32[]{:S(2)}, u32[]{:S(2)}) collective-permute-start(bf16[4,88,2816]{2,1,0:T(8,128)(2,1)} %get-tuple-element.29), channel_id=1, source_target_pairs={{0,2},{2,0},{4,6},{6,4},{8,10},{10,8},{12,14},{14,12},{16,18},{18,... | collective-permute-start | bytes 5947400 | tf_op jit(solution)/shard_map/ppermute | solution.py:222
  103.9 44.2 %collective-permute-start.7 = (bf16[2,2,88,2816]{3,2,1,0:T(8,128)(2,1)}, bf16[2,2,88,2816]{3,2,1,0:T(8,128)(2,1)}, u32[]{:S(2)}, u32[]{:S(2)}) collective-permute-start(bf16[2,2,88,2816]{3,2,1,0:T(8,128)(2,1)} %pad_maximum_fusion), channel_id=1, source_target_pairs={{0,4},{2,6},{4,0},{6,2},{8,12},{10,14},{12,8},{14,10},{16,20},{18,... | collective-permute-start | bytes 5947400 | tf_op jit(solution)/shard_map/ppermute | solution.py:222
  129.4 2.7 copy-start.36
  129.4 2.7 copy-start.37
  133.0 15.1 %copy-start.22 = (bf16[1,2,88,2816]{3,2,1,0:T(8,128)(2,1)S(1)}, bf16[1,2,88,2816]{3,2,1,0:T(8,128)(2,1)}, u32[]{:S(2)}) copy-start(bf16[1,2,88,2816]{3,2,1,0:T(8,128)(2,1)} %get-tuple-element.129) | copy-start | bytes 2973700
  133.0 15.1 %copy-start.24 = (bf16[1,2,88,2816]{3,2,1,0:T(8,128)(2,1)S(1)}, bf16[1,2,88,2816]{3,2,1,0:T(8,128)(2,1)}, u32[]{:S(2)}) copy-start(bf16[1,2,88,2816]{3,2,1,0:T(8,128)(2,1)} %get-tuple-element.130) | copy-start | bytes 2973700
  148.1 3.2 copy-start.13
  150.8 22.1 %collective-permute-start.8 = (bf16[2,88,2816]{2,1,0:T(8,128)(2,1)}, bf16[2,88,2816]{2,1,0:T(8,128)(2,1)}, u32[]{:S(2)}, u32[]{:S(2)}) collective-permute-start(bf16[2,88,2816]{2,1,0:T(8,128)(2,1)} %fusion.20), channel_id=1, source_target_pairs={{0,8},{2,10},{4,12},{6,14},{8,0},{10,2},{12,4},{14,6},{16,24},{18,... | collective-permute-start | bytes 2973704 | tf_op jit(solution)/shard_map/ppermute | solution.py:222
  158.3 4.1 copy-start.53
  158.3 46.4 %collective-permute-start.13 = (bf16[2,2,88,2816]{3,2,1,0:T(8,128)(2,1)}, bf16[2,2,88,2816]{3,2,1,0:T(8,128)(2,1)}, u32[]{:S(2)}, u32[]{:S(2)}) collective-permute-start(bf16[2,2,88,2816]{3,2,1,0:T(8,128)(2,1)} %pad_maximum_fusion.1), channel_id=1, source_target_pairs={{0,4},{2,6},{4,0},{6,2},{8,12},{10,14},{12,8},{14,10},{16,20},{18,... | collective-permute-start | bytes 5947400 | tf_op jit(solution)/shard_map/ppermute | solution.py:222
  158.4 33.3 %collective-permute-start.5 = (bf16[4,88,2112]{2,1,0:T(8,128)(2,1)}, bf16[4,88,2112]{2,1,0:T(8,128)(2,1)}, u32[]{:S(2)}, u32[]{:S(2)}) collective-permute-start(bf16[4,88,2112]{2,1,0:T(8,128)(2,1)} %get-tuple-element.30), channel_id=1, source_target_pairs={{0,2},{2,0},{4,6},{6,4},{8,10},{10,8},{12,14},{14,12},{16,18},{18,... | collective-permute-start | bytes 4460552 | tf_op jit(solution)/shard_map/ppermute | solution.py:222
  162.4 10.6 %copy-start.23 = (bf16[1,2,88,2816]{3,2,1,0:T(8,128)(2,1)S(1)}, bf16[1,2,88,2816]{3,2,1,0:T(8,128)(2,1)}, u32[]{:S(2)}) copy-start(bf16[1,2,88,2816]{3,2,1,0:T(8,128)(2,1)} %get-tuple-element.129) | copy-start | bytes 2973700
  162.4 10.6 %copy-start.25 = (bf16[1,2,88,2816]{3,2,1,0:T(8,128)(2,1)S(1)}, bf16[1,2,88,2816]{3,2,1,0:T(8,128)(2,1)}, u32[]{:S(2)}) copy-start(bf16[1,2,88,2816]{3,2,1,0:T(8,128)(2,1)} %get-tuple-element.130) | copy-start | bytes 2973700
  166.0 44.5 %copy-start.8 = (bf16[2,5,32,16,768]{4,3,2,1,0:T(8,128)(2,1)}, bf16[2,5,32,16,768]{4,3,2,1,0:T(8,128)(2,1)S(1)}, u32[]{:S(2)}) copy-start(bf16[2,5,32,16,768]{4,3,2,1,0:T(8,128)(2,1)S(1)} %convolution_bitcast_fusion.1.refs_4_) | copy-start | bytes 23592964
  175.1 1.9 collective-permute-start.9
  175.3 30.1 %copy-start.18 = (bf16[1,2,88,2816]{3,2,1,0:T(8,128)(2,1)}, bf16[1,2,88,2816]{3,2,1,0:T(8,128)(2,1)S(1)}, u32[]{:S(2)}) copy-start(bf16[1,2,88,2816]{3,2,1,0:T(8,128)(2,1)S(1)} %maximum_bitcast_fusion.6) | copy-start | bytes 2973700
  175.3 16.4 %copy-start.17 = (bf16[4,88,2112]{2,1,0:T(8,128)(2,1)S(1)}, bf16[4,88,2112]{2,1,0:T(8,128)(2,1)}, u32[]{:S(2)}) copy-start(bf16[4,88,2112]{2,1,0:T(8,128)(2,1)} %get-tuple-element.62) | copy-start | bytes 4460548
  176.3 29.1 %copy-start.20 = (bf16[1,2,88,2816]{3,2,1,0:T(8,128)(2,1)}, bf16[1,2,88,2816]{3,2,1,0:T(8,128)(2,1)S(1)}, u32[]{:S(2)}) copy-start(bf16[1,2,88,2816]{3,2,1,0:T(8,128)(2,1)S(1)} %maximum_bitcast_fusion.7) | copy-start | bytes 2973700
  177.1 27.6 %collective-permute-start.10 = (bf16[88,2816]{1,0:T(8,128)(2,1)S(1)}, bf16[88,2816]{1,0:T(8,128)(2,1)S(1)}, u32[]{:S(2)}, u32[]{:S(2)}) collective-permute-start(bf16[88,2816]{1,0:T(8,128)(2,1)S(1)} %bitcast_select_fusion.8), channel_id=1, source_target_pairs={{0,16},{2,18},{4,20},{6,22},{8,24},{10,26},{12,28},{14,30},{16,0},... | collective-permute-start | bytes 1486856 | tf_op jit(solution)/shard_map/ppermute | solution.py:222
  196.9 51.9 %collective-permute-start.6 = (bf16[2,2,88,2112]{3,2,1,0:T(8,128)(2,1)}, bf16[2,2,88,2112]{3,2,1,0:T(8,128)(2,1)}, u32[]{:S(2)}, u32[]{:S(2)}) collective-permute-start(bf16[2,2,88,2112]{3,2,1,0:T(8,128)(2,1)} %pad_maximum_fusion.2), channel_id=1, source_target_pairs={{0,4},{2,6},{4,0},{6,2},{8,12},{10,14},{12,8},{14,10},{16,20},{18,... | collective-permute-start | bytes 4460552 | tf_op jit(solution)/shard_map/ppermute | solution.py:222
  205.3 4.3 %collective-permute-start.12 = (bf16[88,2816]{1,0:T(8,128)(2,1)S(1)}, bf16[88,2816]{1,0:T(8,128)(2,1)S(1)}, u32[]{:S(2)}, u32[]{:S(2)}) collective-permute-start(bf16[88,2816]{1,0:T(8,128)(2,1)S(1)} %fusion.33), channel_id=1, source_target_pairs={{0,1},{1,0},{2,3},{3,2},{4,5},{5,4},{6,7},{7,6},{8,9},{9,8},{10,11... | collective-permute-start | bytes 1486856 | tf_op jit(solution)/shard_map/ppermute | solution.py:217
  208.0 38.4 %collective-permute-start.15 = (bf16[2,88,2816]{2,1,0:T(8,128)(2,1)}, bf16[2,88,2816]{2,1,0:T(8,128)(2,1)}, u32[]{:S(2)}, u32[]{:S(2)}) collective-permute-start(bf16[2,88,2816]{2,1,0:T(8,128)(2,1)} %fusion.17), channel_id=1, source_target_pairs={{0,8},{2,10},{4,12},{6,14},{8,0},{10,2},{12,4},{14,6},{16,24},{18,... | collective-permute-start | bytes 2973704 | tf_op jit(solution)/shard_map/ppermute | solution.py:222
  239.6 6.8 %copy-start.19 = (bf16[1,2,88,2816]{3,2,1,0:T(8,128)(2,1)S(1)}, bf16[1,2,88,2816]{3,2,1,0:T(8,128)(2,1)}, u32[]{:S(2)}) copy-start(bf16[1,2,88,2816]{3,2,1,0:T(8,128)(2,1)} %copy-done.18) | copy-start | bytes 2973700
  239.6 6.8 %copy-start.21 = (bf16[1,2,88,2816]{3,2,1,0:T(8,128)(2,1)S(1)}, bf16[1,2,88,2816]{3,2,1,0:T(8,128)(2,1)}, u32[]{:S(2)}) copy-start(bf16[1,2,88,2816]{3,2,1,0:T(8,128)(2,1)} %copy-done.20) | copy-start | bytes 2973700
  239.6 6.8 %copy-start.41 = (pred[2]{0:T(512)(128)(4,1)S(1)}, pred[2]{0:T(512)(128)(4,1)}, u32[]{:S(2)}) copy-start(pred[2]{0:T(512)(128)(4,1)} %copy-done.40) | copy-start | bytes 10
  239.6 6.8 %copy-start.43 = (pred[2]{0:T(512)(128)(4,1)S(1)}, pred[2]{0:T(512)(128)(4,1)}, u32[]{:S(2)}) copy-start(pred[2]{0:T(512)(128)(4,1)} %copy-done.42) | copy-start | bytes 10
  248.6 5.2 %copy-start.3 = (bf16[2,5,3,88,128]{4,3,2,1,0:T(8,128)(2,1)S(1)}, bf16[2,5,3,88,128]{4,3,2,1,0:T(8,128)(2,1)}, u32[]{:S(2)}) copy-start(bf16[2,5,3,88,128]{4,3,2,1,0:T(8,128)(2,1)} %pad_maximum_fusion.6.refs_5_) | copy-start | bytes 2027524
  248.6 5.2 %copy-start.5 = (bf16[3,128,256]{2,1,0:T(8,128)(2,1)S(1)}, bf16[3,128,256]{2,1,0:T(8,128)(2,1)}, u32[]{:S(2)}) copy-start(bf16[3,128,256]{2,1,0:T(8,128)(2,1)} %add_convert_fusion.refs_6_) | copy-start | bytes 589828
  248.6 5.2 %copy-start.6 = (f32[1,32]{1,0:T(1,128)S(1)}, f32[1,32]{1,0:T(1,128)}, u32[]{:S(2)}) copy-start(f32[1,32]{1,0:T(1,128)} %get-tuple-element.108.refs_0_) | copy-start | bytes 388
  248.6 5.2 %copy-start.10 = (f32[5,88,768]{2,1,0:T(8,128)S(1)}, f32[5,88,768]{2,1,0:T(8,128)}, u32[]{:S(2)}) copy-start(f32[5,88,768]{2,1,0:T(8,128)} %copy-done.9) | copy-start | bytes 4055044
  248.6 2.4 collective-permute-start.16
  250.5 28.0 %collective-permute-start.14 = (bf16[2,88,2112]{2,1,0:T(8,128)(2,1)S(1)}, bf16[2,88,2112]{2,1,0:T(8,128)(2,1)S(1)}, u32[]{:S(2)}, u32[]{:S(2)}) collective-permute-start(bf16[2,88,2112]{2,1,0:T(8,128)(2,1)S(1)} %fusion.27), channel_id=1, source_target_pairs={{0,8},{2,10},{4,12},{6,14},{8,0},{10,2},{12,4},{14,6},{16,24},{18,... | collective-permute-start | bytes 2230280 | tf_op jit(solution)/shard_map/ppermute | solution.py:222
  251.1 30.5 %collective-permute-start.19 = (bf16[88,2816]{1,0:T(8,128)(2,1)S(1)}, bf16[88,2816]{1,0:T(8,128)(2,1)S(1)}, u32[]{:S(2)}, u32[]{:S(2)}) collective-permute-start(bf16[88,2816]{1,0:T(8,128)(2,1)S(1)} %bitcast_select_fusion.7), channel_id=1, source_target_pairs={{0,16},{2,18},{4,20},{6,22},{8,24},{10,26},{12,28},{14,30},{16,0},... | collective-permute-start | bytes 1486856 | tf_op jit(solution)/shard_map/ppermute | solution.py:222
  280.2 2.2 collective-permute-start.17
  282.3 4.4 %collective-permute-start.20 = (bf16[88,2816]{1,0:T(8,128)(2,1)S(1)}, bf16[88,2816]{1,0:T(8,128)(2,1)S(1)}, u32[]{:S(2)}, u32[]{:S(2)}) collective-permute-start(bf16[88,2816]{1,0:T(8,128)(2,1)S(1)} %fusion.32), channel_id=1, source_target_pairs={{0,1},{1,0},{2,3},{3,2},{4,5},{5,4},{6,7},{7,6},{8,9},{9,8},{10,11... | collective-permute-start | bytes 1486856 | tf_op jit(solution)/shard_map/ppermute | solution.py:217
  282.4 25.7 %collective-permute-start.18 = (bf16[88,2112]{1,0:T(8,128)(2,1)S(1)}, bf16[88,2112]{1,0:T(8,128)(2,1)S(1)}, u32[]{:S(2)}, u32[]{:S(2)}) collective-permute-start(bf16[88,2112]{1,0:T(8,128)(2,1)S(1)} %bitcast_select_fusion.10), channel_id=1, source_target_pairs={{0,16},{2,18},{4,20},{6,22},{8,24},{10,26},{12,28},{14,30},{16,0},... | collective-permute-start | bytes 1115144 | tf_op jit(solution)/shard_map/ppermute | solution.py:222
  287.5 21.3 %copy-start.34 = (bf16[2,5,16,44,24]{3,2,4,1,0:T(8,128)(2,1)S(1)}, bf16[2,5,16,44,24]{3,2,4,1,0:T(8,128)(2,1)}, u32[]{:S(2)}) copy-start(bf16[2,5,16,44,24]{3,2,4,1,0:T(8,128)(2,1)} %copy.100) | copy-start | bytes 1013764
  287.5 21.3 %copy-start.45 = (s32[768]{0:T(1024)S(1)}, s32[768]{0:T(1024)}, u32[]{:S(2)}) copy-start(s32[768]{0:T(1024)} %copy-done.44) | copy-start | bytes 9220
  287.5 21.3 %copy-start.54 = (pred[768]{0:T(1024)(128)(4,1)S(1)}, pred[768]{0:T(1024)(128)(4,1)}, u32[]{:S(2)}) copy-start(pred[768]{0:T(1024)(128)(4,1)} %iota_compare_fusion.8) | copy-start | bytes 2308
  308.7 1.8 collective-permute-start.21
  366.5 7.3 %copy-start.47 = (s32[5]{0:T(128)S(1)}, s32[5]{0:T(128)}, u32[]{:S(2)}) copy-start(s32[5]{0:T(128)} %copy-done.46) | copy-start | bytes 64
  368.9 36.5 %all-to-all-start.1 = ((f32[16,40,484]{2,1,0:T(8,128)}), f32[16,40,484]{2,1,0:T(8,128)S(1)}, u32[]{:S(2)}, u32[]{:S(2)}) async-start(f32[16,40,484]{2,1,0:T(8,128)} %reshape.569), calls=%async_computation.1 | async-start | bytes 2621440 | tf_op jit(solution)/shard_map/all_to_all | solution.py:434
  405.6 2.8 copy-start.1
  (17 other events, 27.7 us)
where the time goes:
time: 413 us; the launch traced here: 409 us
  waiting for transfers between devices  116 us (28%)
  Pallas kernels  115 us (28%)
  local copies, waits for them, and re-layouts  69.8 us (17%)
  other arithmetic  55.8 us (14%)
  starting transfers between devices  31.2 us (8%)
  matrix products  18 us (4%)
    pallas_call x6, Pallas kernels, triples_call(): pl.pallas_call(functools.partial(triples_kernel, last), grid=(groups,), i...  115 us
    ppermute x12, waiting for transfers between devices, across(): return lax.ppermute(x, 'pair', [(t, t ^ bit) for t in range(count)])  83.8 us
    all_to_all x1, waiting for transfers between devices, on_device_scatter(): came = lax.all_to_all(total, 'pair', 0, 0, tiled=True)  31.4 us
    ppermute x12, starting transfers between devices, across(): return lax.ppermute(x, 'pair', [(t, t ^ bit) for t in range(count)])  18.3 us
    select_n x3, other arithmetic, block(): return jnp.where(self.from_here(0)[w], pick(kept, beta), pick(came, beta))  13.1 us
    select_n x3, other arithmetic, split_cores(): return (jnp.where(same, mine, theirs), jnp.where(same, theirs, mine))  12.2 us
    dot_general x3, matrix products, spread_holes(): return jnp.einsum('wgqab,ae->wgbqe', hole, spread)  12.1 us
    optimization_barrier x3, local copies, waits for them, and re-layouts, after(): return lax.optimization_barrier((x,) + others)[0]  10.6 us
  transfers between devices with their start and end apart: 24, of which 10 were waited for; matrix products, arithmetic and copies ran while one was open for 30% of the time, Pallas kernels for 15%

commit v1 on v0

--- a/solution.py
+++ b/solution.py
@@ -127,8 +127,8 @@
 
 def b_chunks(block):
     unit = LANE // math.gcd(LANE, block)
-    size = 2 * unit
-    return [(first, min(size, block - first)) for first in range(0, block, size)]
+    sizes = (unit, unit, 2 * unit, block - 4 * unit)
+    return [(sum(sizes[:n]), size) for n, size in enumerate(sizes)]
 
 
 def triples_kernel(last, *refs):
@@ -304,12 +304,27 @@
     for leaving in sent_x:
         leaving_x.append(after(leaving, x[-1]) if x else leaving)
         x.append(across(leaving_x[-1], 1))
-    kept_y, sent_y = [], []
-    for kept, came in zip(kept_x, x):
-        kept, leaving = path.split_low(kept, after(came, sent_y[-1]) if sent_y else came)
-        kept_y.append(kept)
-        sent_y.append(leaving)
-    y = [across(leaving, 2) for leaving in sent_y]
+    kept_y, sent_y, kept_z, sent_z, kept_h, sent_h = {}, {}, {}, {}, {}, {}
+    y, z, h, ready = {}, {}, {}, {}
+
+    def to_low(chunk, *tokens):
+        kept_y[chunk], sent_y[chunk] = path.split_low(kept_x[chunk], after(x[chunk], *tokens))
+        y[chunk] = across(sent_y[chunk], 2)
+
+    def to_high(chunk, *tokens):
+        kept_z[chunk], sent_z[chunk] = path.split_high(kept_y[chunk], after(y[chunk], *tokens))
+        z[chunk] = across(sent_z[chunk], 4)
+
+    def to_top(chunk, *tokens):
+        kept_h[chunk], sent_h[chunk] = path.split_top(kept_z[chunk], after(z[chunk], *tokens))
+        h[chunk] = across(sent_h[chunk], 8)
+
+    def arrive(chunk, *tokens):
+        ready[chunk] = path.join(kept_h[chunk], after(h[chunk], *tokens))
+
+    to_low(0, sent_x[0])
+    to_low(1, sent_y[0])
+    to_high(0, sent_y[1])
 
     pair_sym = occ_irrep[pair_i] ^ occ_irrep[pair_j]
     mine = lax.dynamic_slice_in_dim(after(amplitudes, sent_x[0]), core * share, share, 2)
@@ -327,7 +342,7 @@
     sent = jnp.einsum("rh,hx->rx", chosen, stored)
     sent = sent.reshape(chips, kinds * local_pairs + 1, share)
     came = lax.all_to_all(sent, "pair", 0, 0, tiled=True)
-    came = after(came, sent_y[0], leaving_x[1])
+    came = after(came, sent_z[0], leaving_x[2])
     came = came.reshape(chips * (kinds * local_pairs + 1), share)
     label_rows = after(target, leaving_x[1]) * (kinds * local_pairs + 1) + kinds * local_pairs
     both = came[label_rows][:, : 2 * local_pairs].astype(jnp.int32).reshape(chips, 2, local_pairs)
@@ -393,41 +408,39 @@
         return triples_call(w, last, energies, vt, v, at, areps[chunk], ct, mask, ecol, lrow, total)
 
     calls = [(chunk, w) for chunk in range(len(chunks)) for w in range(windows)]
-    kept_z, sent_z, kept_h, sent_h, z, h, ready = {}, {}, {}, {}, {}, {}, {}
-
-    def to_high(chunk, token=None):
-        came_y = y[chunk] if token is None else after(y[chunk], token)
-        kept_z[chunk], sent_z[chunk] = path.split_high(kept_y[chunk], came_y)
-        z[chunk] = across(sent_z[chunk], 4)
-        return sent_z[chunk]
-
-    def to_top(chunk, token=None):
-        came_z = z[chunk] if token is None else after(z[chunk], token)
-        kept_h[chunk], sent_h[chunk] = path.split_top(kept_z[chunk], came_z)
-        h[chunk] = across(sent_h[chunk], 8)
-        return sent_h[chunk]
-
-    def arrive(chunk, token=None):
-        came_h = h[chunk] if token is None else after(h[chunk], token)
-        ready[chunk] = path.join(kept_h[chunk], came_h)
-        return ready[chunk]
-
-    plan = {0: [(to_top, 1), (to_high, 2)], 1: [(arrive, 1), (to_top, 2)], 2: [(arrive, 2)]}
-    to_high(0, amps)
-    at = after(at, sent_z[0], sent_y[1], leaving_x[2])
-    areps = [spread_holes(0, at)]
-    to_top(0, areps[0])
-    ct = after(ct, sent_h[0])
+    to_top(0, amps)
+    to_high(1, sent_h[0])
+    to_low(2, sent_z[1])
+    at = after(at, sent_y[2], leaving_x[3])
+    areps = {0: spread_holes(0, at)}
+    ct = after(ct, areps[0])
     arrive(0, ct)
-    ready[0] = after(ready[0], to_high(1, sent_h[0]), sent_y[2])
+    to_top(1, ready[0])
+    ready[0] = after(ready[0], sent_h[1])
     total = None
     for n, (chunk, w) in enumerate(calls):
         total = run(chunk, w, ready[chunk], total)
-        issued = [move(number, total) for move, number in plan.get(n, [])]
         if n == 0:
-            areps += [spread_holes(number, total) for number in range(1, len(chunks))]
-        if issued:
-            total = after(total, *issued)
+            arrive(1, total)
+            areps[1] = spread_holes(1, total)
+            total = after(total, ready[1])
+        elif n == 1:
+            to_low(3, total)
+            total = after(total, sent_y[3])
+        elif n == 2:
+            to_high(2, total)
+            total = after(total, sent_z[2])
+        elif n == 3:
+            areps[2] = spread_holes(2, total)
+            to_top(2, areps[2])
+            areps[3] = spread_holes(3, sent_h[2])
+            to_high(3, areps[3])
+            arrive(2, sent_z[3])
+            to_top(3, ready[2])
+            total = after(total, sent_h[3])
+        elif n == 4:
+            arrive(3, total)
+            total = after(total, ready[3])
     total = total[:, :used].reshape(pairs, share)[rank]
     cut = 8 if share % 8 == 0 else 1
     total = total.reshape(chips, local_pairs * cut, share // cut)
@@ -443,6 +456,7 @@
     chips, cores = lax.axis_size("pair"), lax.axis_size("irrep")
     fits = lax.axis_size("vtile") == 1 and cores == 2 and betas == 8 and chips == betas * cores
     fits = fits and args[8].shape[0] == 2 and block % 2 == 0 and block < LANE
+    fits = fits and all(size > 0 and size % 2 == 0 for _, size in b_chunks(block))
     if fits and args[5].shape[0] <= 256:
         return on_device_scatter(*args)
     return on_device_gather(*args)

time: 413 us -> 457 us (1.11)
  local copies, waits for them, and re-layouts: 69.8 us -> 85.7 us
  waiting for transfers between devices: 116 us -> 131 us
  starting transfers between devices: 31.2 us -> 36.8 us
  Pallas kernels: 115 us -> 120 us
    ppermute x12 -> x16, waiting for transfers between devices: 83.8 us -> 94.5 us  [across(): return lax.ppermute(x, 'pair', [(t, t ^ bit) for t in range(count)])]
    unnamed x111 -> x109, local copies, waits for them, and re-layouts: 3.88 us -> 10 us
    pallas_call x6 -> x8, Pallas kernels: 115 us -> 120 us  [triples_call(): pl.pallas_call(functools.partial(triples_kernel, last), grid=(groups,), i...]
    optimization_barrier x3 -> x4, local copies, waits for them, and re-layouts: 10.6 us -> 13.8 us  [after(): return lax.optimization_barrier((x,) + others)[0]]
    ppermute x12 -> x16, starting transfers between devices: 18.3 us -> 21.1 us  [across(): return lax.ppermute(x, 'pair', [(t, t ^ bit) for t in range(count)])]
    dot_general x3 -> x4, matrix products: 12.1 us -> 14.4 us  [spread_holes(): return jnp.einsum('wgqab,ae->wgbqe', hole, spread)]
    select_n x3 -> x4, other arithmetic: 13.1 us -> 14.6 us  [block(): return jnp.where(self.from_here(0)[w], pick(kept, beta), pick(came, beta))]
    slice x2 -> x3, local copies, waits for them, and re-layouts: 9.42 us -> 8.24 us  [on_device_scatter(): local[:, :, first * block:(first + size) * block]]
  transfers between devices with their start and end apart: 24 -> 31, of which waited for: 10 -> 12; matrix products, arithmetic and copies ran while one was open for 30% -> 29% of each run, Pallas kernels for 15% -> 15%
where the time goes in v1:
time: 457 us; the launch traced here: 452 us
  waiting for transfers between devices  131 us (29%)
  Pallas kernels  120 us (26%)
  local copies, waits for them, and re-layouts  85.7 us (19%)
  other arithmetic  55.7 us (12%)
  starting transfers between devices  36.8 us (8%)
  matrix products  19.5 us (4%)
    pallas_call x8, Pallas kernels, triples_call(): pl.pallas_call(functools.partial(triples_kernel, last), grid=(groups,), i...  120 us
    ppermute x16, waiting for transfers between devices, across(): return lax.ppermute(x, 'pair', [(t, t ^ bit) for t in range(count)])  94.5 us
    all_to_all x1, waiting for transfers between devices, on_device_scatter(): came = lax.all_to_all(total, 'pair', 0, 0, tiled=True)  31.4 us
    ppermute x16, starting transfers between devices, across(): return lax.ppermute(x, 'pair', [(t, t ^ bit) for t in range(count)])  21.1 us
    select_n x4, other arithmetic, block(): return jnp.where(self.from_here(0)[w], pick(kept, beta), pick(came, beta))  14.6 us
    dot_general x4, matrix products, spread_holes(): return jnp.einsum('wgqab,ae->wgbqe', hole, spread)  14.4 us
    optimization_barrier x4, local copies, waits for them, and re-layouts, after(): return lax.optimization_barrier((x,) + others)[0]  13.8 us
    select_n x4, other arithmetic, split_cores(): return (jnp.where(same, mine, theirs), jnp.where(same, theirs, mine))  11.7 us
  transfers between devices with their start and end apart: 31, of which 12 were waited for; matrix products, arithmetic and copies ran while one was open for 29% of the time, Pallas kernels for 15%

profile of v1, /device:TPU:12, one launch (start us, length us, event | category | flops | bytes accessed | tf_op | source)
XLA Modules:
  0.0 452.2 jit_solution(3936810469653525766)
XLA Ops:
  0.0 3.8 fusion.93
  3.8 2.9 dynamic-slice_bitcast_fusion.2
  8.3 2.4 slice.256
  10.7 1.5 dynamic-slice_bitcast_fusion
  13.2 2.1 slice.255
  15.4 1.6 copy-done.15
  29.9 2.7 bitcast_select_fusion.4
  32.7 2.5 collective-permute-start.4
  35.3 2.1 fusion.43
  37.4 6.9 %all-to-all-start = ((bf16[16,16,3872]{2,1,0:T(8,128)(2,1)}), bf16[16,16,3872]{2,1,0:T(8,128)(2,1)S(1)}, u32[]{:S(2)}, u32[]{:S(2)}) async-start(bf16[16,16,3872]{2,1,0:T(8,128)(2,1)} %bitcast.277), calls=%async_computation | async-start | bytes 4063232 | tf_op jit(solution)/shard_map/all_to_all | solution.py:344
  44.3 1.8 bitcast_select_fusion.6
  46.7 3.4 bitcast_select_fusion.3
  50.1 8.1 %collective-permute-done.4 = bf16[4,88,1408]{2,1,0:T(8,128)(2,1)} collective-permute-done((bf16[4,88,1408]{2,1,0:T(8,128)(2,1)}, bf16[4,88,1408]{2,1,0:T(8,128)(2,1)}, u32[]{:S(2)}, u32[]{:S(2)}) %collective-permute-start.4) | collective-permute-done | bytes 991264 | tf_op jit(solution)/shard_map/ppermute | solution.py:222
  58.2 2.7 collective-permute-start.5
  60.9 3.2 dynamic-slice_select_fusion.27
  64.5 37.1 %collective-permute-done.5 = bf16[4,88,1408]{2,1,0:T(8,128)(2,1)S(1)} collective-permute-done((bf16[4,88,1408]{2,1,0:T(8,128)(2,1)S(1)}, bf16[4,88,1408]{2,1,0:T(8,128)(2,1)S(1)}, u32[]{:S(2)}, u32[]{:S(2)}) %collective-permute-start.5) | collective-permute-done | bytes 991264 | tf_op jit(solution)/shard_map/ppermute | solution.py:222
  101.6 1.7 dynamic-slice_select_fusion.17
  103.9 1.7 copy-done.13
  105.5 3.8 bitcast_select_fusion
  110.0 7.2 %collective-permute-done.9 = bf16[2,88,1408]{2,1,0:T(8,128)(2,1)S(1)} collective-permute-done((bf16[2,88,1408]{2,1,0:T(8,128)(2,1)S(1)}, bf16[2,88,1408]{2,1,0:T(8,128)(2,1)S(1)}, u32[]{:S(2)}, u32[]{:S(2)}) %collective-permute-start.9) | collective-permute-done | bytes 495648 | tf_op jit(solution)/shard_map/ppermute | solution.py:222
  119.9 2.3 collective-permute-start.11
  122.2 11.0 %collective-permute-done.13 = bf16[2,2,88,1408]{3,2,1,0:T(8,128)(2,1)S(1)} collective-permute-done((bf16[2,2,88,1408]{3,2,1,0:T(8,128)(2,1)S(1)}, bf16[2,2,88,1408]{3,2,1,0:T(8,128)(2,1)S(1)}, u32[]{:S(2)}, u32[]{:S(2)}) %collective-permute-start.13) | collective-permute-done | bytes 991264 | tf_op jit(solution)/shard_map/ppermute | solution.py:222
  141.2 3.0 gather_fusion.6
  144.2 2.4 slice.265
  146.8 4.7 %slice.99 = bf16[2,5,16,44,88]{4,3,2,1,0:T(8,128)(2,1)S(1)} reshape(bf16[160,3872]{1,0:T(8,128)(2,1)} %slice.265) | data formatting | bytes 2478080 | tf_op jit(solution)/shard_map/slice | solution.py:364
  151.6 2.0 slice.270
  153.5 1.9 slice.268
  156.3 1.7 squeeze.286
  163.5 5.1 %fusion.94 = (bf16[2,5,16,44,16]{4,3,2,1,0:T(8,128)(2,1)}, bf16[2,5,16,44,16]{4,3,2,1,0:T(8,128)(2,1)}) fusion(bf16[2,5,16,44,88]{4,3,2,1,0:T(8,128)(2,1)} %copy-done.10), kind=kLoop, calls=%fused_computation.270 | loop fusion | bytes 901120 | tf_op jit(solution)/shard_map/slice | solution.py:400
  168.6 5.2 %dynamic-slice_select_fusion.1 = (bf16[1,88,2816]{2,1,0:T(8,128)(2,1)}, bf16[1,88,2816]{2,1,0:T(8,128)(2,1)}, bf16[1,88,2816]{2,1,0:T(8,128)(2,1)S(1)}, bf16[1,8...) fusion(bf16[4,88,2816]{2,1,0:T(8,128)(2,1)} %collective-permute, ...), kind=kLoop, calls=%fused_computation.114 | loop fusion | flops 1982464 | bytes 11894818 | tf_op jit(solution)/shard_map/jit(_where)/select_n | solution.py:251
  175.7 3.1 copy.104
  178.9 2.4 convolution_bitcast_fusion.3.refs_4_
  188.2 4.0 collective-permute-start.17
  192.7 11.4 %triples.8.refs_9_ = f32[5,88,768]{2,1,0:T(8,128)S(1)} custom-call(f32[1,16]{1,0:T(1,128)S(1)} %get-tuple-element.142.refs_0_, bf16[2,16,88,128]{3,2,1,0:T(8,128)(2,1)S(1)} %bitcast.266, bf16[2,88,1408]{2,1,0:T(8,128)(2,1)S(1)} %pad_maximum_fusion.7.refs_2_, bf16[5,128,768]{2,1,0:T(8,128)(2,1)S(1)} %pad.18.refs_3_, ...), custom_call_target="tpu_custom_call" | custom-call | flops 14879293440 | bytes 5148672 | tf_op jit(solution)/shard_map/triples/pallas_call | solution.py:197
  205.2 3.2 copy.106
  208.5 1.6 fusion.47
  210.4 2.4 convolution_bitcast_fusion.2.refs_4_
  214.1 11.4 %triples.9.refs_9_ = f32[5,88,768]{2,1,0:T(8,128)S(1)} custom-call(f32[1,16]{1,0:T(1,128)S(1)} %get-tuple-element.143.refs_0_, bf16[2,16,88,128]{3,2,1,0:T(8,128)(2,1)S(1)} %bitcast.267, bf16[2,88,1408]{2,1,0:T(8,128)(2,1)S(1)} %pad_maximum_fusion.7.refs_2_, bf16[5,128,768]{2,1,0:T(8,128)(2,1)S(1)} %pad.18.refs_3_, ...), custom_call_target="tpu_custom_call" | custom-call | flops 14879293440 | bytes 5148672 | tf_op jit(solution)/shard_map/triples/pallas_call | solution.py:197
  225.6 4.6 %dynamic-slice_select_fusion.11 = (bf16[1,88,2112]{2,1,0:T(8,128)(2,1)S(1)}, bf16[1,88,2112]{2,1,0:T(8,128)(2,1)S(1)}, bf16[1,88,2112]{2,1,0:T(8,128)(2,1)S(1)},...) fusion(bf16[4,88,2112]{2,1,0:T(8,128)(2,1)} %collective-permute, ...), kind=kLoop, calls=%fused_computation.133 | loop fusion | flops 1486848 | bytes 8921122 | tf_op jit(solution)/shard_map/jit(_where)/select_n | solution.py:251
  232.7 11.7 %triples.10.refs_9_ = f32[5,88,768]{2,1,0:T(8,128)S(1)} custom-call(f32[1,16]{1,0:T(1,128)S(1)} %get-tuple-element.141.refs_0_, bf16[2,16,88,128]{3,2,1,0:T(8,128)(2,1)S(1)} %bitcast.264, bf16[2,88,1408]{2,1,0:T(8,128)(2,1)S(1)} %pad_maximum_fusion.8.refs_2_, bf16[5,128,768]{2,1,0:T(8,128)(2,1)S(1)} %pad.18.refs_3_, ...), custom_call_target="tpu_custom_call" | custom-call | flops 14879293440 | bytes 5148672 | tf_op jit(solution)/shard_map/triples/pallas_call | solution.py:197
  244.5 2.6 fusion.13
  247.1 1.8 collective-permute-start.21
  248.9 11.5 %triples.11.refs_9_ = f32[5,88,768]{2,1,0:T(8,128)S(1)} custom-call(f32[1,16]{1,0:T(1,128)S(1)} %get-tuple-element.140.refs_0_, bf16[2,16,88,128]{3,2,1,0:T(8,128)(2,1)S(1)} %bitcast.265, bf16[2,88,1408]{2,1,0:T(8,128)(2,1)S(1)} %pad_maximum_fusion.8.refs_2_, bf16[5,128,768]{2,1,0:T(8,128)(2,1)S(1)} %pad.18.refs_3_, ...), custom_call_target="tpu_custom_call" | custom-call | flops 14879293440 | bytes 5148672 | tf_op jit(solution)/shard_map/triples/pallas_call | solution.py:197
  261.5 4.2 copy.108
  265.7 6.7 %convolution_bitcast_fusion.refs_4_ = bf16[2,5,32,16,768]{4,3,2,1,0:T(8,128)(2,1)} fusion(bf16[2,5,16,44,32]{3,2,4,1,0:T(8,128)(2,1)} %copy.108, s32[768]{0:T(1024)S(1)} %get-tuple-element.158, pred[768]{0:T(1024)(128)(4,1)S(1)} %iota_compare_fusion.8), kind=kOutput, calls=%fused_computation.14 | convolution fusion | flops 346097664 | bytes 8318720 | tf_op jit(solution)/shard_map/wgqab,ae->wgbqe/dot_general | solution.py:401
  272.5 2.0 fusion.17
  278.0 3.3 copy.110
  281.2 2.9 convolution_bitcast_fusion.1.refs_4_
  284.2 1.6 fusion.20
  285.8 13.7 %collective-permute-done.24 = bf16[88,2816]{1,0:T(8,128)(2,1)} collective-permute-done((bf16[88,2816]{1,0:T(8,128)(2,1)}, bf16[88,2816]{1,0:T(8,128)(2,1)}, u32[]{:S(2)}, u32[]{:S(2)}) %collective-permute-start.24) | collective-permute-done | bytes 495648 | tf_op jit(solution)/shard_map/ppermute | solution.py:222
  301.3 2.7 collective-permute-start.23
  304.2 17.4 %collective-permute-done.23 = bf16[2,88,2112]{2,1,0:T(8,128)(2,1)S(1)} collective-permute-done((bf16[2,88,2112]{2,1,0:T(8,128)(2,1)S(1)}, bf16[2,88,2112]{2,1,0:T(8,128)(2,1)S(1)}, u32[]{:S(2)}, u32[]{:S(2)}) %collective-permute-start.23) | collective-permute-done | bytes 743456 | tf_op jit(solution)/shard_map/ppermute | solution.py:222
  321.7 1.5 fusion.24
  325.1 2.6 collective-permute-start.27
  327.6 20.6 %triples.12.refs_9_ = f32[5,88,768]{2,1,0:T(8,128)S(1)} custom-call(f32[1,32]{1,0:T(1,128)S(1)} %get-tuple-element.137.refs_0_, bf16[2,32,88,128]{3,2,1,0:T(8,128)(2,1)S(1)} %bitcast.260, bf16[2,88,2816]{2,1,0:T(8,128)(2,1)S(1)} %pad_maximum_fusion.4.refs_2_, bf16[5,128,768]{2,1,0:T(8,128)(2,1)S(1)} %pad.18.refs_3_, ...), custom_call_target="tpu_custom_call" | custom-call | flops 29758586880 | bytes 10297344 | tf_op jit(solution)/shard_map/triples/pallas_call | solution.py:197
  349.1 1.6 collective-permute-done.28
  351.3 20.5 %triples.13.refs_9_ = f32[5,88,768]{2,1,0:T(8,128)S(1)} custom-call(f32[1,32]{1,0:T(1,128)S(1)} %get-tuple-element.136.refs_0_, bf16[2,32,88,128]{3,2,1,0:T(8,128)(2,1)S(1)} %bitcast.261, bf16[2,88,2816]{2,1,0:T(8,128)(2,1)S(1)} %pad_maximum_fusion.4.refs_2_, bf16[5,128,768]{2,1,0:T(8,128)(2,1)S(1)} %pad.18.refs_3_, ...), custom_call_target="tpu_custom_call" | custom-call | flops 29758586880 | bytes 10297344 | tf_op jit(solution)/shard_map/triples/pallas_call | solution.py:197
  371.9 15.8 %triples.14.refs_9_ = f32[5,88,768]{2,1,0:T(8,128)S(1)} custom-call(f32[1,24]{1,0:T(1,128)S(1)} %get-tuple-element.138.refs_0_, bf16[2,24,88,128]{3,2,1,0:T(8,128)(2,1)S(1)} %bitcast.262, bf16[2,88,2112]{2,1,0:T(8,128)(2,1)S(1)} %pad_maximum_fusion.5.refs_2_, bf16[5,128,768]{2,1,0:T(8,128)(2,1)S(1)} %pad.18.refs_3_, ...), custom_call_target="tpu_custom_call" | custom-call | flops 22318940160 | bytes 7723008 | tf_op jit(solution)/shard_map/triples/pallas_call | solution.py:197
  387.7 17.3 %triples.15 = f32[5,768,88]{2,1,0:T(8,128)S(1)} custom-call(f32[1,24]{1,0:T(1,128)S(1)} %get-tuple-element.139.refs_0_, bf16[2,24,88,128]{3,2,1,0:T(8,128)(2,1)S(1)} %bitcast.263, bf16[2,88,2112]{2,1,0:T(8,128)(2,1)S(1)} %pad_maximum_fusion.5.refs_2_, bf16[5,128,768]{2,1,0:T(8,128)(2,1)S(1)} %pad.18.refs_3_, ...), custom_call_target="tpu_custom_call" | custom-call | flops 22318940160 | bytes 7723008 | tf_op jit(solution)/shard_map/triples/pallas_call | solution.py:197
  406.3 1.9 reshape.577
  409.3 2.4 reshape.578
  411.6 5.7 %all-to-all-start.1 = ((f32[16,40,484]{2,1,0:T(8,128)}), f32[16,40,484]{2,1,0:T(8,128)S(1)}, u32[]{:S(2)}, u32[]{:S(2)}) async-start(f32[16,40,484]{2,1,0:T(8,128)} %reshape.578), calls=%async_computation.1 | async-start | bytes 2621440 | tf_op jit(solution)/shard_map/all_to_all | solution.py:447
  417.5 31.4 %all-to-all-done.1 = f32[16,40,484]{2,1,0:T(8,128)S(1)} async-done(((f32[16,40,484]{2,1,0:T(8,128)}), f32[16,40,484]{2,1,0:T(8,128)S(1)}, u32[]{:S(2)}, u32[]{:S(2)}) %all-to-all-start.1) | async-done | bytes 1239072 | tf_op jit(solution)/shard_map/all_to_all | solution.py:447
  449.5 2.4 gather_fusion.13
  (319 shorter events, 60.1 us)
Async XLA Ops:
  0.0 35.2 %copy-start = (bf16[5,8,7744]{2,1,0:T(8,128)(2,1)S(1)}, bf16[5,8,7744]{2,1,0:T(8,128)(2,1)}, u32[]{:S(2)}) copy-start(bf16[5,8,7744]{2,1,0:T(8,128)(2,1)} %param.10) | copy-start | bytes 1858564
  3.8 4.0 copy-start.21
  6.7 23.2 %collective-permute-start.3 = (bf16[4,88,1408]{2,1,0:T(8,128)(2,1)}, bf16[4,88,1408]{2,1,0:T(8,128)(2,1)}, u32[]{:S(2)}, u32[]{:S(2)}) collective-permute-start(bf16[4,88,1408]{2,1,0:T(8,128)(2,1)} %dynamic-slice_bitcast_fusion.2), channel_id=1, source_target_pairs={{0,1},{1,0},{2,3},{3,2},{4,5},{5,4},{6,7},{7,6},{8,9},{9,8},{10,11... | collective-permute-start | bytes 2973704 | tf_op jit(solution)/shard_map/ppermute | solution.py:217
  7.8 36.4 %collective-permute-start.2 = (bf16[4,88,1408]{2,1,0:T(8,128)(2,1)}, bf16[4,88,1408]{2,1,0:T(8,128)(2,1)}, u32[]{:S(2)}, u32[]{:S(2)}) collective-permute-start(bf16[4,88,1408]{2,1,0:T(8,128)(2,1)} %dynamic-slice_bitcast_fusion.3), channel_id=1, source_target_pairs={{0,1},{1,0},{2,3},{3,2},{4,5},{5,4},{6,7},{7,6},{8,9},{9,8},{10,11... | collective-permute-start | bytes 2973704 | tf_op jit(solution)/shard_map/ppermute | solution.py:217
  13.2 90.6 %collective-permute-start.1 = (bf16[4,88,2816]{2,1,0:T(8,128)(2,1)}, bf16[4,88,2816]{2,1,0:T(8,128)(2,1)}, u32[]{:S(2)}, u32[]{:S(2)}) collective-permute-start(bf16[4,88,2816]{2,1,0:T(8,128)(2,1)} %dynamic-slice_bitcast_fusion), channel_id=1, source_target_pairs={{0,1},{1,0},{2,3},{3,2},{4,5},{5,4},{6,7},{7,6},{8,9},{9,8},{10,11... | collective-permute-start | bytes 5947400 | tf_op jit(solution)/shard_map/ppermute | solution.py:217
  15.3 3.4 copy-start.46
  15.3 3.5 copy-start.53
  15.4 3.5 copy-start.50
  15.4 4.1 copy-start.8
  15.4 6.7 %copy-start.51 = (s32[5]{0:T(128)S(1)}, s32[5]{0:T(128)}, u32[]{:S(2)}) copy-start(s32[5]{0:T(128)} %param.17) | copy-start | bytes 64
  15.4 6.7 %copy-start.52 = (s32[5]{0:T(128)S(1)}, s32[5]{0:T(128)}, u32[]{:S(2)}) copy-start(s32[5]{0:T(128)} %param.16) | copy-start | bytes 64
  17.0 7.1 %copy-start.47 = (f32[8,88]{1,0:T(8,128)S(1)}, f32[8,88]{1,0:T(8,128)}, u32[]{:S(2)}) copy-start(f32[8,88]{1,0:T(8,128)} %param.14) | copy-start | bytes 8452
  17.0 8.9 %copy-start.9 = (f32[30]{0:T(128)S(1)}, f32[30]{0:T(128)}, u32[]{:S(2)}) copy-start(f32[30]{0:T(128)} %param.13) | copy-start | bytes 364
  18.3 27.9 %collective-permute-start = (bf16[4,88,2112]{2,1,0:T(8,128)(2,1)}, bf16[4,88,2112]{2,1,0:T(8,128)(2,1)}, u32[]{:S(2)}, u32[]{:S(2)}) collective-permute-start(bf16[4,88,2112]{2,1,0:T(8,128)(2,1)} %dynamic-slice_bitcast_fusion.1), channel_id=1, source_target_pairs={{0,1},{1,0},{2,3},{3,2},{4,5},{5,4},{6,7},{7,6},{8,9},{9,8},{10,11... | collective-permute-start | bytes 4460552 | tf_op jit(solution)/shard_map/ppermute | solution.py:217
  18.8 9.9 %collective-permute-start.12 = (bf16[2,30,30,88]{3,0,2,1:T(2,128)(2,1)S(1)}, bf16[2,30,30,88]{3,0,2,1:T(2,128)(2,1)}, u32[]{:S(2)}, u32[]{:S(2)}) collective-permute-start(bf16[2,30,30,88]{3,0,2,1:T(2,128)(2,1)S(1)} %copy-done.46), channel_id=1, source_target_pairs={{0,1},{1,0},{2,3},{3,2},{4,5},{5,4},{6,7},{7,6},{8,9},{9,8},{10,11... | collective-permute-start | bytes 950408 | tf_op jit(solution)/shard_map/ppermute | solution.py:217
  20.1 9.8 %copy-start.22 = (bf16[8,88,1408]{2,1,0:T(8,128)(2,1)S(1)}, bf16[8,88,1408]{2,1,0:T(8,128)(2,1)}, u32[]{:S(2)}) copy-start(bf16[8,88,1408]{2,1,0:T(8,128)(2,1)} %get-tuple-element.74) | copy-start | bytes 5947396
  32.7 25.5 %collective-permute-start.4 = (bf16[4,88,1408]{2,1,0:T(8,128)(2,1)}, bf16[4,88,1408]{2,1,0:T(8,128)(2,1)}, u32[]{:S(2)}, u32[]{:S(2)}) collective-permute-start(bf16[4,88,1408]{2,1,0:T(8,128)(2,1)} %get-tuple-element.99), channel_id=1, source_target_pairs={{0,2},{2,0},{4,6},{6,4},{8,10},{10,8},{12,14},{14,12},{16,18},{18,... | collective-permute-start | bytes 2973704 | tf_op jit(solution)/shard_map/ppermute | solution.py:222
  37.4 97.1 %all-to-all-start = ((bf16[16,16,3872]{2,1,0:T(8,128)(2,1)}), bf16[16,16,3872]{2,1,0:T(8,128)(2,1)S(1)}, u32[]{:S(2)}, u32[]{:S(2)}) async-start(bf16[16,16,3872]{2,1,0:T(8,128)(2,1)} %bitcast.277), calls=%async_computation | async-start | bytes 4063232 | tf_op jit(solution)/shard_map/all_to_all | solution.py:344
  46.1 14.8 %copy-start.20 = (bf16[4,88,1408]{2,1,0:T(8,128)(2,1)S(1)}, bf16[4,88,1408]{2,1,0:T(8,128)(2,1)}, u32[]{:S(2)}) copy-start(bf16[4,88,1408]{2,1,0:T(8,128)(2,1)} %get-tuple-element.98) | copy-start | bytes 2973700
  58.2 43.4 %collective-permute-start.5 = (bf16[4,88,1408]{2,1,0:T(8,128)(2,1)S(1)}, bf16[4,88,1408]{2,1,0:T(8,128)(2,1)S(1)}, u32[]{:S(2)}, u32[]{:S(2)}) collective-permute-start(bf16[4,88,1408]{2,1,0:T(8,128)(2,1)S(1)} %get-tuple-element.38), channel_id=1, source_target_pairs={{0,2},{2,0},{4,6},{6,4},{8,10},{10,8},{12,14},{14,12},{16,18},{18,... | collective-permute-start | bytes 2973704 | tf_op jit(solution)/shard_map/ppermute | solution.py:222
  64.3 39.2 %collective-permute-start.8 = (bf16[2,2,88,1408]{3,2,1,0:T(8,128)(2,1)S(1)}, bf16[2,2,88,1408]{3,2,1,0:T(8,128)(2,1)S(1)}, u32[]{:S(2)}, u32[]{:S(2)}) collective-permute-start(bf16[2,2,88,1408]{3,2,1,0:T(8,128)(2,1)S(1)} %pad_maximum_fusion.2), channel_id=1, source_target_pairs={{0,4},{2,6},{4,0},{6,2},{8,12},{10,14},{12,8},{14,10},{16,20},{18,... | collective-permute-start | bytes 2973704 | tf_op jit(solution)/shard_map/ppermute | solution.py:222
  103.8 13.4 %collective-permute-start.9 = (bf16[2,88,1408]{2,1,0:T(8,128)(2,1)S(1)}, bf16[2,88,1408]{2,1,0:T(8,128)(2,1)S(1)}, u32[]{:S(2)}, u32[]{:S(2)}) collective-permute-start(bf16[2,88,1408]{2,1,0:T(8,128)(2,1)S(1)} %fusion.34), channel_id=1, source_target_pairs={{0,8},{2,10},{4,12},{6,14},{8,0},{10,2},{12,4},{14,6},{16,24},{18,... | collective-permute-start | bytes 1486856 | tf_op jit(solution)/shard_map/ppermute | solution.py:222
  109.3 24.0 %collective-permute-start.13 = (bf16[2,2,88,1408]{3,2,1,0:T(8,128)(2,1)S(1)}, bf16[2,2,88,1408]{3,2,1,0:T(8,128)(2,1)S(1)}, u32[]{:S(2)}, u32[]{:S(2)}) collective-permute-start(bf16[2,2,88,1408]{3,2,1,0:T(8,128)(2,1)S(1)} %pad_maximum_fusion.3), channel_id=1, source_target_pairs={{0,4},{2,6},{4,0},{6,2},{8,12},{10,14},{12,8},{14,10},{16,20},{18,... | collective-permute-start | bytes 2973704 | tf_op jit(solution)/shard_map/ppermute | solution.py:222
  109.7 58.9 %collective-permute-start.6 = (bf16[4,88,2816]{2,1,0:T(8,128)(2,1)}, bf16[4,88,2816]{2,1,0:T(8,128)(2,1)}, u32[]{:S(2)}, u32[]{:S(2)}) collective-permute-start(bf16[4,88,2816]{2,1,0:T(8,128)(2,1)} %get-tuple-element.39), channel_id=1, source_target_pairs={{0,2},{2,0},{4,6},{6,4},{8,10},{10,8},{12,14},{14,12},{16,18},{18,... | collective-permute-start | bytes 5947400 | tf_op jit(solution)/shard_map/ppermute | solution.py:222
  117.5 16.9 %copy-start.30 = (bf16[2,88,1408]{2,1,0:T(8,128)(2,1)}, bf16[2,88,1408]{2,1,0:T(8,128)(2,1)S(1)}, u32[]{:S(2)}) copy-start(bf16[2,88,1408]{2,1,0:T(8,128)(2,1)S(1)} %fusion.38) | copy-start | bytes 1486852
  117.5 1.6 collective-permute-start.10
  117.6 17.5 %copy-start.26 = (bf16[1,2,88,1408]{3,2,1,0:T(8,128)(2,1)}, bf16[1,2,88,1408]{3,2,1,0:T(8,128)(2,1)S(1)}, u32[]{:S(2)}) copy-start(bf16[1,2,88,1408]{3,2,1,0:T(8,128)(2,1)S(1)} %maximum_bitcast_fusion.15) | copy-start | bytes 1486852
  117.7 16.7 %copy-start.28 = (bf16[1,2,88,1408]{3,2,1,0:T(8,128)(2,1)}, bf16[1,2,88,1408]{3,2,1,0:T(8,128)(2,1)S(1)}, u32[]{:S(2)}) copy-start(bf16[1,2,88,1408]{3,2,1,0:T(8,128)(2,1)S(1)} %maximum_bitcast_fusion.14) | copy-start | bytes 1486852
  119.9 61.4 %collective-permute-start.11 = (bf16[88,1408]{1,0:T(8,128)(2,1)}, bf16[88,1408]{1,0:T(8,128)(2,1)}, u32[]{:S(2)}, u32[]{:S(2)}) collective-permute-start(bf16[88,1408]{1,0:T(8,128)(2,1)} %bitcast_select_fusion.14), channel_id=1, source_target_pairs={{0,16},{2,18},{4,20},{6,22},{8,24},{10,26},{12,28},{14,30},{16,0},... | collective-permute-start | bytes 743432 | tf_op jit(solution)/shard_map/ppermute | solution.py:222
  134.4 49.3 %collective-permute-start.15 = (bf16[2,88,1408]{2,1,0:T(8,128)(2,1)}, bf16[2,88,1408]{2,1,0:T(8,128)(2,1)}, u32[]{:S(2)}, u32[]{:S(2)}) collective-permute-start(bf16[2,88,1408]{2,1,0:T(8,128)(2,1)} %fusion.31), channel_id=1, source_target_pairs={{0,8},{2,10},{4,12},{6,14},{8,0},{10,2},{12,4},{14,6},{16,24},{18,... | collective-permute-start | bytes 1486856 | tf_op jit(solution)/shard_map/ppermute | solution.py:222
  153.5 2.8 slice-start
  163.4 5.1 %copy-start.11 = (bf16[4,88,2816]{2,1,0:T(8,128)(2,1)S(1)}, bf16[4,88,2816]{2,1,0:T(8,128)(2,1)}, u32[]{:S(2)}) copy-start(bf16[4,88,2816]{2,1,0:T(8,128)(2,1)} %get-tuple-element.76) | copy-start | bytes 5947396
  168.5 57.0 %collective-permute-start.7 = (bf16[4,88,2112]{2,1,0:T(8,128)(2,1)}, bf16[4,88,2112]{2,1,0:T(8,128)(2,1)}, u32[]{:S(2)}, u32[]{:S(2)}) collective-permute-start(bf16[4,88,2112]{2,1,0:T(8,128)(2,1)} %get-tuple-element.40), channel_id=1, source_target_pairs={{0,2},{2,0},{4,6},{6,4},{8,10},{10,8},{12,14},{14,12},{16,18},{18,... | collective-permute-start | bytes 4460552 | tf_op jit(solution)/shard_map/ppermute | solution.py:222
  175.4 69.0 %collective-permute-start.20 = (bf16[2,2,88,2816]{3,2,1,0:T(8,128)(2,1)}, bf16[2,2,88,2816]{3,2,1,0:T(8,128)(2,1)}, u32[]{:S(2)}, u32[]{:S(2)}) collective-permute-start(bf16[2,2,88,2816]{3,2,1,0:T(8,128)(2,1)} %pad_maximum_fusion), channel_id=1, source_target_pairs={{0,4},{2,6},{4,0},{6,2},{8,12},{10,14},{12,8},{14,10},{16,20},{18,... | collective-permute-start | bytes 5947400 | tf_op jit(solution)/shard_map/ppermute | solution.py:222
  178.9 3.5 copy-start.33
  178.9 3.5 copy-start.34
  181.2 11.4 %copy-start.2 = (bf16[2,5,16,16,768]{4,3,2,1,0:T(8,128)(2,1)}, bf16[2,5,16,16,768]{4,3,2,1,0:T(8,128)(2,1)S(1)}, u32[]{:S(2)}) copy-start(bf16[2,5,16,16,768]{4,3,2,1,0:T(8,128)(2,1)S(1)} %convolution_bitcast_fusion.3.refs_4_) | copy-start | bytes 11796484
  182.0 1.6 collective-permute-start.14
  185.8 6.8 %copy-start.32 = (bf16[2,88,1408]{2,1,0:T(8,128)(2,1)}, bf16[2,88,1408]{2,1,0:T(8,128)(2,1)S(1)}, u32[]{:S(2)}) copy-start(bf16[2,88,1408]{2,1,0:T(8,128)(2,1)S(1)} %fusion.28) | copy-start | bytes 1486852
  185.8 1.6 collective-permute-start.16
  187.4 5.3 %copy-start.44 = (bf16[88,1408]{1,0:T(8,128)(2,1)}, bf16[88,1408]{1,0:T(8,128)(2,1)S(1)}, u32[]{:S(2)}) copy-start(bf16[88,1408]{1,0:T(8,128)(2,1)S(1)} %collective-permute-done.16) | copy-start | bytes 743428
  188.2 20.3 %collective-permute-start.17 = (bf16[88,1408]{1,0:T(8,128)(2,1)}, bf16[88,1408]{1,0:T(8,128)(2,1)}, u32[]{:S(2)}, u32[]{:S(2)}) collective-permute-start(bf16[88,1408]{1,0:T(8,128)(2,1)} %bitcast_select_fusion.13), channel_id=1, source_target_pairs={{0,16},{2,18},{4,20},{6,22},{8,24},{10,26},{12,28},{14,30},{16,0},... | collective-permute-start | bytes 743432 | tf_op jit(solution)/shard_map/ppermute | solution.py:222
  205.2 3.2 copy-start.45
  210.1 2.7 collective-permute-start.18
  210.4 3.0 copy-start.3
  214.1 11.4 %copy-start.14 = (bf16[4,88,2112]{2,1,0:T(8,128)(2,1)S(1)}, bf16[4,88,2112]{2,1,0:T(8,128)(2,1)}, u32[]{:S(2)}) copy-start(bf16[4,88,2112]{2,1,0:T(8,128)(2,1)} %get-tuple-element.78) | copy-start | bytes 4460548
  231.6 52.6 %collective-permute-start.19 = (bf16[2,2,88,2112]{3,2,1,0:T(8,128)(2,1)}, bf16[2,2,88,2112]{3,2,1,0:T(8,128)(2,1)}, u32[]{:S(2)}, u32[]{:S(2)}) collective-permute-start(bf16[2,2,88,2112]{3,2,1,0:T(8,128)(2,1)} %pad_maximum_fusion.1), channel_id=1, source_target_pairs={{0,4},{2,6},{4,0},{6,2},{8,12},{10,14},{12,8},{14,10},{16,20},{18,... | collective-permute-start | bytes 4460552 | tf_op jit(solution)/shard_map/ppermute | solution.py:222
  232.7 11.8 %copy-start.17 = (bf16[1,2,88,2816]{3,2,1,0:T(8,128)(2,1)S(1)}, bf16[1,2,88,2816]{3,2,1,0:T(8,128)(2,1)}, u32[]{:S(2)}) copy-start(bf16[1,2,88,2816]{3,2,1,0:T(8,128)(2,1)} %maximum_bitcast_fusion.3) | copy-start | bytes 2973700
  232.7 11.8 %copy-start.18 = (bf16[1,2,88,2816]{3,2,1,0:T(8,128)(2,1)S(1)}, bf16[1,2,88,2816]{3,2,1,0:T(8,128)(2,1)}, u32[]{:S(2)}) copy-start(bf16[1,2,88,2816]{3,2,1,0:T(8,128)(2,1)} %maximum_bitcast_fusion.2) | copy-start | bytes 2973700
  247.1 25.4 %collective-permute-start.21 = (bf16[2,88,2816]{2,1,0:T(8,128)(2,1)}, bf16[2,88,2816]{2,1,0:T(8,128)(2,1)}, u32[]{:S(2)}, u32[]{:S(2)}) collective-permute-start(bf16[2,88,2816]{2,1,0:T(8,128)(2,1)} %fusion.13), channel_id=1, source_target_pairs={{0,8},{2,10},{4,12},{6,14},{8,0},{10,2},{12,4},{14,6},{16,24},{18,... | collective-permute-start | bytes 2973704 | tf_op jit(solution)/shard_map/ppermute | solution.py:222
  265.7 6.7 %copy-start.19 = (bf16[1,2,88,2816]{3,2,1,0:T(8,128)(2,1)S(1)}, bf16[1,2,88,2816]{3,2,1,0:T(8,128)(2,1)}, u32[]{:S(2)}) copy-start(bf16[1,2,88,2816]{3,2,1,0:T(8,128)(2,1)} %maximum_bitcast_fusion.2) | copy-start | bytes 2973700
  274.6 2.4 collective-permute-start.22
  277.8 21.7 %collective-permute-start.24 = (bf16[88,2816]{1,0:T(8,128)(2,1)}, bf16[88,2816]{1,0:T(8,128)(2,1)}, u32[]{:S(2)}, u32[]{:S(2)}) collective-permute-start(bf16[88,2816]{1,0:T(8,128)(2,1)} %bitcast_select_fusion.9), channel_id=1, source_target_pairs={{0,16},{2,18},{4,20},{6,22},{8,24},{10,26},{12,28},{14,30},{16,0},... | collective-permute-start | bytes 1486856 | tf_op jit(solution)/shard_map/ppermute | solution.py:222
  281.2 3.0 copy-start.23
  284.2 15.3 %copy-start.25 = (bf16[2,88,2816]{2,1,0:T(8,128)(2,1)S(1)}, bf16[2,88,2816]{2,1,0:T(8,128)(2,1)}, u32[]{:S(2)}) copy-start(bf16[2,88,2816]{2,1,0:T(8,128)(2,1)} %copy-done.24) | copy-start | bytes 2973700
  300.2 3.8 collective-permute-start.25
  301.3 20.4 %collective-permute-start.23 = (bf16[2,88,2112]{2,1,0:T(8,128)(2,1)S(1)}, bf16[2,88,2112]{2,1,0:T(8,128)(2,1)S(1)}, u32[]{:S(2)}, u32[]{:S(2)}) collective-permute-start(bf16[2,88,2112]{2,1,0:T(8,128)(2,1)S(1)} %fusion.20), channel_id=1, source_target_pairs={{0,8},{2,10},{4,12},{6,14},{8,0},{10,2},{12,4},{14,6},{16,24},{18,... | collective-permute-start | bytes 2230280 | tf_op jit(solution)/shard_map/ppermute | solution.py:222
  323.2 4.4 copy-start.5
  323.2 1.8 collective-permute-start.26
  325.1 23.1 %collective-permute-start.27 = (bf16[88,2112]{1,0:T(8,128)(2,1)S(1)}, bf16[88,2112]{1,0:T(8,128)(2,1)S(1)}, u32[]{:S(2)}, u32[]{:S(2)}) collective-permute-start(bf16[88,2112]{1,0:T(8,128)(2,1)S(1)} %bitcast_select_fusion.10), channel_id=1, source_target_pairs={{0,16},{2,18},{4,20},{6,22},{8,24},{10,26},{12,28},{14,30},{16,0},... | collective-permute-start | bytes 1115144 | tf_op jit(solution)/shard_map/ppermute | solution.py:222
  348.9 1.8 collective-permute-start.28
  409.3 8.1 %copy-start.49 = (s32[5]{0:T(128)S(1)}, s32[5]{0:T(128)}, u32[]{:S(2)}) copy-start(s32[5]{0:T(128)} %copy-done.48) | copy-start | bytes 64
  411.6 37.3 %all-to-all-start.1 = ((f32[16,40,484]{2,1,0:T(8,128)}), f32[16,40,484]{2,1,0:T(8,128)S(1)}, u32[]{:S(2)}, u32[]{:S(2)}) async-start(f32[16,40,484]{2,1,0:T(8,128)} %reshape.578), calls=%async_computation.1 | async-start | bytes 2621440 | tf_op jit(solution)/shard_map/all_to_all | solution.py:447
  449.2 2.8 copy-start.1
  (22 other events, 38.0 us)

commit v2 on v1

--- a/solution.py
+++ b/solution.py
@@ -425,22 +425,22 @@
             areps[1] = spread_holes(1, total)
             total = after(total, ready[1])
         elif n == 1:
-            to_low(3, total)
+            to_high(2, total)
+            to_low(3, sent_z[2])
             total = after(total, sent_y[3])
         elif n == 2:
-            to_high(2, total)
-            total = after(total, sent_z[2])
+            to_top(2, total)
+            total = after(total, sent_h[2])
         elif n == 3:
             areps[2] = spread_holes(2, total)
-            to_top(2, areps[2])
-            areps[3] = spread_holes(3, sent_h[2])
+            areps[3] = spread_holes(3, areps[2])
             to_high(3, areps[3])
             arrive(2, sent_z[3])
-            to_top(3, ready[2])
+        elif n == 4:
+            to_top(3, total)
             total = after(total, sent_h[3])
-        elif n == 4:
+        elif n == 5:
             arrive(3, total)
-            total = after(total, ready[3])
     total = total[:, :used].reshape(pairs, share)[rank]
     cut = 8 if share % 8 == 0 else 1
     total = total.reshape(chips, local_pairs * cut, share // cut)

time: 457 us -> 432 us (0.945)
  waiting for transfers between devices: 131 us -> 106 us
    ppermute x16, waiting for transfers between devices: 94.5 us -> 68.5 us  [across(): return lax.ppermute(x, 'pair', [(t, t ^ bit) for t in range(count)])]
    unnamed x109 -> x99, local copies, waits for them, and re-layouts: 10 us -> 9.36 us
  transfers between devices with their start and end apart: 31 -> 31, of which waited for: 12 -> 12; matrix products, arithmetic and copies ran while one was open for 29% -> 32% of each run, Pallas kernels for 15% -> 20%
where the time goes in v2:
time: 432 us; the launch traced here: 427 us
  Pallas kernels  121 us (28%)
  waiting for transfers between devices  106 us (25%)
  local copies, waits for them, and re-layouts  86 us (20%)
  other arithmetic  55 us (13%)
  starting transfers between devices  34.8 us (8%)
  matrix products  20.4 us (5%)
    pallas_call x8, Pallas kernels, triples_call(): pl.pallas_call(functools.partial(triples_kernel, last), grid=(groups,), i...  121 us
    ppermute x16, waiting for transfers between devices, across(): return lax.ppermute(x, 'pair', [(t, t ^ bit) for t in range(count)])  68.5 us
    all_to_all x1, waiting for transfers between devices, on_device_scatter(): came = lax.all_to_all(total, 'pair', 0, 0, tiled=True)  31.8 us
    ppermute x16, starting transfers between devices, across(): return lax.ppermute(x, 'pair', [(t, t ^ bit) for t in range(count)])  19.5 us
    dot_general x4, matrix products, spread_holes(): return jnp.einsum('wgqab,ae->wgbqe', hole, spread)  14.3 us
    select_n x4, other arithmetic, block(): return jnp.where(self.from_here(0)[w], pick(kept, beta), pick(came, beta))  14 us
    optimization_barrier x4, local copies, waits for them, and re-layouts, after(): return lax.optimization_barrier((x,) + others)[0]  13.8 us
    select_n x4, other arithmetic, split_cores(): return (jnp.where(same, mine, theirs), jnp.where(same, theirs, mine))  11.5 us
  transfers between devices with their start and end apart: 31, of which 12 were waited for; matrix products, arithmetic and copies ran while one was open for 32% of the time, Pallas kernels for 20%

profile of v2, /device:TPU:12, one launch (start us, length us, event | category | flops | bytes accessed | tf_op | source)
XLA Modules:
  0.0 427.0 jit_solution(6514459739281938628)
XLA Ops:
  0.0 3.8 fusion.93
  3.8 2.9 dynamic-slice_bitcast_fusion.2
  8.3 2.4 slice.256
  10.7 1.5 dynamic-slice_bitcast_fusion
  13.2 2.1 slice.255
  15.4 1.5 copy-done.15
  28.8 2.3 fusion.41
  31.0 2.7 bitcast_select_fusion.4
  33.7 1.5 collective-permute-start.4
  35.4 2.0 fusion.43
  37.4 6.9 %all-to-all-start = ((bf16[16,16,3872]{2,1,0:T(8,128)(2,1)}), bf16[16,16,3872]{2,1,0:T(8,128)(2,1)S(1)}, u32[]{:S(2)}, u32[]{:S(2)}) async-start(bf16[16,16,3872]{2,1,0:T(8,128)(2,1)} %bitcast.277), calls=%async_computation | async-start | bytes 4063232 | tf_op jit(solution)/shard_map/all_to_all | solution.py:344
  44.3 1.8 bitcast_select_fusion.6
  46.7 3.3 bitcast_select_fusion.3
  50.0 8.8 %collective-permute-done.4 = bf16[4,88,1408]{2,1,0:T(8,128)(2,1)} collective-permute-done((bf16[4,88,1408]{2,1,0:T(8,128)(2,1)}, bf16[4,88,1408]{2,1,0:T(8,128)(2,1)}, u32[]{:S(2)}, u32[]{:S(2)}) %collective-permute-start.4) | collective-permute-done | bytes 991264 | tf_op jit(solution)/shard_map/ppermute | solution.py:222
  58.9 2.2 collective-permute-start.5
  61.0 3.3 dynamic-slice_select_fusion.17
  64.8 37.0 %collective-permute-done.5 = bf16[4,88,1408]{2,1,0:T(8,128)(2,1)S(1)} collective-permute-done((bf16[4,88,1408]{2,1,0:T(8,128)(2,1)S(1)}, bf16[4,88,1408]{2,1,0:T(8,128)(2,1)S(1)}, u32[]{:S(2)}, u32[]{:S(2)}) %collective-permute-start.5) | collective-permute-done | bytes 991264 | tf_op jit(solution)/shard_map/ppermute | solution.py:222
  101.8 1.7 dynamic-slice_select_fusion.23
  104.1 1.7 copy-done.13
  105.8 3.7 bitcast_select_fusion
  111.0 6.0 %collective-permute-done.10 = bf16[2,88,1408]{2,1,0:T(8,128)(2,1)S(1)} collective-permute-done((bf16[2,88,1408]{2,1,0:T(8,128)(2,1)S(1)}, bf16[2,88,1408]{2,1,0:T(8,128)(2,1)S(1)}, u32[]{:S(2)}, u32[]{:S(2)}) %collective-permute-start.10) | collective-permute-done | bytes 495648 | tf_op jit(solution)/shard_map/ppermute | solution.py:222
  119.6 2.1 collective-permute-start.13
  121.6 11.3 %collective-permute-done.8 = bf16[2,2,88,1408]{3,2,1,0:T(8,128)(2,1)S(1)} collective-permute-done((bf16[2,2,88,1408]{3,2,1,0:T(8,128)(2,1)S(1)}, bf16[2,2,88,1408]{3,2,1,0:T(8,128)(2,1)S(1)}, u32[]{:S(2)}, u32[]{:S(2)}) %collective-permute-start.8) | collective-permute-done | bytes 991264 | tf_op jit(solution)/shard_map/ppermute | solution.py:222
  141.0 3.0 gather_fusion.6
  143.9 2.5 slice.265
  146.6 4.7 %slice.99 = bf16[2,5,16,44,88]{4,3,2,1,0:T(8,128)(2,1)S(1)} reshape(bf16[160,3872]{1,0:T(8,128)(2,1)} %slice.265) | data formatting | bytes 2478080 | tf_op jit(solution)/shard_map/slice | solution.py:364
  151.3 1.9 slice.269
  153.3 1.9 slice.268
  156.2 2.7 squeeze.289
  160.3 1.6 copy.87
  162.1 1.5 convolution_bitcast_fusion.4
  167.8 5.1 %fusion.94 = (bf16[2,5,16,44,16]{4,3,2,1,0:T(8,128)(2,1)}, bf16[2,5,16,44,16]{4,3,2,1,0:T(8,128)(2,1)}) fusion(bf16[2,5,16,44,88]{4,3,2,1,0:T(8,128)(2,1)} %copy-done.10), kind=kLoop, calls=%fused_computation.270 | loop fusion | bytes 901120 | tf_op jit(solution)/shard_map/slice | solution.py:400
  172.9 5.3 %dynamic-slice_select_fusion.3 = (bf16[1,88,2816]{2,1,0:T(8,128)(2,1)S(1)}, bf16[1,88,2816]{2,1,0:T(8,128)(2,1)S(1)}, bf16[1,88,2816]{2,1,0:T(8,128)(2,1)S(1)}, ...) fusion(bf16[4,88,2816]{2,1,0:T(8,128)(2,1)} %collective-permute, ...), kind=kLoop, calls=%fused_computation.116 | loop fusion | flops 1982464 | bytes 11894818 | tf_op jit(solution)/shard_map/jit(_where)/select_n | solution.py:251
  181.6 3.2 copy.104
  184.8 2.3 convolution_bitcast_fusion.3.refs_4_
  194.1 4.8 %collective-permute-start.18 = (bf16[88,1408]{1,0:T(8,128)(2,1)}, bf16[88,1408]{1,0:T(8,128)(2,1)}, u32[]{:S(2)}, u32[]{:S(2)}) collective-permute-start(bf16[88,1408]{1,0:T(8,128)(2,1)} %bitcast_select_fusion.13), channel_id=1, source_target_pairs={{0,16},{2,18},{4,20},{6,22},{8,24},{10,26},{12,28},{14,30},{16,0},... | collective-permute-start | bytes 743432 | tf_op jit(solution)/shard_map/ppermute | solution.py:222
  199.3 11.5 %triples.8.refs_9_ = f32[5,88,768]{2,1,0:T(8,128)S(1)} custom-call(f32[1,16]{1,0:T(1,128)S(1)} %get-tuple-element.140.refs_0_, bf16[2,16,88,128]{3,2,1,0:T(8,128)(2,1)S(1)} %bitcast.266, bf16[2,88,1408]{2,1,0:T(8,128)(2,1)S(1)} %pad_maximum_fusion.7.refs_2_, bf16[5,128,768]{2,1,0:T(8,128)(2,1)S(1)} %pad.18.refs_3_, ...), custom_call_target="tpu_custom_call" | custom-call | flops 14879293440 | bytes 5148672 | tf_op jit(solution)/shard_map/triples/pallas_call | solution.py:197
  212.0 3.2 copy.106
  215.2 1.6 fusion.47
  217.1 2.4 convolution_bitcast_fusion.2.refs_4_
  220.8 11.4 %triples.9.refs_9_ = f32[5,88,768]{2,1,0:T(8,128)S(1)} custom-call(f32[1,16]{1,0:T(1,128)S(1)} %get-tuple-element.141.refs_0_, bf16[2,16,88,128]{3,2,1,0:T(8,128)(2,1)S(1)} %bitcast.267, bf16[2,88,1408]{2,1,0:T(8,128)(2,1)S(1)} %pad_maximum_fusion.7.refs_2_, bf16[5,128,768]{2,1,0:T(8,128)(2,1)S(1)} %pad.18.refs_3_, ...), custom_call_target="tpu_custom_call" | custom-call | flops 14879293440 | bytes 5148672 | tf_op jit(solution)/shard_map/triples/pallas_call | solution.py:197
  232.3 1.7 fusion.17
  234.5 3.7 dynamic-slice_select_fusion.11
  239.6 1.5 collective-permute-start.20
  241.2 11.7 %triples.10.refs_9_ = f32[5,88,768]{2,1,0:T(8,128)S(1)} custom-call(f32[1,16]{1,0:T(1,128)S(1)} %get-tuple-element.138.refs_0_, bf16[2,16,88,128]{3,2,1,0:T(8,128)(2,1)S(1)} %bitcast.264, bf16[2,88,1408]{2,1,0:T(8,128)(2,1)S(1)} %pad_maximum_fusion.8.refs_2_, bf16[5,128,768]{2,1,0:T(8,128)(2,1)S(1)} %pad.18.refs_3_, ...), custom_call_target="tpu_custom_call" | custom-call | flops 14879293440 | bytes 5148672 | tf_op jit(solution)/shard_map/triples/pallas_call | solution.py:197
  252.9 5.4 %collective-permute-done.21 = bf16[2,88,2816]{2,1,0:T(8,128)(2,1)S(1)} collective-permute-done((bf16[2,88,2816]{2,1,0:T(8,128)(2,1)S(1)}, bf16[2,88,2816]{2,1,0:T(8,128)(2,1)S(1)}, u32[]{:S(2)}, u32[]{:S(2)}) %collective-permute-start.21) | collective-permute-done | bytes 991264 | tf_op jit(solution)/shard_map/ppermute | solution.py:222
  258.2 1.7 fusion.14
  262.4 11.4 %triples.11.refs_9_ = f32[5,88,768]{2,1,0:T(8,128)S(1)} custom-call(f32[1,16]{1,0:T(1,128)S(1)} %get-tuple-element.139.refs_0_, bf16[2,16,88,128]{3,2,1,0:T(8,128)(2,1)S(1)} %bitcast.265, bf16[2,88,1408]{2,1,0:T(8,128)(2,1)S(1)} %pad_maximum_fusion.8.refs_2_, bf16[5,128,768]{2,1,0:T(8,128)(2,1)S(1)} %pad.18.refs_3_, ...), custom_call_target="tpu_custom_call" | custom-call | flops 14879293440 | bytes 5148672 | tf_op jit(solution)/shard_map/triples/pallas_call | solution.py:197
  274.9 4.2 copy.108
  279.1 6.6 %convolution_bitcast_fusion.refs_4_ = bf16[2,5,32,16,768]{4,3,2,1,0:T(8,128)(2,1)} fusion(bf16[2,5,16,44,32]{3,2,4,1,0:T(8,128)(2,1)} %copy.108, s32[768]{0:T(1024)S(1)} %get-tuple-element.156, pred[768]{0:T(1024)(128)(4,1)S(1)} %iota_compare_fusion.8), kind=kOutput, calls=%fused_computation.14 | convolution fusion | flops 346097664 | bytes 8318720 | tf_op jit(solution)/shard_map/wgqab,ae->wgbqe/dot_general | solution.py:401
  285.7 3.3 copy.110
  289.0 3.0 convolution_bitcast_fusion.1.refs_4_
  292.0 1.6 fusion.20
  298.7 20.7 %triples.12.refs_9_ = f32[5,88,768]{2,1,0:T(8,128)S(1)} custom-call(f32[1,32]{1,0:T(1,128)S(1)} %get-tuple-element.137.refs_0_, bf16[2,32,88,128]{3,2,1,0:T(8,128)(2,1)S(1)} %bitcast.260, bf16[2,88,2816]{2,1,0:T(8,128)(2,1)S(1)} %pad_maximum_fusion.4.refs_2_, bf16[5,128,768]{2,1,0:T(8,128)(2,1)S(1)} %pad.18.refs_3_, ...), custom_call_target="tpu_custom_call" | custom-call | flops 29758586880 | bytes 10297344 | tf_op jit(solution)/shard_map/triples/pallas_call | solution.py:197
  319.4 1.5 fusion.24
  322.8 2.9 collective-permute-start.27
  325.7 20.7 %triples.13.refs_9_ = f32[5,88,768]{2,1,0:T(8,128)S(1)} custom-call(f32[1,32]{1,0:T(1,128)S(1)} %get-tuple-element.136.refs_0_, bf16[2,32,88,128]{3,2,1,0:T(8,128)(2,1)S(1)} %bitcast.261, bf16[2,88,2816]{2,1,0:T(8,128)(2,1)S(1)} %pad_maximum_fusion.4.refs_2_, bf16[5,128,768]{2,1,0:T(8,128)(2,1)S(1)} %pad.18.refs_3_, ...), custom_call_target="tpu_custom_call" | custom-call | flops 29758586880 | bytes 10297344 | tf_op jit(solution)/shard_map/triples/pallas_call | solution.py:197
  347.3 1.6 collective-permute-done.28
  349.6 15.9 %triples.14.refs_9_ = f32[5,88,768]{2,1,0:T(8,128)S(1)} custom-call(f32[1,24]{1,0:T(1,128)S(1)} %get-tuple-element.134.refs_0_, bf16[2,24,88,128]{3,2,1,0:T(8,128)(2,1)S(1)} %bitcast.262, bf16[2,88,2112]{2,1,0:T(8,128)(2,1)S(1)} %pad_maximum_fusion.5.refs_2_, bf16[5,128,768]{2,1,0:T(8,128)(2,1)S(1)} %pad.18.refs_3_, ...), custom_call_target="tpu_custom_call" | custom-call | flops 22318940160 | bytes 7723008 | tf_op jit(solution)/shard_map/triples/pallas_call | solution.py:197
  365.5 17.3 %triples.15 = f32[5,768,88]{2,1,0:T(8,128)S(1)} custom-call(f32[1,24]{1,0:T(1,128)S(1)} %get-tuple-element.135.refs_0_, bf16[2,24,88,128]{3,2,1,0:T(8,128)(2,1)S(1)} %bitcast.263, bf16[2,88,2112]{2,1,0:T(8,128)(2,1)S(1)} %pad_maximum_fusion.5.refs_2_, bf16[5,128,768]{2,1,0:T(8,128)(2,1)S(1)} %pad.18.refs_3_, ...), custom_call_target="tpu_custom_call" | custom-call | flops 22318940160 | bytes 7723008 | tf_op jit(solution)/shard_map/triples/pallas_call | solution.py:197
  384.6 2.4 reshape.578
  386.9 4.9 %all-to-all-start.1 = ((f32[16,40,484]{2,1,0:T(8,128)}), f32[16,40,484]{2,1,0:T(8,128)S(1)}, u32[]{:S(2)}, u32[]{:S(2)}) async-start(f32[16,40,484]{2,1,0:T(8,128)} %reshape.578), calls=%async_computation.1 | async-start | bytes 2621440 | tf_op jit(solution)/shard_map/all_to_all | solution.py:447
  392.0 31.8 %all-to-all-done.1 = f32[16,40,484]{2,1,0:T(8,128)S(1)} async-done(((f32[16,40,484]{2,1,0:T(8,128)}), f32[16,40,484]{2,1,0:T(8,128)S(1)}, u32[]{:S(2)}, u32[]{:S(2)}) %all-to-all-start.1) | async-done | bytes 1239072 | tf_op jit(solution)/shard_map/all_to_all | solution.py:447
  424.4 2.4 gather_fusion.13
  (309 shorter events, 62.3 us)
Async XLA Ops:
  0.0 35.2 %copy-start = (bf16[5,8,7744]{2,1,0:T(8,128)(2,1)S(1)}, bf16[5,8,7744]{2,1,0:T(8,128)(2,1)}, u32[]{:S(2)}) copy-start(bf16[5,8,7744]{2,1,0:T(8,128)(2,1)} %param.10) | copy-start | bytes 1858564
  3.8 6.9 %copy-start.20 = (bf16[8,88,1408]{2,1,0:T(8,128)(2,1)}, bf16[8,88,1408]{2,1,0:T(8,128)(2,1)S(1)}, u32[]{:S(2)}) copy-start(bf16[8,88,1408]{2,1,0:T(8,128)(2,1)S(1)} %get-tuple-element.73) | copy-start | bytes 5947396
  6.7 24.3 %collective-permute-start.3 = (bf16[4,88,1408]{2,1,0:T(8,128)(2,1)}, bf16[4,88,1408]{2,1,0:T(8,128)(2,1)}, u32[]{:S(2)}, u32[]{:S(2)}) collective-permute-start(bf16[4,88,1408]{2,1,0:T(8,128)(2,1)} %dynamic-slice_bitcast_fusion.2), channel_id=1, source_target_pairs={{0,1},{1,0},{2,3},{3,2},{4,5},{5,4},{6,7},{7,6},{8,9},{9,8},{10,11... | collective-permute-start | bytes 2973704 | tf_op jit(solution)/shard_map/ppermute | solution.py:217
  7.8 36.5 %collective-permute-start.2 = (bf16[4,88,1408]{2,1,0:T(8,128)(2,1)}, bf16[4,88,1408]{2,1,0:T(8,128)(2,1)}, u32[]{:S(2)}, u32[]{:S(2)}) collective-permute-start(bf16[4,88,1408]{2,1,0:T(8,128)(2,1)} %dynamic-slice_bitcast_fusion.3), channel_id=1, source_target_pairs={{0,1},{1,0},{2,3},{3,2},{4,5},{5,4},{6,7},{7,6},{8,9},{9,8},{10,11... | collective-permute-start | bytes 2973704 | tf_op jit(solution)/shard_map/ppermute | solution.py:217
  10.7 2.6 copy-start.12
  13.2 90.9 %collective-permute-start.1 = (bf16[4,88,2816]{2,1,0:T(8,128)(2,1)}, bf16[4,88,2816]{2,1,0:T(8,128)(2,1)}, u32[]{:S(2)}, u32[]{:S(2)}) collective-permute-start(bf16[4,88,2816]{2,1,0:T(8,128)(2,1)} %dynamic-slice_bitcast_fusion), channel_id=1, source_target_pairs={{0,1},{1,0},{2,3},{3,2},{4,5},{5,4},{6,7},{7,6},{8,9},{9,8},{10,11... | collective-permute-start | bytes 5947400 | tf_op jit(solution)/shard_map/ppermute | solution.py:217
  15.3 3.5 copy-start.48
  15.4 3.5 copy-start.43
  15.4 4.2 copy-start.8
  15.4 6.8 %copy-start.44 = (s32[5]{0:T(128)S(1)}, s32[5]{0:T(128)}, u32[]{:S(2)}) copy-start(s32[5]{0:T(128)} %param.17) | copy-start | bytes 64
  15.4 6.8 %copy-start.45 = (s32[5]{0:T(128)S(1)}, s32[5]{0:T(128)}, u32[]{:S(2)}) copy-start(s32[5]{0:T(128)} %param.16) | copy-start | bytes 64
  16.9 7.2 %copy-start.40 = (f32[8,88]{1,0:T(8,128)S(1)}, f32[8,88]{1,0:T(8,128)}, u32[]{:S(2)}) copy-start(f32[8,88]{1,0:T(8,128)} %param.14) | copy-start | bytes 8452
  16.9 9.0 %copy-start.9 = (f32[30]{0:T(128)S(1)}, f32[30]{0:T(128)}, u32[]{:S(2)}) copy-start(f32[30]{0:T(128)} %param.13) | copy-start | bytes 364
  18.2 27.9 %collective-permute-start = (bf16[4,88,2112]{2,1,0:T(8,128)(2,1)}, bf16[4,88,2112]{2,1,0:T(8,128)(2,1)}, u32[]{:S(2)}, u32[]{:S(2)}) collective-permute-start(bf16[4,88,2112]{2,1,0:T(8,128)(2,1)} %dynamic-slice_bitcast_fusion.1), channel_id=1, source_target_pairs={{0,1},{1,0},{2,3},{3,2},{4,5},{5,4},{6,7},{7,6},{8,9},{9,8},{10,11... | collective-permute-start | bytes 4460552 | tf_op jit(solution)/shard_map/ppermute | solution.py:217
  18.8 10.0 %collective-permute-start.14 = (bf16[2,30,30,88]{3,0,2,1:T(2,128)(2,1)}, bf16[2,30,30,88]{3,0,2,1:T(2,128)(2,1)}, u32[]{:S(2)}, u32[]{:S(2)}) collective-permute-start(bf16[2,30,30,88]{3,0,2,1:T(2,128)(2,1)} %param.12), channel_id=1, source_target_pairs={{0,1},{1,0},{2,3},{3,2},{4,5},{5,4},{6,7},{7,6},{8,9},{9,8},{10,11... | collective-permute-start | bytes 950408 | tf_op jit(solution)/shard_map/ppermute | solution.py:217
  20.2 10.9 %copy-start.21 = (bf16[8,88,1408]{2,1,0:T(8,128)(2,1)S(1)}, bf16[8,88,1408]{2,1,0:T(8,128)(2,1)}, u32[]{:S(2)}) copy-start(bf16[8,88,1408]{2,1,0:T(8,128)(2,1)} %get-tuple-element.72) | copy-start | bytes 5947396
  33.7 25.1 %collective-permute-start.4 = (bf16[4,88,1408]{2,1,0:T(8,128)(2,1)}, bf16[4,88,1408]{2,1,0:T(8,128)(2,1)}, u32[]{:S(2)}, u32[]{:S(2)}) collective-permute-start(bf16[4,88,1408]{2,1,0:T(8,128)(2,1)} %get-tuple-element.97), channel_id=1, source_target_pairs={{0,2},{2,0},{4,6},{6,4},{8,10},{10,8},{12,14},{14,12},{16,18},{18,... | collective-permute-start | bytes 2973704 | tf_op jit(solution)/shard_map/ppermute | solution.py:222
  37.4 96.8 %all-to-all-start = ((bf16[16,16,3872]{2,1,0:T(8,128)(2,1)}), bf16[16,16,3872]{2,1,0:T(8,128)(2,1)S(1)}, u32[]{:S(2)}, u32[]{:S(2)}) async-start(bf16[16,16,3872]{2,1,0:T(8,128)(2,1)} %bitcast.277), calls=%async_computation | async-start | bytes 4063232 | tf_op jit(solution)/shard_map/all_to_all | solution.py:344
  44.3 2.5 copy-start.16
  46.1 14.9 %copy-start.19 = (bf16[4,88,1408]{2,1,0:T(8,128)(2,1)S(1)}, bf16[4,88,1408]{2,1,0:T(8,128)(2,1)}, u32[]{:S(2)}) copy-start(bf16[4,88,1408]{2,1,0:T(8,128)(2,1)} %get-tuple-element.96) | copy-start | bytes 2973700
  58.9 43.0 %collective-permute-start.5 = (bf16[4,88,1408]{2,1,0:T(8,128)(2,1)S(1)}, bf16[4,88,1408]{2,1,0:T(8,128)(2,1)S(1)}, u32[]{:S(2)}, u32[]{:S(2)}) collective-permute-start(bf16[4,88,1408]{2,1,0:T(8,128)(2,1)S(1)} %get-tuple-element.37), channel_id=1, source_target_pairs={{0,2},{2,0},{4,6},{6,4},{8,10},{10,8},{12,14},{14,12},{16,18},{18,... | collective-permute-start | bytes 2973704 | tf_op jit(solution)/shard_map/ppermute | solution.py:222
  64.6 39.2 %collective-permute-start.9 = (bf16[2,2,88,1408]{3,2,1,0:T(8,128)(2,1)S(1)}, bf16[2,2,88,1408]{3,2,1,0:T(8,128)(2,1)S(1)}, u32[]{:S(2)}, u32[]{:S(2)}) collective-permute-start(bf16[2,2,88,1408]{3,2,1,0:T(8,128)(2,1)S(1)} %pad_maximum_fusion.2), channel_id=1, source_target_pairs={{0,4},{2,6},{4,0},{6,2},{8,12},{10,14},{12,8},{14,10},{16,20},{18,... | collective-permute-start | bytes 2973704 | tf_op jit(solution)/shard_map/ppermute | solution.py:222
  104.0 12.9 %collective-permute-start.10 = (bf16[2,88,1408]{2,1,0:T(8,128)(2,1)S(1)}, bf16[2,88,1408]{2,1,0:T(8,128)(2,1)S(1)}, u32[]{:S(2)}, u32[]{:S(2)}) collective-permute-start(bf16[2,88,1408]{2,1,0:T(8,128)(2,1)S(1)} %fusion.27), channel_id=1, source_target_pairs={{0,8},{2,10},{4,12},{6,14},{8,0},{10,2},{12,4},{14,6},{16,24},{18,... | collective-permute-start | bytes 1486856 | tf_op jit(solution)/shard_map/ppermute | solution.py:222
  109.5 23.5 %collective-permute-start.8 = (bf16[2,2,88,1408]{3,2,1,0:T(8,128)(2,1)S(1)}, bf16[2,2,88,1408]{3,2,1,0:T(8,128)(2,1)S(1)}, u32[]{:S(2)}, u32[]{:S(2)}) collective-permute-start(bf16[2,2,88,1408]{3,2,1,0:T(8,128)(2,1)S(1)} %pad_maximum_fusion.3), channel_id=1, source_target_pairs={{0,4},{2,6},{4,0},{6,2},{8,12},{10,14},{12,8},{14,10},{16,20},{18,... | collective-permute-start | bytes 2973704 | tf_op jit(solution)/shard_map/ppermute | solution.py:222
  109.7 63.1 %collective-permute-start.6 = (bf16[4,88,2816]{2,1,0:T(8,128)(2,1)}, bf16[4,88,2816]{2,1,0:T(8,128)(2,1)}, u32[]{:S(2)}, u32[]{:S(2)}) collective-permute-start(bf16[4,88,2816]{2,1,0:T(8,128)(2,1)} %get-tuple-element.38), channel_id=1, source_target_pairs={{0,2},{2,0},{4,6},{6,4},{8,10},{10,8},{12,14},{14,12},{16,18},{18,... | collective-permute-start | bytes 5947400 | tf_op jit(solution)/shard_map/ppermute | solution.py:222
  117.2 16.8 %copy-start.30 = (bf16[2,88,1408]{2,1,0:T(8,128)(2,1)}, bf16[2,88,1408]{2,1,0:T(8,128)(2,1)S(1)}, u32[]{:S(2)}) copy-start(bf16[2,88,1408]{2,1,0:T(8,128)(2,1)S(1)} %fusion.31) | copy-start | bytes 1486852
  117.3 1.6 collective-permute-start.11
  117.4 17.4 %copy-start.26 = (bf16[1,2,88,1408]{3,2,1,0:T(8,128)(2,1)}, bf16[1,2,88,1408]{3,2,1,0:T(8,128)(2,1)S(1)}, u32[]{:S(2)}) copy-start(bf16[1,2,88,1408]{3,2,1,0:T(8,128)(2,1)S(1)} %maximum_bitcast_fusion.11) | copy-start | bytes 1486852
  117.5 16.6 %copy-start.28 = (bf16[1,2,88,1408]{3,2,1,0:T(8,128)(2,1)}, bf16[1,2,88,1408]{3,2,1,0:T(8,128)(2,1)S(1)}, u32[]{:S(2)}) copy-start(bf16[1,2,88,1408]{3,2,1,0:T(8,128)(2,1)S(1)} %maximum_bitcast_fusion.10) | copy-start | bytes 1486852
  119.6 67.6 %collective-permute-start.13 = (bf16[88,1408]{1,0:T(8,128)(2,1)}, bf16[88,1408]{1,0:T(8,128)(2,1)}, u32[]{:S(2)}, u32[]{:S(2)}) collective-permute-start(bf16[88,1408]{1,0:T(8,128)(2,1)} %bitcast_select_fusion.15), channel_id=1, source_target_pairs={{0,16},{2,18},{4,20},{6,22},{8,24},{10,26},{12,28},{14,30},{16,0},... | collective-permute-start | bytes 743432 | tf_op jit(solution)/shard_map/ppermute | solution.py:222
  134.1 55.5 %collective-permute-start.16 = (bf16[2,88,1408]{2,1,0:T(8,128)(2,1)}, bf16[2,88,1408]{2,1,0:T(8,128)(2,1)}, u32[]{:S(2)}, u32[]{:S(2)}) collective-permute-start(bf16[2,88,1408]{2,1,0:T(8,128)(2,1)} %fusion.38), channel_id=1, source_target_pairs={{0,8},{2,10},{4,12},{6,14},{8,0},{10,2},{12,4},{14,6},{16,24},{18,... | collective-permute-start | bytes 1486856 | tf_op jit(solution)/shard_map/ppermute | solution.py:222
  135.3 8.6 %copy-start.46 = (s32[80]{0:T(128)}, s32[80]{0:T(128)S(1)}, u32[]{:S(2)}) copy-start(s32[80]{0:T(128)S(1)} %convert_reduce_fusion) | copy-start | bytes 964
  151.3 9.0 %copy-start.10 = (bf16[2,5,16,44,88]{4,3,2,1,0:T(8,128)(2,1)}, bf16[2,5,16,44,88]{4,3,2,1,0:T(8,128)(2,1)S(1)}, u32[]{:S(2)}) copy-start(bf16[2,5,16,44,88]{4,3,2,1,0:T(8,128)(2,1)S(1)} %slice.99) | copy-start | bytes 3717124
  153.3 2.9 slice-start
  167.8 5.1 %copy-start.11 = (bf16[4,88,2816]{2,1,0:T(8,128)(2,1)S(1)}, bf16[4,88,2816]{2,1,0:T(8,128)(2,1)}, u32[]{:S(2)}) copy-start(bf16[4,88,2816]{2,1,0:T(8,128)(2,1)} %get-tuple-element.74) | copy-start | bytes 5947396
  179.8 52.5 %collective-permute-start.12 = (bf16[2,2,88,2816]{3,2,1,0:T(8,128)(2,1)}, bf16[2,2,88,2816]{3,2,1,0:T(8,128)(2,1)}, u32[]{:S(2)}, u32[]{:S(2)}) collective-permute-start(bf16[2,2,88,2816]{3,2,1,0:T(8,128)(2,1)} %pad_maximum_fusion), channel_id=1, source_target_pairs={{0,4},{2,6},{4,0},{6,2},{8,12},{10,14},{12,8},{14,10},{16,20},{18,... | collective-permute-start | bytes 5947400 | tf_op jit(solution)/shard_map/ppermute | solution.py:222
  180.2 54.3 %collective-permute-start.7 = (bf16[4,88,2112]{2,1,0:T(8,128)(2,1)}, bf16[4,88,2112]{2,1,0:T(8,128)(2,1)}, u32[]{:S(2)}, u32[]{:S(2)}) collective-permute-start(bf16[4,88,2112]{2,1,0:T(8,128)(2,1)} %get-tuple-element.39), channel_id=1, source_target_pairs={{0,2},{2,0},{4,6},{6,4},{8,10},{10,8},{12,14},{14,12},{16,18},{18,... | collective-permute-start | bytes 4460552 | tf_op jit(solution)/shard_map/ppermute | solution.py:222
  184.8 2.4 copy-start.31
  184.8 3.2 copy-start.36
  187.2 12.2 %copy-start.2 = (bf16[2,5,16,16,768]{4,3,2,1,0:T(8,128)(2,1)}, bf16[2,5,16,16,768]{4,3,2,1,0:T(8,128)(2,1)S(1)}, u32[]{:S(2)}) copy-start(bf16[2,5,16,16,768]{4,3,2,1,0:T(8,128)(2,1)S(1)} %convolution_bitcast_fusion.3.refs_4_) | copy-start | bytes 11796484
  187.9 1.6 collective-permute-start.15
  188.0 2.4 copy-start.38
  191.7 7.6 %copy-start.32 = (bf16[2,88,1408]{2,1,0:T(8,128)(2,1)}, bf16[2,88,1408]{2,1,0:T(8,128)(2,1)S(1)}, u32[]{:S(2)}) copy-start(bf16[2,88,1408]{2,1,0:T(8,128)(2,1)S(1)} %fusion.35) | copy-start | bytes 1486852
  191.7 1.6 collective-permute-start.17
  194.1 21.1 %collective-permute-start.18 = (bf16[88,1408]{1,0:T(8,128)(2,1)}, bf16[88,1408]{1,0:T(8,128)(2,1)}, u32[]{:S(2)}, u32[]{:S(2)}) collective-permute-start(bf16[88,1408]{1,0:T(8,128)(2,1)} %bitcast_select_fusion.13), channel_id=1, source_target_pairs={{0,16},{2,18},{4,20},{6,22},{8,24},{10,26},{12,28},{14,30},{16,0},... | collective-permute-start | bytes 743432 | tf_op jit(solution)/shard_map/ppermute | solution.py:222
  216.8 2.7 collective-permute-start.19
  217.1 3.0 copy-start.3
  220.8 11.5 %copy-start.17 = (bf16[1,2,88,2816]{3,2,1,0:T(8,128)(2,1)S(1)}, bf16[1,2,88,2816]{3,2,1,0:T(8,128)(2,1)}, u32[]{:S(2)}) copy-start(bf16[1,2,88,2816]{3,2,1,0:T(8,128)(2,1)} %maximum_bitcast_fusion.1) | copy-start | bytes 2973700
  220.8 11.5 %copy-start.18 = (bf16[1,2,88,2816]{3,2,1,0:T(8,128)(2,1)S(1)}, bf16[1,2,88,2816]{3,2,1,0:T(8,128)(2,1)}, u32[]{:S(2)}) copy-start(bf16[1,2,88,2816]{3,2,1,0:T(8,128)(2,1)} %maximum_bitcast_fusion) | copy-start | bytes 2973700
  234.0 24.2 %collective-permute-start.21 = (bf16[2,88,2816]{2,1,0:T(8,128)(2,1)S(1)}, bf16[2,88,2816]{2,1,0:T(8,128)(2,1)S(1)}, u32[]{:S(2)}, u32[]{:S(2)}) collective-permute-start(bf16[2,88,2816]{2,1,0:T(8,128)(2,1)S(1)} %fusion.17), channel_id=1, source_target_pairs={{0,8},{2,10},{4,12},{6,14},{8,0},{10,2},{12,4},{14,6},{16,24},{18,... | collective-permute-start | bytes 2973704 | tf_op jit(solution)/shard_map/ppermute | solution.py:222
  239.6 52.3 %collective-permute-start.20 = (bf16[2,2,88,2112]{3,2,1,0:T(8,128)(2,1)}, bf16[2,2,88,2112]{3,2,1,0:T(8,128)(2,1)}, u32[]{:S(2)}, u32[]{:S(2)}) collective-permute-start(bf16[2,2,88,2112]{3,2,1,0:T(8,128)(2,1)} %pad_maximum_fusion.1), channel_id=1, source_target_pairs={{0,4},{2,6},{4,0},{6,2},{8,12},{10,14},{12,8},{14,10},{16,20},{18,... | collective-permute-start | bytes 4460552 | tf_op jit(solution)/shard_map/ppermute | solution.py:222
  260.0 2.2 collective-permute-start.22
  262.2 31.4 %collective-permute-start.24 = (bf16[88,2816]{1,0:T(8,128)(2,1)S(1)}, bf16[88,2816]{1,0:T(8,128)(2,1)}, u32[]{:S(2)}, u32[]{:S(2)}) collective-permute-start(bf16[88,2816]{1,0:T(8,128)(2,1)S(1)} %bitcast_select_fusion.9), channel_id=1, source_target_pairs={{0,16},{2,18},{4,20},{6,22},{8,24},{10,26},{12,28},{14,30},{16,0},... | collective-permute-start | bytes 1486856 | tf_op jit(solution)/shard_map/ppermute | solution.py:222
  289.0 3.0 copy-start.22
  289.0 3.0 copy-start.23
  294.3 2.9 collective-permute-start.25
  295.8 23.6 %collective-permute-start.23 = (bf16[2,88,2112]{2,1,0:T(8,128)(2,1)S(1)}, bf16[2,88,2112]{2,1,0:T(8,128)(2,1)S(1)}, u32[]{:S(2)}, u32[]{:S(2)}) collective-permute-start(bf16[2,88,2112]{2,1,0:T(8,128)(2,1)S(1)} %fusion.20), channel_id=1, source_target_pairs={{0,8},{2,10},{4,12},{6,14},{8,0},{10,2},{12,4},{14,6},{16,24},{18,... | collective-permute-start | bytes 2230280 | tf_op jit(solution)/shard_map/ppermute | solution.py:222
  321.0 1.8 collective-permute-start.26
  322.8 23.6 %collective-permute-start.27 = (bf16[88,2112]{1,0:T(8,128)(2,1)S(1)}, bf16[88,2112]{1,0:T(8,128)(2,1)S(1)}, u32[]{:S(2)}, u32[]{:S(2)}) collective-permute-start(bf16[88,2112]{1,0:T(8,128)(2,1)S(1)} %bitcast_select_fusion.10), channel_id=1, source_target_pairs={{0,16},{2,18},{4,20},{6,22},{8,24},{10,26},{12,28},{14,30},{16,0},... | collective-permute-start | bytes 1115144 | tf_op jit(solution)/shard_map/ppermute | solution.py:222
  325.7 21.6 %copy-start.47 = (s32[80]{0:T(128)S(1)}, s32[80]{0:T(128)}, u32[]{:S(2)}) copy-start(s32[80]{0:T(128)} %copy-done.46) | copy-start | bytes 964
  347.2 1.8 collective-permute-start.28
  384.5 7.3 %copy-start.42 = (s32[5]{0:T(128)S(1)}, s32[5]{0:T(128)}, u32[]{:S(2)}) copy-start(s32[5]{0:T(128)} %copy-done.41) | copy-start | bytes 64
  386.9 36.9 %all-to-all-start.1 = ((f32[16,40,484]{2,1,0:T(8,128)}), f32[16,40,484]{2,1,0:T(8,128)S(1)}, u32[]{:S(2)}, u32[]{:S(2)}) async-start(f32[16,40,484]{2,1,0:T(8,128)} %reshape.578), calls=%async_computation.1 | async-start | bytes 2621440 | tf_op jit(solution)/shard_map/all_to_all | solution.py:447
  424.0 2.8 copy-start.1
  (17 other events, 28.1 us)

commit v3 on v2

--- a/solution.py
+++ b/solution.py
@@ -297,6 +297,8 @@
     chunks = b_chunks(block)
     local = slabs[0, :, 0]
     path = SlabPath(owner, k_irrep, me, core)
+    labels = jnp.pad(jnp.concatenate([pair_i, pair_j]), (0, LANE - 2 * local_pairs))
+    labels = lax.all_to_all(jnp.broadcast_to(labels, (chips, 1, LANE)), "pair", 0, 0, tiled=True)
     kept_x, sent_x = zip(
         *[path.split_cores(local[:, :, first * block : (first + size) * block]) for first, size in chunks]
     )
@@ -332,22 +334,17 @@
     wanted = jnp.stack([target >> 1] + [(target >> 1) ^ (target & 1) ^ k_irrep[w] for w in range(windows)], 1)
     index = wanted[:, :, None] ^ pair_sym[None, None, :]
     kinds = 1 + windows
-    labels = jnp.concatenate([pair_i, pair_j]).astype(bf16)
-    labels = jnp.pad(labels, (0, share - labels.shape[0]))[None]
-    stored = jnp.concatenate([mine.reshape(local_pairs * betas, share), labels], 0)
+    stored = mine.reshape(local_pairs * betas, share)
     index = index + betas * jnp.arange(local_pairs, dtype=jnp.int32)
-    index = index.reshape(chips, kinds * local_pairs)
-    index = jnp.pad(index, ((0, 0), (0, 1)), constant_values=local_pairs * betas).reshape(-1)
+    index = jnp.pad(index.reshape(chips, -1), ((0, 0), (0, 1)), constant_values=-1).reshape(-1)
     chosen = (index[:, None] == jnp.arange(stored.shape[0], dtype=jnp.int32)[None, :]).astype(bf16)
     sent = jnp.einsum("rh,hx->rx", chosen, stored)
     sent = sent.reshape(chips, kinds * local_pairs + 1, share)
     came = lax.all_to_all(sent, "pair", 0, 0, tiled=True)
-    came = after(came, sent_z[0], leaving_x[2])
-    came = came.reshape(chips * (kinds * local_pairs + 1), share)
-    label_rows = after(target, leaving_x[1]) * (kinds * local_pairs + 1) + kinds * local_pairs
-    both = came[label_rows][:, : 2 * local_pairs].astype(jnp.int32).reshape(chips, 2, local_pairs)
-    both = both.transpose(1, 0, 2).reshape(2, pairs)
-
+
+    labels = after(labels, sent)
+    both = labels[:, 0, : 2 * local_pairs]
+    both = both.reshape(chips, 2, local_pairs).transpose(1, 0, 2).reshape(2, pairs)
     numbers = jnp.arange(pairs, dtype=jnp.int32)
     ahead = both[0][None, :] < both[0][:, None]
     tied = (both[0][None, :] == both[0][:, None]) & (numbers[None, :] < numbers[:, None])
@@ -357,22 +354,7 @@
     first = jnp.sum(placed * both[0][None, :], axis=1)
     second = jnp.sum(placed * both[1][None, :], axis=1)
 
-    source = (order // local_pairs) * (kinds * local_pairs + 1) + order % local_pairs
-    source = source[None, :] + local_pairs * jnp.arange(kinds, dtype=jnp.int32)[:, None]
-    amps = came[source]
-    amps = amps.reshape(kinds, groups, GROUP, rows, block)
-    holes = amps[1:]
     used = GROUP * rows
-    at = amps[0].transpose(0, 3, 1, 2).reshape(groups, block, used)
-    at = jnp.pad(at, ((0, 0), (0, LANE - block), (0, lanes - used)))
-    lane = jnp.arange(lanes, dtype=jnp.int32)
-    spread = ((lane[None, :] % rows == jnp.arange(rows)[:, None]) & (lane < used)[None, :]).astype(bf16)
-    lane_pair = lane // rows
-    mask = jnp.stack([
-        (jnp.repeat(start + jnp.arange(depth), GROUP)[:, None] == lane_pair[None, n * TILE : (n + 1) * TILE])
-        for n, start in enumerate(starts)
-    ]).astype(bf16)
-
     coupled = jnp.where(gamma == core, couplings, swap_cores(couplings))
     chosen = (second.reshape(groups, GROUP)[:, :, None] == jnp.arange(occ_irrep.shape[0])).astype(bf16)
     coupled = jnp.einsum("gql,wljc->wgqjc", chosen, coupled)
@@ -390,6 +372,23 @@
     lrow = energy_a[None] - (base[None] + occ_energy[window_k][:, None])[:, :, None]
     lrow = lrow.reshape(windows, groups, 1, used)
     lrow = jnp.pad(lrow, ((0, 0), (0, 0), (0, 0), (0, lanes - used)), constant_values=1.0)
+    source = (order // local_pairs) * (kinds * local_pairs + 1) + order % local_pairs
+    source = source[None, :] + local_pairs * jnp.arange(kinds, dtype=jnp.int32)[:, None]
+    came = after(came, sent_z[0], leaving_x[2], ct, lrow, source)
+    came = came.reshape(chips * (kinds * local_pairs + 1), share)
+    amps = came[source]
+    amps = amps.reshape(kinds, groups, GROUP, rows, block)
+    holes = lax.optimization_barrier(amps[1:].transpose(0, 1, 4, 2, 3))
+    at = amps[0].transpose(0, 3, 1, 2).reshape(groups, block, used)
+    at = jnp.pad(at, ((0, 0), (0, LANE - block), (0, lanes - used)))
+    lane = jnp.arange(lanes, dtype=jnp.int32)
+    spread = ((lane[None, :] % rows == jnp.arange(rows)[:, None]) & (lane < used)[None, :]).astype(bf16)
+    lane_pair = lane // rows
+    mask = jnp.stack([
+        (jnp.repeat(start + jnp.arange(depth), GROUP)[:, None] == lane_pair[None, n * TILE : (n + 1) * TILE])
+        for n, start in enumerate(starts)
+    ]).astype(bf16)
+
     ecol = jnp.broadcast_to(pick(vir_energy, gamma)[:, None], (block, TILE))
     energy_b = vir_energy[m ^ gamma ^ k_irrep]
 
@@ -397,8 +396,8 @@
 
     def spread_holes(chunk, *tokens):
         start, size = chunks[chunk]
-        hole = after(holes[:, :, :, :, start : start + size], *tokens)
-        return jnp.einsum("wgqab,ae->wgbqe", hole, spread)
+        hole = after(holes, *tokens)[:, :, start : start + size]
+        return jnp.einsum("wgbqa,ae->wgbqe", hole, spread)
 
     def run(chunk, w, v, total):
         start, size = chunks[chunk]
@@ -457,7 +456,7 @@
     fits = lax.axis_size("vtile") == 1 and cores == 2 and betas == 8 and chips == betas * cores
     fits = fits and args[8].shape[0] == 2 and block % 2 == 0 and block < LANE
     fits = fits and all(size > 0 and size % 2 == 0 for _, size in b_chunks(block))
-    if fits and args[5].shape[0] <= 256:
+    if fits and 2 * args[6].shape[0] <= LANE:
         return on_device_scatter(*args)
     return on_device_gather(*args)
 

time: 432 us -> 411 us (0.951)
  local copies, waits for them, and re-layouts: 86 us -> 68.1 us
  starting transfers between devices: 34.8 us -> 46.2 us
  other arithmetic: 55 us -> 45 us
    optimization_barrier x4 -> x0, local copies, waits for them, and re-layouts: 13.8 us -> none  [after(): return lax.optimization_barrier((x,) + others)[0]]
    all_to_all x0 -> x1, starting transfers between devices: none -> 7.17 us  [on_device_scatter(): lax.all_to_all(jnp.broadcast_to(labels, (chips, 1, LANE)), 'pair', 0, 0,...]
    slice x5, local copies, waits for them, and re-layouts: 16.2 us -> 9.87 us  [the longest x4 9.79 us: on_device_scatter(): holes = lax.optimization_barrier(amps[1:].transpose(0, 1, 4, 2, 3))]
    ppermute x16, starting transfers between devices: 19.5 us -> 25.4 us  [across(): return lax.ppermute(x, 'pair', [(t, t ^ bit) for t in range(count)])]
    unnamed x99 -> x83, local copies, waits for them, and re-layouts: 9.36 us -> 4.24 us
    dot_general x4, matrix products: 14.3 us -> 9.3 us  [spread_holes(): return jnp.einsum('wgbqa,ae->wgbqe', hole, spread)]
    ppermute x16, waiting for transfers between devices: 68.5 us -> 64.1 us  [across(): return lax.ppermute(x, 'pair', [(t, t ^ bit) for t in range(count)])]
  transfers between devices with their start and end apart: 31 -> 32, of which waited for: 12 -> 15; matrix products, arithmetic and copies ran while one was open for 32% -> 26% of each run, Pallas kernels for 20% -> 22%
where the time goes in v3:
time: 411 us; the launch traced here: 405 us
  Pallas kernels  121 us (29%)
  waiting for transfers between devices  105 us (26%)
  local copies, waits for them, and re-layouts  68.1 us (17%)
  starting transfers between devices  46.2 us (11%)
  other arithmetic  45 us (11%)
  matrix products  16.9 us (4%)
    pallas_call x8, Pallas kernels, triples_call(): pl.pallas_call(functools.partial(triples_kernel, last), grid=(groups,), i...  121 us
    ppermute x16, waiting for transfers between devices, across(): return lax.ppermute(x, 'pair', [(t, t ^ bit) for t in range(count)])  64.1 us
    all_to_all x1, waiting for transfers between devices, on_device_scatter(): came = lax.all_to_all(total, 'pair', 0, 0, tiled=True)  31.4 us
    ppermute x16, starting transfers between devices, across(): return lax.ppermute(x, 'pair', [(t, t ^ bit) for t in range(count)])  25.4 us
    select_n x4, other arithmetic, split_cores(): return (jnp.where(same, mine, theirs), jnp.where(same, theirs, mine))  13.1 us
    select_n x4, other arithmetic, block(): return jnp.where(self.from_here(0)[w], pick(kept, beta), pick(came, beta))  10.6 us
    slice x4, local copies, waits for them, and re-layouts, on_device_scatter(): holes = lax.optimization_barrier(amps[1:].transpose(0, 1, 4, 2, 3))  9.79 us
    dot_general x4, matrix products, spread_holes(): return jnp.einsum('wgbqa,ae->wgbqe', hole, spread)  9.3 us
  transfers between devices with their start and end apart: 32, of which 15 were waited for; matrix products, arithmetic and copies ran while one was open for 26% of the time, Pallas kernels for 22%

profile of v3, /device:TPU:12, one launch (start us, length us, event | category | flops | bytes accessed | tf_op | source)
XLA Modules:
  0.0 405.0 jit_solution(4071373377976193197)
XLA Ops:
  0.0 3.8 fusion.95
  3.8 3.0 dynamic-slice_bitcast_fusion.2
  7.4 7.2 %all-to-all-start = ((s32[16,1,128]{2,1,0:T(1,128)}), s32[16,1,128]{2,1,0:T(1,128)S(1)}, u32[]{:S(2)}, u32[]{:S(2)}) async-start(s32[16,1,128]{2,1,0:T(1,128)} %broadcast_in_dim.145), calls=%async_computation | async-start | bytes 16384 | tf_op jit(solution)/shard_map/all_to_all | solution.py:301
  16.2 2.4 slice.254
  18.5 1.6 dynamic-slice_bitcast_fusion
  21.1 2.1 slice.253
  23.3 1.6 copy-done.9
  38.3 1.5 fusion.41
  39.8 2.7 bitcast_select_fusion.4
  42.5 2.0 fusion.43
  50.4 1.5 collective-permute-start.4
  51.9 6.6 %all-to-all-start.1 = ((bf16[16,16,3872]{2,1,0:T(8,128)(2,1)}), bf16[16,16,3872]{2,1,0:T(8,128)(2,1)S(1)}, u32[]{:S(2)}, u32[]{:S(2)}) async-start(bf16[16,16,3872]{2,1,0:T(8,128)(2,1)} %fusion.43), calls=%async_computation.1 | async-start | bytes 4063232 | tf_op jit(solution)/shard_map/all_to_all | solution.py:343
  58.7 1.6 convolution_bitcast_fusion
  61.6 2.0 fusion.8
  64.6 2.8 bitcast_select_fusion.6
  70.7 3.9 bitcast_select_fusion.3
  74.6 9.6 %collective-permute-done.4 = bf16[4,88,1408]{2,1,0:T(8,128)(2,1)} collective-permute-done((bf16[4,88,1408]{2,1,0:T(8,128)(2,1)}, bf16[4,88,1408]{2,1,0:T(8,128)(2,1)}, u32[]{:S(2)}, u32[]{:S(2)}) %collective-permute-start.4) | collective-permute-done | bytes 991264 | tf_op jit(solution)/shard_map/ppermute | solution.py:222
  84.2 3.0 collective-permute-start.5
  87.2 3.3 dynamic-slice_select_fusion.17
  91.0 26.5 %collective-permute-done.5 = bf16[4,88,1408]{2,1,0:T(8,128)(2,1)S(1)} collective-permute-done((bf16[4,88,1408]{2,1,0:T(8,128)(2,1)S(1)}, bf16[4,88,1408]{2,1,0:T(8,128)(2,1)S(1)}, u32[]{:S(2)}, u32[]{:S(2)}) %collective-permute-start.5) | collective-permute-done | bytes 991264 | tf_op jit(solution)/shard_map/ppermute | solution.py:222
  117.5 1.6 dynamic-slice_select_fusion.23
  121.3 3.7 bitcast_select_fusion
  125.6 1.5 collective-permute-start.6
  127.1 4.9 %collective-permute-done.10 = bf16[2,88,1408]{2,1,0:T(8,128)(2,1)S(1)} collective-permute-done((bf16[2,88,1408]{2,1,0:T(8,128)(2,1)S(1)}, bf16[2,88,1408]{2,1,0:T(8,128)(2,1)S(1)}, u32[]{:S(2)}, u32[]{:S(2)}) %collective-permute-start.10) | collective-permute-done | bytes 495648 | tf_op jit(solution)/shard_map/ppermute | solution.py:222
  134.7 2.4 collective-permute-start.13
  137.1 10.9 %collective-permute-done.8 = bf16[2,2,88,1408]{3,2,1,0:T(8,128)(2,1)S(1)} collective-permute-done((bf16[2,2,88,1408]{3,2,1,0:T(8,128)(2,1)S(1)}, bf16[2,2,88,1408]{3,2,1,0:T(8,128)(2,1)S(1)}, u32[]{:S(2)}, u32[]{:S(2)}) %collective-permute-start.8) | collective-permute-done | bytes 991264 | tf_op jit(solution)/shard_map/ppermute | solution.py:222
  149.8 3.0 gather_fusion.10
  153.8 2.8 squeeze.289
  156.6 2.4 reshape.585
  159.0 2.2 copy.62
  161.2 4.5 %slice.99 = bf16[2,5,16,44,88]{4,3,2,1,0:T(8,128)(2,1)} reshape(bf16[160,3872]{1,0:T(8,128)(2,1)S(1)} %slice-done.1) | data formatting | bytes 2478080 | tf_op jit(solution)/shard_map/slice | solution.py:381
  165.6 5.3 %copy.61 = bf16[2,5,16,44,88]{3,2,4,1,0:T(8,128)(2,1)} copy(bf16[2,5,16,44,88]{4,3,2,1,0:T(8,128)(2,1)} %slice.99) | data formatting | bytes 2478080 | tf_op jit(solution)/shard_map/slice | solution.py:381
  172.2 4.0 dynamic-slice_select_fusion.3
  176.4 1.4 pad_maximum_fusion
  181.8 1.4 collective-permute-done.15
  186.3 3.4 collective-permute-start.18
  190.2 11.5 %triples.8.refs_9_ = f32[5,88,768]{2,1,0:T(8,128)S(1)} custom-call(f32[1,16]{1,0:T(1,128)S(1)} %get-tuple-element.138.refs_0_, bf16[2,16,88,128]{3,2,1,0:T(8,128)(2,1)S(1)} %bitcast.265, bf16[2,88,1408]{2,1,0:T(8,128)(2,1)S(1)} %pad_maximum_fusion.7.refs_2_, bf16[5,128,768]{2,1,0:T(8,128)(2,1)S(1)} %pad.19.refs_3_, ...), custom_call_target="tpu_custom_call" | custom-call | flops 14879293440 | bytes 5148672 | tf_op jit(solution)/shard_map/triples/pallas_call | solution.py:197
  204.4 11.5 %triples.9.refs_9_ = f32[5,88,768]{2,1,0:T(8,128)S(1)} custom-call(f32[1,16]{1,0:T(1,128)S(1)} %get-tuple-element.139.refs_0_, bf16[2,16,88,128]{3,2,1,0:T(8,128)(2,1)S(1)} %bitcast.266, bf16[2,88,1408]{2,1,0:T(8,128)(2,1)S(1)} %pad_maximum_fusion.7.refs_2_, bf16[5,128,768]{2,1,0:T(8,128)(2,1)S(1)} %pad.19.refs_3_, ...), custom_call_target="tpu_custom_call" | custom-call | flops 14879293440 | bytes 5148672 | tf_op jit(solution)/shard_map/triples/pallas_call | solution.py:197
  215.9 5.3 %collective-permute-done.12 = bf16[2,2,88,2816]{3,2,1,0:T(8,128)(2,1)S(1)} collective-permute-done((bf16[2,2,88,2816]{3,2,1,0:T(8,128)(2,1)}, bf16[2,2,88,2816]{3,2,1,0:T(8,128)(2,1)S(1)}, u32[]{:S(2)}, u32[]{:S(2)}) %collective-permute-start.12) | collective-permute-done | bytes 1982496 | tf_op jit(solution)/shard_map/ppermute | solution.py:222
  221.2 1.4 fusion.17
  222.6 1.5 collective-permute-start.21
  224.0 1.7 dynamic-slice_select_fusion.11
  227.9 11.5 %triples.10.refs_9_ = f32[5,88,768]{2,1,0:T(8,128)S(1)} custom-call(f32[1,16]{1,0:T(1,128)S(1)} %get-tuple-element.136.refs_0_, bf16[2,16,88,128]{3,2,1,0:T(8,128)(2,1)S(1)} %bitcast.263, bf16[2,88,1408]{2,1,0:T(8,128)(2,1)S(1)} %pad_maximum_fusion.8.refs_2_, bf16[5,128,768]{2,1,0:T(8,128)(2,1)S(1)} %pad.19.refs_3_, ...), custom_call_target="tpu_custom_call" | custom-call | flops 14879293440 | bytes 5148672 | tf_op jit(solution)/shard_map/triples/pallas_call | solution.py:197
  239.4 4.5 %collective-permute-done.21 = bf16[2,88,2816]{2,1,0:T(8,128)(2,1)} collective-permute-done((bf16[2,88,2816]{2,1,0:T(8,128)(2,1)}, bf16[2,88,2816]{2,1,0:T(8,128)(2,1)}, u32[]{:S(2)}, u32[]{:S(2)}) %collective-permute-start.21) | collective-permute-done | bytes 991264 | tf_op jit(solution)/shard_map/ppermute | solution.py:222
  244.0 1.6 fusion.14
  245.9 1.7 collective-permute-done.22
  247.7 2.4 collective-permute-start.24
  250.1 11.7 %triples.11.refs_9_ = f32[5,88,768]{2,1,0:T(8,128)S(1)} custom-call(f32[1,16]{1,0:T(1,128)S(1)} %get-tuple-element.137.refs_0_, bf16[2,16,88,128]{3,2,1,0:T(8,128)(2,1)S(1)} %bitcast.264, bf16[2,88,1408]{2,1,0:T(8,128)(2,1)S(1)} %pad_maximum_fusion.8.refs_2_, bf16[5,128,768]{2,1,0:T(8,128)(2,1)S(1)} %pad.19.refs_3_, ...), custom_call_target="tpu_custom_call" | custom-call | flops 14879293440 | bytes 5148672 | tf_op jit(solution)/shard_map/triples/pallas_call | solution.py:197
  261.8 5.3 %fusion.72.refs_4_ = bf16[2,5,32,16,768]{4,3,2,1,0:T(8,128)(2,1)} fusion(bf16[2,5,88,16,44]{4,3,2,1,0:T(8,128)(2,1)S(1)} %bitcast.272, s32[768]{0:T(1024)S(1)} %get-tuple-element.150, pred[768]{0:T(1024)(128)(4,1)S(1)} %copy-done.29), kind=kOutput, calls=%fused_computation.197 | convolution fusion | flops 346097664 | bytes 9107200 | tf_op jit(solution)/shard_map/wgbqa,ae->wgbqe/dot_general | solution.py:400
  267.1 1.7 fusion.70.refs_4_
  269.2 2.4 collective-permute-done.24
  272.4 2.5 collective-permute-start.23
  275.7 20.7 %triples.12.refs_9_ = f32[5,88,768]{2,1,0:T(8,128)S(1)} custom-call(f32[1,32]{1,0:T(1,128)S(1)} %get-tuple-element.135.refs_0_, bf16[2,32,88,128]{3,2,1,0:T(8,128)(2,1)S(1)} %bitcast.259, bf16[2,88,2816]{2,1,0:T(8,128)(2,1)S(1)} %pad_maximum_fusion.4.refs_2_, bf16[5,128,768]{2,1,0:T(8,128)(2,1)S(1)} %pad.19.refs_3_, ...), custom_call_target="tpu_custom_call" | custom-call | flops 29758586880 | bytes 10297344 | tf_op jit(solution)/shard_map/triples/pallas_call | solution.py:197
  297.1 1.6 collective-permute-done.26
  298.7 2.7 collective-permute-start.27
  301.4 20.7 %triples.13.refs_9_ = f32[5,88,768]{2,1,0:T(8,128)S(1)} custom-call(f32[1,32]{1,0:T(1,128)S(1)} %get-tuple-element.134.refs_0_, bf16[2,32,88,128]{3,2,1,0:T(8,128)(2,1)S(1)} %bitcast.260, bf16[2,88,2816]{2,1,0:T(8,128)(2,1)S(1)} %pad_maximum_fusion.4.refs_2_, bf16[5,128,768]{2,1,0:T(8,128)(2,1)S(1)} %pad.19.refs_3_, ...), custom_call_target="tpu_custom_call" | custom-call | flops 29758586880 | bytes 10297344 | tf_op jit(solution)/shard_map/triples/pallas_call | solution.py:197
  322.9 1.6 collective-permute-done.28
  325.2 15.9 %triples.14.refs_9_ = f32[5,88,768]{2,1,0:T(8,128)S(1)} custom-call(f32[1,24]{1,0:T(1,128)S(1)} %get-tuple-element.132.refs_0_, bf16[2,24,88,128]{3,2,1,0:T(8,128)(2,1)S(1)} %bitcast.261, bf16[2,88,2112]{2,1,0:T(8,128)(2,1)S(1)} %pad_maximum_fusion.5.refs_2_, bf16[5,128,768]{2,1,0:T(8,128)(2,1)S(1)} %pad.19.refs_3_, ...), custom_call_target="tpu_custom_call" | custom-call | flops 22318940160 | bytes 7723008 | tf_op jit(solution)/shard_map/triples/pallas_call | solution.py:197
  341.2 17.2 %triples.15 = f32[5,768,88]{2,1,0:T(8,128)S(1)} custom-call(f32[1,24]{1,0:T(1,128)S(1)} %get-tuple-element.133.refs_0_, bf16[2,24,88,128]{3,2,1,0:T(8,128)(2,1)S(1)} %bitcast.262, bf16[2,88,2112]{2,1,0:T(8,128)(2,1)S(1)} %pad_maximum_fusion.5.refs_2_, bf16[5,128,768]{2,1,0:T(8,128)(2,1)S(1)} %pad.19.refs_3_, ...), custom_call_target="tpu_custom_call" | custom-call | flops 22318940160 | bytes 7723008 | tf_op jit(solution)/shard_map/triples/pallas_call | solution.py:197
  359.7 1.9 reshape.590
  362.7 2.4 reshape.591
  365.1 5.1 %all-to-all-start.2 = ((f32[16,40,484]{2,1,0:T(8,128)}), f32[16,40,484]{2,1,0:T(8,128)S(1)}, u32[]{:S(2)}, u32[]{:S(2)}) async-start(f32[16,40,484]{2,1,0:T(8,128)} %reshape.591), calls=%async_computation.2 | async-start | bytes 2621440 | tf_op jit(solution)/shard_map/all_to_all | solution.py:446
  370.4 31.4 %all-to-all-done.2 = f32[16,40,484]{2,1,0:T(8,128)S(1)} async-done(((f32[16,40,484]{2,1,0:T(8,128)}), f32[16,40,484]{2,1,0:T(8,128)S(1)}, u32[]{:S(2)}, u32[]{:S(2)}) %all-to-all-start.2) | async-done | bytes 1239072 | tf_op jit(solution)/shard_map/all_to_all | solution.py:446
  402.4 2.4 gather_fusion.12
  (284 shorter events, 56.0 us)
Async XLA Ops:
  0.0 42.5 %copy-start = (bf16[5,8,7744]{2,1,0:T(8,128)(2,1)S(1)}, bf16[5,8,7744]{2,1,0:T(8,128)(2,1)}, u32[]{:S(2)}) copy-start(bf16[5,8,7744]{2,1,0:T(8,128)(2,1)} %param.10) | copy-start | bytes 1858564
  3.8 11.9 %copy-start.12 = (bf16[8,88,1408]{2,1,0:T(8,128)(2,1)}, bf16[8,88,1408]{2,1,0:T(8,128)(2,1)S(1)}, u32[]{:S(2)}) copy-start(bf16[8,88,1408]{2,1,0:T(8,128)(2,1)S(1)} %get-tuple-element.73) | copy-start | bytes 5947396
  3.8 3.0 copy-start.36
  3.8 3.0 copy-start.37
  6.7 33.0 %collective-permute-start.3 = (bf16[4,88,1408]{2,1,0:T(8,128)(2,1)}, bf16[4,88,1408]{2,1,0:T(8,128)(2,1)}, u32[]{:S(2)}, u32[]{:S(2)}) collective-permute-start(bf16[4,88,1408]{2,1,0:T(8,128)(2,1)} %dynamic-slice_bitcast_fusion.2), channel_id=1, source_target_pairs={{0,1},{1,0},{2,3},{3,2},{4,5},{5,4},{6,7},{7,6},{8,9},{9,8},{10,11... | collective-permute-start | bytes 2973704 | tf_op jit(solution)/shard_map/ppermute | solution.py:217
  7.4 37.1 %all-to-all-start = ((s32[16,1,128]{2,1,0:T(1,128)}), s32[16,1,128]{2,1,0:T(1,128)S(1)}, u32[]{:S(2)}, u32[]{:S(2)}) async-start(s32[16,1,128]{2,1,0:T(1,128)} %broadcast_in_dim.145), calls=%async_computation | async-start | bytes 16384 | tf_op jit(solution)/shard_map/all_to_all | solution.py:301
  14.6 23.7 %collective-permute-start.14 = (bf16[2,30,30,88]{3,0,2,1:T(2,128)(2,1)}, bf16[2,30,30,88]{3,0,2,1:T(2,128)(2,1)}, u32[]{:S(2)}, u32[]{:S(2)}) collective-permute-start(bf16[2,30,30,88]{3,0,2,1:T(2,128)(2,1)} %param.12), channel_id=1, source_target_pairs={{0,1},{1,0},{2,3},{3,2},{4,5},{5,4},{6,7},{7,6},{8,9},{9,8},{10,11... | collective-permute-start | bytes 950408 | tf_op jit(solution)/shard_map/ppermute | solution.py:217
  15.7 48.9 %collective-permute-start.2 = (bf16[4,88,1408]{2,1,0:T(8,128)(2,1)}, bf16[4,88,1408]{2,1,0:T(8,128)(2,1)}, u32[]{:S(2)}, u32[]{:S(2)}) collective-permute-start(bf16[4,88,1408]{2,1,0:T(8,128)(2,1)} %dynamic-slice_bitcast_fusion.3), channel_id=1, source_target_pairs={{0,1},{1,0},{2,3},{3,2},{4,5},{5,4},{6,7},{7,6},{8,9},{9,8},{10,11... | collective-permute-start | bytes 2973704 | tf_op jit(solution)/shard_map/ppermute | solution.py:217
  18.5 2.6 copy-start.5
  21.1 99.1 %collective-permute-start.1 = (bf16[4,88,2816]{2,1,0:T(8,128)(2,1)}, bf16[4,88,2816]{2,1,0:T(8,128)(2,1)}, u32[]{:S(2)}, u32[]{:S(2)}) collective-permute-start(bf16[4,88,2816]{2,1,0:T(8,128)(2,1)} %dynamic-slice_bitcast_fusion), channel_id=1, source_target_pairs={{0,1},{1,0},{2,3},{3,2},{4,5},{5,4},{6,7},{7,6},{8,9},{9,8},{10,11... | collective-permute-start | bytes 5947400 | tf_op jit(solution)/shard_map/ppermute | solution.py:217
  23.2 4.0 copy-start.40
  23.3 4.0 copy-start.2
  24.8 6.8 %copy-start.35 = (s32[2]{0:T(128)S(1)}, s32[2]{0:T(128)}, u32[]{:S(2)}) copy-start(s32[2]{0:T(128)} %param.19) | copy-start | bytes 28
  24.8 8.4 %copy-start.26 = (f32[8,88]{1,0:T(8,128)S(1)}, f32[8,88]{1,0:T(8,128)}, u32[]{:S(2)}) copy-start(f32[8,88]{1,0:T(8,128)} %param.14) | copy-start | bytes 8452
  24.8 10.1 %copy-start.3 = (f32[30]{0:T(128)S(1)}, f32[30]{0:T(128)}, u32[]{:S(2)}) copy-start(f32[30]{0:T(128)} %param.13) | copy-start | bytes 364
  26.1 44.6 %collective-permute-start = (bf16[4,88,2112]{2,1,0:T(8,128)(2,1)}, bf16[4,88,2112]{2,1,0:T(8,128)(2,1)}, u32[]{:S(2)}, u32[]{:S(2)}) collective-permute-start(bf16[4,88,2112]{2,1,0:T(8,128)(2,1)} %dynamic-slice_bitcast_fusion.1), channel_id=1, source_target_pairs={{0,1},{1,0},{2,3},{3,2},{4,5},{5,4},{6,7},{7,6},{8,9},{9,8},{10,11... | collective-permute-start | bytes 4460552 | tf_op jit(solution)/shard_map/ppermute | solution.py:217
  27.9 11.9 %copy-start.14 = (bf16[8,88,1408]{2,1,0:T(8,128)(2,1)S(1)}, bf16[8,88,1408]{2,1,0:T(8,128)(2,1)}, u32[]{:S(2)}) copy-start(bf16[8,88,1408]{2,1,0:T(8,128)(2,1)} %get-tuple-element.72) | copy-start | bytes 5947396
  37.4 5.2 %copy-start.27 = (f32[2,88]{1,0:T(2,128)}, f32[2,88]{1,0:T(2,128)S(1)}, u32[]{:S(2)}) copy-start(f32[2,88]{1,0:T(2,128)S(1)} %gather_fusion.1) | copy-start | bytes 2116
  45.0 6.9 %copy-start.38 = (s32[80]{0:T(128)}, s32[80]{0:T(128)S(1)}, u32[]{:S(2)}) copy-start(s32[80]{0:T(128)S(1)} %convert_reduce_fusion) | copy-start | bytes 964
  50.4 33.8 %collective-permute-start.4 = (bf16[4,88,1408]{2,1,0:T(8,128)(2,1)}, bf16[4,88,1408]{2,1,0:T(8,128)(2,1)}, u32[]{:S(2)}, u32[]{:S(2)}) collective-permute-start(bf16[4,88,1408]{2,1,0:T(8,128)(2,1)} %get-tuple-element.97), channel_id=1, source_target_pairs={{0,2},{2,0},{4,6},{6,4},{8,10},{10,8},{12,14},{14,12},{16,18},{18,... | collective-permute-start | bytes 2973704 | tf_op jit(solution)/shard_map/ppermute | solution.py:222
  51.9 97.9 %all-to-all-start.1 = ((bf16[16,16,3872]{2,1,0:T(8,128)(2,1)}), bf16[16,16,3872]{2,1,0:T(8,128)(2,1)S(1)}, u32[]{:S(2)}, u32[]{:S(2)}) async-start(bf16[16,16,3872]{2,1,0:T(8,128)(2,1)} %fusion.43), calls=%async_computation.1 | async-start | bytes 4063232 | tf_op jit(solution)/shard_map/all_to_all | solution.py:343
  61.6 3.0 copy-start.13
  64.6 3.1 copy-start.20
  70.7 13.6 %copy-start.23 = (bf16[4,88,1408]{2,1,0:T(8,128)(2,1)S(1)}, bf16[4,88,1408]{2,1,0:T(8,128)(2,1)}, u32[]{:S(2)}) copy-start(bf16[4,88,1408]{2,1,0:T(8,128)(2,1)} %get-tuple-element.37) | copy-start | bytes 2973700
  70.7 16.5 %copy-start.10 = (bf16[4,88,1408]{2,1,0:T(8,128)(2,1)S(1)}, bf16[4,88,1408]{2,1,0:T(8,128)(2,1)}, u32[]{:S(2)}) copy-start(bf16[4,88,1408]{2,1,0:T(8,128)(2,1)} %get-tuple-element.96) | copy-start | bytes 2973700
  84.2 33.2 %collective-permute-start.5 = (bf16[4,88,1408]{2,1,0:T(8,128)(2,1)S(1)}, bf16[4,88,1408]{2,1,0:T(8,128)(2,1)S(1)}, u32[]{:S(2)}, u32[]{:S(2)}) collective-permute-start(bf16[4,88,1408]{2,1,0:T(8,128)(2,1)S(1)} %copy-done.23), channel_id=1, source_target_pairs={{0,2},{2,0},{4,6},{6,4},{8,10},{10,8},{12,14},{14,12},{16,18},{18,... | collective-permute-start | bytes 2973704 | tf_op jit(solution)/shard_map/ppermute | solution.py:222
  90.6 26.8 %copy-start.11 = (bf16[4,88,1408]{2,1,0:T(8,128)(2,1)S(1)}, bf16[4,88,1408]{2,1,0:T(8,128)(2,1)}, u32[]{:S(2)}) copy-start(bf16[4,88,1408]{2,1,0:T(8,128)(2,1)} %get-tuple-element.94) | copy-start | bytes 2973700
  90.8 28.6 %collective-permute-start.9 = (bf16[2,2,88,1408]{3,2,1,0:T(8,128)(2,1)S(1)}, bf16[2,2,88,1408]{3,2,1,0:T(8,128)(2,1)S(1)}, u32[]{:S(2)}, u32[]{:S(2)}) collective-permute-start(bf16[2,2,88,1408]{3,2,1,0:T(8,128)(2,1)S(1)} %pad_maximum_fusion.2), channel_id=1, source_target_pairs={{0,4},{2,6},{4,0},{6,2},{8,12},{10,14},{12,8},{14,10},{16,20},{18,... | collective-permute-start | bytes 2973704 | tf_op jit(solution)/shard_map/ppermute | solution.py:222
  119.6 12.4 %copy-start.30 = (pred[2]{0:T(512)(128)(4,1)S(1)}, pred[2]{0:T(512)(128)(4,1)}, u32[]{:S(2)}) copy-start(pred[2]{0:T(512)(128)(4,1)} %get-tuple-element.141) | copy-start | bytes 10
  119.6 12.4 %collective-permute-start.10 = (bf16[2,88,1408]{2,1,0:T(8,128)(2,1)S(1)}, bf16[2,88,1408]{2,1,0:T(8,128)(2,1)S(1)}, u32[]{:S(2)}, u32[]{:S(2)}) collective-permute-start(bf16[2,88,1408]{2,1,0:T(8,128)(2,1)S(1)} %fusion.27), channel_id=1, source_target_pairs={{0,8},{2,10},{4,12},{6,14},{8,0},{10,2},{12,4},{14,6},{16,24},{18,... | collective-permute-start | bytes 1486856 | tf_op jit(solution)/shard_map/ppermute | solution.py:222
  125.1 23.0 %collective-permute-start.8 = (bf16[2,2,88,1408]{3,2,1,0:T(8,128)(2,1)S(1)}, bf16[2,2,88,1408]{3,2,1,0:T(8,128)(2,1)S(1)}, u32[]{:S(2)}, u32[]{:S(2)}) collective-permute-start(bf16[2,2,88,1408]{3,2,1,0:T(8,128)(2,1)S(1)} %pad_maximum_fusion.3), channel_id=1, source_target_pairs={{0,4},{2,6},{4,0},{6,2},{8,12},{10,14},{12,8},{14,10},{16,20},{18,... | collective-permute-start | bytes 2973704 | tf_op jit(solution)/shard_map/ppermute | solution.py:222
  125.6 46.5 %collective-permute-start.6 = (bf16[4,88,2816]{2,1,0:T(8,128)(2,1)}, bf16[4,88,2816]{2,1,0:T(8,128)(2,1)}, u32[]{:S(2)}, u32[]{:S(2)}) collective-permute-start(bf16[4,88,2816]{2,1,0:T(8,128)(2,1)} %get-tuple-element.38), channel_id=1, source_target_pairs={{0,2},{2,0},{4,6},{6,4},{8,10},{10,8},{12,14},{14,12},{16,18},{18,... | collective-permute-start | bytes 5947400 | tf_op jit(solution)/shard_map/ppermute | solution.py:222
  132.3 16.8 %copy-start.17 = (bf16[2,88,1408]{2,1,0:T(8,128)(2,1)}, bf16[2,88,1408]{2,1,0:T(8,128)(2,1)S(1)}, u32[]{:S(2)}) copy-start(bf16[2,88,1408]{2,1,0:T(8,128)(2,1)S(1)} %fusion.31) | copy-start | bytes 1486852
  132.3 1.6 collective-permute-start.11
  132.6 16.6 %copy-start.15 = (bf16[1,2,88,1408]{3,2,1,0:T(8,128)(2,1)}, bf16[1,2,88,1408]{3,2,1,0:T(8,128)(2,1)S(1)}, u32[]{:S(2)}) copy-start(bf16[1,2,88,1408]{3,2,1,0:T(8,128)(2,1)S(1)} %maximum_bitcast_fusion.10) | copy-start | bytes 1486852
  134.7 46.3 %collective-permute-start.13 = (bf16[88,1408]{1,0:T(8,128)(2,1)}, bf16[88,1408]{1,0:T(8,128)(2,1)}, u32[]{:S(2)}, u32[]{:S(2)}) collective-permute-start(bf16[88,1408]{1,0:T(8,128)(2,1)} %bitcast_select_fusion.15), channel_id=1, source_target_pairs={{0,16},{2,18},{4,20},{6,22},{8,24},{10,26},{12,28},{14,30},{16,0},... | collective-permute-start | bytes 743432 | tf_op jit(solution)/shard_map/ppermute | solution.py:222
  149.1 34.2 %collective-permute-start.16 = (bf16[2,88,1408]{2,1,0:T(8,128)(2,1)}, bf16[2,88,1408]{2,1,0:T(8,128)(2,1)}, u32[]{:S(2)}, u32[]{:S(2)}) collective-permute-start(bf16[2,88,1408]{2,1,0:T(8,128)(2,1)} %fusion.38), channel_id=1, source_target_pairs={{0,8},{2,10},{4,12},{6,14},{8,0},{10,2},{12,4},{14,6},{16,24},{18,... | collective-permute-start | bytes 1486856 | tf_op jit(solution)/shard_map/ppermute | solution.py:222
  156.6 4.6 %slice-start.1 = ((bf16[240,3872]{1,0:T(8,128)(2,1)}), bf16[160,3872]{1,0:T(8,128)(2,1)S(1)}, s32[]{:S(2)}) async-start(bf16[240,3872]{1,0:T(8,128)(2,1)} %gather_fusion.10), calls=%async_computation.4 | async-start | bytes 2539520 | tf_op jit(solution)/shard_map/slice | solution.py:381
  165.6 6.5 %copy-start.4 = (bf16[4,88,2816]{2,1,0:T(8,128)(2,1)S(1)}, bf16[4,88,2816]{2,1,0:T(8,128)(2,1)}, u32[]{:S(2)}) copy-start(bf16[4,88,2816]{2,1,0:T(8,128)(2,1)} %get-tuple-element.74) | copy-start | bytes 5947396
  176.3 3.5 copy-start.7
  176.3 3.5 copy-start.29
  177.8 43.4 %collective-permute-start.12 = (bf16[2,2,88,2816]{3,2,1,0:T(8,128)(2,1)}, bf16[2,2,88,2816]{3,2,1,0:T(8,128)(2,1)S(1)}, u32[]{:S(2)}, u32[]{:S(2)}) collective-permute-start(bf16[2,2,88,2816]{3,2,1,0:T(8,128)(2,1)} %pad_maximum_fusion), channel_id=1, source_target_pairs={{0,4},{2,6},{4,0},{6,2},{8,12},{10,14},{12,8},{14,10},{16,20},{18,... | collective-permute-start | bytes 5947400 | tf_op jit(solution)/shard_map/ppermute | solution.py:222
  178.7 45.4 %collective-permute-start.7 = (bf16[4,88,2112]{2,1,0:T(8,128)(2,1)}, bf16[4,88,2112]{2,1,0:T(8,128)(2,1)S(1)}, u32[]{:S(2)}, u32[]{:S(2)}) collective-permute-start(bf16[4,88,2112]{2,1,0:T(8,128)(2,1)} %get-tuple-element.39), channel_id=1, source_target_pairs={{0,2},{2,0},{4,6},{6,4},{8,10},{10,8},{12,14},{14,12},{16,18},{18,... | collective-permute-start | bytes 4460552 | tf_op jit(solution)/shard_map/ppermute | solution.py:222
  181.6 1.6 collective-permute-start.15
  184.7 5.4 %copy-start.34 = (f32[88]{0:T(128)S(1)}, f32[88]{0:T(128)}, u32[]{:S(2)}) copy-start(f32[88]{0:T(128)} %fusion.94) | copy-start | bytes 1060
  184.7 1.6 collective-permute-start.17
  186.3 15.4 %collective-permute-start.18 = (bf16[88,1408]{1,0:T(8,128)(2,1)S(1)}, bf16[88,1408]{1,0:T(8,128)(2,1)S(1)}, u32[]{:S(2)}, u32[]{:S(2)}) collective-permute-start(bf16[88,1408]{1,0:T(8,128)(2,1)S(1)} %bitcast_select_fusion.13), channel_id=1, source_target_pairs={{0,16},{2,18},{4,20},{6,22},{8,24},{10,26},{12,28},{14,30},{16,0},... | collective-permute-start | bytes 743432 | tf_op jit(solution)/shard_map/ppermute | solution.py:222
  202.3 1.6 collective-permute-start.19
  215.9 8.1 %copy-start.8 = (bf16[4,88,2112]{2,1,0:T(8,128)(2,1)S(1)}, bf16[4,88,2112]{2,1,0:T(8,128)(2,1)}, u32[]{:S(2)}) copy-start(bf16[4,88,2112]{2,1,0:T(8,128)(2,1)} %get-tuple-element.76) | copy-start | bytes 4460548
  222.6 21.4 %collective-permute-start.21 = (bf16[2,88,2816]{2,1,0:T(8,128)(2,1)}, bf16[2,88,2816]{2,1,0:T(8,128)(2,1)}, u32[]{:S(2)}, u32[]{:S(2)}) collective-permute-start(bf16[2,88,2816]{2,1,0:T(8,128)(2,1)} %fusion.17), channel_id=1, source_target_pairs={{0,8},{2,10},{4,12},{6,14},{8,0},{10,2},{12,4},{14,6},{16,24},{18,... | collective-permute-start | bytes 2973704 | tf_op jit(solution)/shard_map/ppermute | solution.py:222
  227.3 41.5 %collective-permute-start.20 = (bf16[2,2,88,2112]{3,2,1,0:T(8,128)(2,1)}, bf16[2,2,88,2112]{3,2,1,0:T(8,128)(2,1)S(1)}, u32[]{:S(2)}, u32[]{:S(2)}) collective-permute-start(bf16[2,2,88,2112]{3,2,1,0:T(8,128)(2,1)} %pad_maximum_fusion.1), channel_id=1, source_target_pairs={{0,4},{2,6},{4,0},{6,2},{8,12},{10,14},{12,8},{14,10},{16,20},{18,... | collective-permute-start | bytes 4460552 | tf_op jit(solution)/shard_map/ppermute | solution.py:222
  227.9 16.1 %copy-start.31 = (pred[2]{0:T(512)(128)(4,1)S(1)}, pred[2]{0:T(512)(128)(4,1)}, u32[]{:S(2)}) copy-start(pred[2]{0:T(512)(128)(4,1)} %get-tuple-element.141) | copy-start | bytes 10
  245.7 1.9 collective-permute-start.22
  247.7 23.9 %collective-permute-start.24 = (bf16[88,2816]{1,0:T(8,128)(2,1)S(1)}, bf16[88,2816]{1,0:T(8,128)(2,1)S(1)}, u32[]{:S(2)}, u32[]{:S(2)}) collective-permute-start(bf16[88,2816]{1,0:T(8,128)(2,1)S(1)} %bitcast_select_fusion.9), channel_id=1, source_target_pairs={{0,16},{2,18},{4,20},{6,22},{8,24},{10,26},{12,28},{14,30},{16,0},... | collective-permute-start | bytes 1486856 | tf_op jit(solution)/shard_map/ppermute | solution.py:222
  268.8 3.5 copy-start.28
  272.2 2.7 collective-permute-start.25
  272.4 24.0 %collective-permute-start.23 = (bf16[2,88,2112]{2,1,0:T(8,128)(2,1)S(1)}, bf16[2,88,2112]{2,1,0:T(8,128)(2,1)S(1)}, u32[]{:S(2)}, u32[]{:S(2)}) collective-permute-start(bf16[2,88,2112]{2,1,0:T(8,128)(2,1)S(1)} %fusion.20), channel_id=1, source_target_pairs={{0,8},{2,10},{4,12},{6,14},{8,0},{10,2},{12,4},{14,6},{16,24},{18,... | collective-permute-start | bytes 2230280 | tf_op jit(solution)/shard_map/ppermute | solution.py:222
  296.9 1.8 collective-permute-start.26
  298.7 23.4 %collective-permute-start.27 = (bf16[88,2112]{1,0:T(8,128)(2,1)S(1)}, bf16[88,2112]{1,0:T(8,128)(2,1)S(1)}, u32[]{:S(2)}, u32[]{:S(2)}) collective-permute-start(bf16[88,2112]{1,0:T(8,128)(2,1)S(1)} %bitcast_select_fusion.10), channel_id=1, source_target_pairs={{0,16},{2,18},{4,20},{6,22},{8,24},{10,26},{12,28},{14,30},{16,0},... | collective-permute-start | bytes 1115144 | tf_op jit(solution)/shard_map/ppermute | solution.py:222
  301.4 21.5 %copy-start.39 = (s32[80]{0:T(128)S(1)}, s32[80]{0:T(128)}, u32[]{:S(2)}) copy-start(s32[80]{0:T(128)} %copy-done.38) | copy-start | bytes 964
  322.8 1.8 collective-permute-start.28
  362.7 7.5 %copy-start.33 = (s32[5]{0:T(128)S(1)}, s32[5]{0:T(128)}, u32[]{:S(2)}) copy-start(s32[5]{0:T(128)} %copy-done.32) | copy-start | bytes 64
  365.1 36.7 %all-to-all-start.2 = ((f32[16,40,484]{2,1,0:T(8,128)}), f32[16,40,484]{2,1,0:T(8,128)S(1)}, u32[]{:S(2)}, u32[]{:S(2)}) async-start(f32[16,40,484]{2,1,0:T(8,128)} %reshape.591), calls=%async_computation.2 | async-start | bytes 2621440 | tf_op jit(solution)/shard_map/all_to_all | solution.py:446
  402.0 2.8 copy-start.1
  (11 other events, 14.1 us)

commit v4 on v3

--- a/solution.py
+++ b/solution.py
@@ -302,6 +302,11 @@
     kept_x, sent_x = zip(
         *[path.split_cores(local[:, :, first * block : (first + size) * block]) for first, size in chunks]
     )
+    owner, window_k, occ_irrep, occ_energy, vir_energy, _ = lax.optimization_barrier(
+        (owner, window_k, occ_irrep, occ_energy, vir_energy, sent_x[0])
+    )
+    k_irrep = occ_irrep[window_k]
+    path.owner, path.k_irrep = owner, k_irrep
     x, leaving_x = [], []
     for leaving in sent_x:
         leaving_x.append(after(leaving, x[-1]) if x else leaving)

time: 411 us -> 409 us (level)
  no operation moved by 1% of the time
where the time goes in v4:
time: 409 us; the launch traced here: 403 us
  Pallas kernels  121 us (30%)
  waiting for transfers between devices  101 us (25%)
  local copies, waits for them, and re-layouts  70.2 us (17%)
  starting transfers between devices  46.3 us (11%)
  other arithmetic  44.3 us (11%)
  matrix products  16.9 us (4%)
    pallas_call x8, Pallas kernels, triples_call(): pl.pallas_call(functools.partial(triples_kernel, last), grid=(groups,), i...  121 us
    ppermute x16, waiting for transfers between devices, across(): return lax.ppermute(x, 'pair', [(t, t ^ bit) for t in range(count)])  60.2 us
    all_to_all x1, waiting for transfers between devices, on_device_scatter(): came = lax.all_to_all(total, 'pair', 0, 0, tiled=True)  31.4 us
    ppermute x16, starting transfers between devices, across(): return lax.ppermute(x, 'pair', [(t, t ^ bit) for t in range(count)])  25.1 us
    select_n x4, other arithmetic, split_cores(): return (jnp.where(same, mine, theirs), jnp.where(same, theirs, mine))  13.1 us
    select_n x4, other arithmetic, block(): return jnp.where(self.from_here(0)[w], pick(kept, beta), pick(came, beta))  10.4 us
    slice x4, local copies, waits for them, and re-layouts, on_device_scatter(): holes = lax.optimization_barrier(amps[1:].transpose(0, 1, 4, 2, 3))  9.81 us
    dot_general x4, matrix products, spread_holes(): return jnp.einsum('wgbqa,ae->wgbqe', hole, spread)  9.33 us
  transfers between devices with their start and end apart: 32, of which 15 were waited for; matrix products, arithmetic and copies ran while one was open for 26% of the time, Pallas kernels for 22%

profile of v4, /device:TPU:12, one launch (start us, length us, event | category | flops | bytes accessed | tf_op | source)
XLA Modules:
  0.0 402.7 jit_solution(4581200390462789333)
XLA Ops:
  0.0 3.8 fusion.95
  3.9 3.0 dynamic-slice_bitcast_fusion.3
  7.6 7.2 %all-to-all-start = ((s32[16,1,128]{2,1,0:T(1,128)}), s32[16,1,128]{2,1,0:T(1,128)S(1)}, u32[]{:S(2)}, u32[]{:S(2)}) async-start(s32[16,1,128]{2,1,0:T(1,128)} %broadcast_in_dim.145), calls=%async_computation | async-start | bytes 16384 | tf_op jit(solution)/shard_map/all_to_all | solution.py:301
  16.4 2.4 slice.255
  18.8 1.6 dynamic-slice_bitcast_fusion
  21.3 2.1 slice.254
  23.4 1.6 copy-done.9
  29.0 2.7 bitcast_select_fusion.6
  36.2 2.1 fusion.43
  44.8 2.5 collective-permute-start.4
  47.4 6.6 %all-to-all-start.1 = ((bf16[16,16,3872]{2,1,0:T(8,128)(2,1)}), bf16[16,16,3872]{2,1,0:T(8,128)(2,1)S(1)}, u32[]{:S(2)}, u32[]{:S(2)}) async-start(bf16[16,16,3872]{2,1,0:T(8,128)(2,1)} %fusion.43), calls=%async_computation.1 | async-start | bytes 4063232 | tf_op jit(solution)/shard_map/all_to_all | solution.py:348
  55.0 1.6 convolution_bitcast_fusion
  58.9 2.0 fusion.8
  61.8 2.8 bitcast_select_fusion.4
  72.2 3.9 bitcast_select_fusion.3
  76.0 3.7 collective-permute-done.4
  79.7 3.0 collective-permute-start.5
  82.7 3.2 dynamic-slice_select_fusion.17
  86.4 26.6 %collective-permute-done.5 = bf16[4,88,1408]{2,1,0:T(8,128)(2,1)S(1)} collective-permute-done((bf16[4,88,1408]{2,1,0:T(8,128)(2,1)S(1)}, bf16[4,88,1408]{2,1,0:T(8,128)(2,1)S(1)}, u32[]{:S(2)}, u32[]{:S(2)}) %collective-permute-start.5) | collective-permute-done | bytes 991264 | tf_op jit(solution)/shard_map/ppermute | solution.py:222
  113.0 1.5 dynamic-slice_select_fusion.23
  116.8 3.8 bitcast_select_fusion
  121.5 6.5 %collective-permute-done.10 = bf16[2,88,1408]{2,1,0:T(8,128)(2,1)S(1)} collective-permute-done((bf16[2,88,1408]{2,1,0:T(8,128)(2,1)S(1)}, bf16[2,88,1408]{2,1,0:T(8,128)(2,1)S(1)}, u32[]{:S(2)}, u32[]{:S(2)}) %collective-permute-start.10) | collective-permute-done | bytes 495648 | tf_op jit(solution)/shard_map/ppermute | solution.py:222
  128.5 1.4 collective-permute-done.11
  130.7 2.5 collective-permute-start.13
  133.2 10.9 %collective-permute-done.8 = bf16[2,2,88,1408]{3,2,1,0:T(8,128)(2,1)S(1)} collective-permute-done((bf16[2,2,88,1408]{3,2,1,0:T(8,128)(2,1)S(1)}, bf16[2,2,88,1408]{3,2,1,0:T(8,128)(2,1)S(1)}, u32[]{:S(2)}, u32[]{:S(2)}) %collective-permute-start.8) | collective-permute-done | bytes 991264 | tf_op jit(solution)/shard_map/ppermute | solution.py:222
  145.8 3.1 gather_fusion.10
  149.9 2.7 squeeze.289
  152.7 2.3 reshape.585
  155.0 2.2 copy.62
  157.2 4.5 %slice.99 = bf16[2,5,16,44,88]{4,3,2,1,0:T(8,128)(2,1)} reshape(bf16[160,3872]{1,0:T(8,128)(2,1)S(1)} %slice-done.1) | data formatting | bytes 2478080 | tf_op jit(solution)/shard_map/slice | solution.py:386
  161.8 5.3 %copy.61 = bf16[2,5,16,44,88]{3,2,4,1,0:T(8,128)(2,1)} copy(bf16[2,5,16,44,88]{4,3,2,1,0:T(8,128)(2,1)} %slice.99) | data formatting | bytes 2478080 | tf_op jit(solution)/shard_map/slice | solution.py:386
  168.3 4.0 dynamic-slice_select_fusion.3
  172.5 1.5 pad_maximum_fusion
  177.2 1.4 collective-permute-done.15
  181.7 4.7 %collective-permute-start.18 = (bf16[88,1408]{1,0:T(8,128)(2,1)S(1)}, bf16[88,1408]{1,0:T(8,128)(2,1)S(1)}, u32[]{:S(2)}, u32[]{:S(2)}) collective-permute-start(bf16[88,1408]{1,0:T(8,128)(2,1)S(1)} %bitcast_select_fusion.13), channel_id=1, source_target_pairs={{0,16},{2,18},{4,20},{6,22},{8,24},{10,26},{12,28},{14,30},{16,0},... | collective-permute-start | bytes 743432 | tf_op jit(solution)/shard_map/ppermute | solution.py:222
  186.9 11.5 %triples.8.refs_9_ = f32[5,88,768]{2,1,0:T(8,128)S(1)} custom-call(f32[1,16]{1,0:T(1,128)S(1)} %get-tuple-element.148.refs_0_, bf16[2,16,88,128]{3,2,1,0:T(8,128)(2,1)S(1)} %bitcast.265, bf16[2,88,1408]{2,1,0:T(8,128)(2,1)S(1)} %pad_maximum_fusion.7.refs_2_, bf16[5,128,768]{2,1,0:T(8,128)(2,1)S(1)} %pad.19.refs_3_, ...), custom_call_target="tpu_custom_call" | custom-call | flops 14879293440 | bytes 5148672 | tf_op jit(solution)/shard_map/triples/pallas_call | solution.py:197
  201.2 11.5 %triples.9.refs_9_ = f32[5,88,768]{2,1,0:T(8,128)S(1)} custom-call(f32[1,16]{1,0:T(1,128)S(1)} %get-tuple-element.149.refs_0_, bf16[2,16,88,128]{3,2,1,0:T(8,128)(2,1)S(1)} %bitcast.266, bf16[2,88,1408]{2,1,0:T(8,128)(2,1)S(1)} %pad_maximum_fusion.7.refs_2_, bf16[5,128,768]{2,1,0:T(8,128)(2,1)S(1)} %pad.19.refs_3_, ...), custom_call_target="tpu_custom_call" | custom-call | flops 14879293440 | bytes 5148672 | tf_op jit(solution)/shard_map/triples/pallas_call | solution.py:197
  212.7 5.2 %collective-permute-done.12 = bf16[2,2,88,2816]{3,2,1,0:T(8,128)(2,1)S(1)} collective-permute-done((bf16[2,2,88,2816]{3,2,1,0:T(8,128)(2,1)}, bf16[2,2,88,2816]{3,2,1,0:T(8,128)(2,1)S(1)}, u32[]{:S(2)}, u32[]{:S(2)}) %collective-permute-start.12) | collective-permute-done | bytes 1982496 | tf_op jit(solution)/shard_map/ppermute | solution.py:222
  217.9 1.4 fusion.17
  219.3 1.5 collective-permute-start.21
  220.7 1.7 dynamic-slice_select_fusion.11
  224.5 11.6 %triples.10.refs_9_ = f32[5,88,768]{2,1,0:T(8,128)S(1)} custom-call(f32[1,16]{1,0:T(1,128)S(1)} %get-tuple-element.146.refs_0_, bf16[2,16,88,128]{3,2,1,0:T(8,128)(2,1)S(1)} %bitcast.263, bf16[2,88,1408]{2,1,0:T(8,128)(2,1)S(1)} %pad_maximum_fusion.8.refs_2_, bf16[5,128,768]{2,1,0:T(8,128)(2,1)S(1)} %pad.19.refs_3_, ...), custom_call_target="tpu_custom_call" | custom-call | flops 14879293440 | bytes 5148672 | tf_op jit(solution)/shard_map/triples/pallas_call | solution.py:197
  236.1 5.1 %collective-permute-done.21 = bf16[2,88,2816]{2,1,0:T(8,128)(2,1)} collective-permute-done((bf16[2,88,2816]{2,1,0:T(8,128)(2,1)}, bf16[2,88,2816]{2,1,0:T(8,128)(2,1)}, u32[]{:S(2)}, u32[]{:S(2)}) %collective-permute-start.21) | collective-permute-done | bytes 991264 | tf_op jit(solution)/shard_map/ppermute | solution.py:222
  241.2 1.6 fusion.14
  243.2 1.7 collective-permute-done.22
  244.9 2.4 collective-permute-start.24
  247.4 11.8 %triples.11.refs_9_ = f32[5,88,768]{2,1,0:T(8,128)S(1)} custom-call(f32[1,16]{1,0:T(1,128)S(1)} %get-tuple-element.147.refs_0_, bf16[2,16,88,128]{3,2,1,0:T(8,128)(2,1)S(1)} %bitcast.264, bf16[2,88,1408]{2,1,0:T(8,128)(2,1)S(1)} %pad_maximum_fusion.8.refs_2_, bf16[5,128,768]{2,1,0:T(8,128)(2,1)S(1)} %pad.19.refs_3_, ...), custom_call_target="tpu_custom_call" | custom-call | flops 14879293440 | bytes 5148672 | tf_op jit(solution)/shard_map/triples/pallas_call | solution.py:197
  259.2 5.3 %fusion.72.refs_4_ = bf16[2,5,32,16,768]{4,3,2,1,0:T(8,128)(2,1)} fusion(bf16[2,5,88,16,44]{4,3,2,1,0:T(8,128)(2,1)S(1)} %bitcast.272, s32[768]{0:T(1024)S(1)} %get-tuple-element.160, pred[768]{0:T(1024)(128)(4,1)S(1)} %iota_compare_fusion.6), kind=kOutput, calls=%fused_computation.197 | convolution fusion | flops 346097664 | bytes 9107200 | tf_op jit(solution)/shard_map/wgbqa,ae->wgbqe/dot_general | solution.py:405
  264.5 1.7 fusion.70.refs_4_
  266.6 2.3 collective-permute-done.24
  269.7 2.5 collective-permute-start.23
  273.0 20.7 %triples.12.refs_9_ = f32[5,88,768]{2,1,0:T(8,128)S(1)} custom-call(f32[1,32]{1,0:T(1,128)S(1)} %get-tuple-element.145.refs_0_, bf16[2,32,88,128]{3,2,1,0:T(8,128)(2,1)S(1)} %bitcast.259, bf16[2,88,2816]{2,1,0:T(8,128)(2,1)S(1)} %pad_maximum_fusion.4.refs_2_, bf16[5,128,768]{2,1,0:T(8,128)(2,1)S(1)} %pad.19.refs_3_, ...), custom_call_target="tpu_custom_call" | custom-call | flops 29758586880 | bytes 10297344 | tf_op jit(solution)/shard_map/triples/pallas_call | solution.py:197
  294.5 1.5 collective-permute-done.26
  296.1 2.7 collective-permute-start.27
  298.8 20.7 %triples.13.refs_9_ = f32[5,88,768]{2,1,0:T(8,128)S(1)} custom-call(f32[1,32]{1,0:T(1,128)S(1)} %get-tuple-element.144.refs_0_, bf16[2,32,88,128]{3,2,1,0:T(8,128)(2,1)S(1)} %bitcast.260, bf16[2,88,2816]{2,1,0:T(8,128)(2,1)S(1)} %pad_maximum_fusion.4.refs_2_, bf16[5,128,768]{2,1,0:T(8,128)(2,1)S(1)} %pad.19.refs_3_, ...), custom_call_target="tpu_custom_call" | custom-call | flops 29758586880 | bytes 10297344 | tf_op jit(solution)/shard_map/triples/pallas_call | solution.py:197
  320.3 1.6 collective-permute-done.28
  322.6 16.0 %triples.14.refs_9_ = f32[5,88,768]{2,1,0:T(8,128)S(1)} custom-call(f32[1,24]{1,0:T(1,128)S(1)} %get-tuple-element.142.refs_0_, bf16[2,24,88,128]{3,2,1,0:T(8,128)(2,1)S(1)} %bitcast.261, bf16[2,88,2112]{2,1,0:T(8,128)(2,1)S(1)} %pad_maximum_fusion.5.refs_2_, bf16[5,128,768]{2,1,0:T(8,128)(2,1)S(1)} %pad.19.refs_3_, ...), custom_call_target="tpu_custom_call" | custom-call | flops 22318940160 | bytes 7723008 | tf_op jit(solution)/shard_map/triples/pallas_call | solution.py:197
  338.5 17.2 %triples.15 = f32[5,768,88]{2,1,0:T(8,128)S(1)} custom-call(f32[1,24]{1,0:T(1,128)S(1)} %get-tuple-element.143.refs_0_, bf16[2,24,88,128]{3,2,1,0:T(8,128)(2,1)S(1)} %bitcast.262, bf16[2,88,2112]{2,1,0:T(8,128)(2,1)S(1)} %pad_maximum_fusion.5.refs_2_, bf16[5,128,768]{2,1,0:T(8,128)(2,1)S(1)} %pad.19.refs_3_, ...), custom_call_target="tpu_custom_call" | custom-call | flops 22318940160 | bytes 7723008 | tf_op jit(solution)/shard_map/triples/pallas_call | solution.py:197
  355.8 1.3 slice.264
  357.1 1.9 reshape.590
  360.1 2.4 reshape.591
  362.5 5.4 %all-to-all-start.2 = ((f32[16,40,484]{2,1,0:T(8,128)}), f32[16,40,484]{2,1,0:T(8,128)S(1)}, u32[]{:S(2)}, u32[]{:S(2)}) async-start(f32[16,40,484]{2,1,0:T(8,128)} %reshape.591), calls=%async_computation.2 | async-start | bytes 2621440 | tf_op jit(solution)/shard_map/all_to_all | solution.py:451
  368.0 31.4 %all-to-all-done.2 = f32[16,40,484]{2,1,0:T(8,128)S(1)} async-done(((f32[16,40,484]{2,1,0:T(8,128)}), f32[16,40,484]{2,1,0:T(8,128)S(1)}, u32[]{:S(2)}, u32[]{:S(2)}) %all-to-all-start.2) | async-done | bytes 1239072 | tf_op jit(solution)/shard_map/all_to_all | solution.py:451
  400.1 2.4 gather_fusion.12
  (272 shorter events, 54.9 us)
Async XLA Ops:
  0.0 36.2 %copy-start = (bf16[5,8,7744]{2,1,0:T(8,128)(2,1)S(1)}, bf16[5,8,7744]{2,1,0:T(8,128)(2,1)}, u32[]{:S(2)}) copy-start(bf16[5,8,7744]{2,1,0:T(8,128)(2,1)} %param.10) | copy-start | bytes 1858564
  3.8 12.1 %copy-start.12 = (bf16[8,88,1408]{2,1,0:T(8,128)(2,1)}, bf16[8,88,1408]{2,1,0:T(8,128)(2,1)S(1)}, u32[]{:S(2)}) copy-start(bf16[8,88,1408]{2,1,0:T(8,128)(2,1)S(1)} %get-tuple-element.82) | copy-start | bytes 5947396
  3.8 3.0 copy-start.30
  3.8 3.0 copy-start.31
  3.9 10.9 %copy-start.25 = (bf16[2,30,30,88]{3,0,2,1:T(2,128)(2,1)S(1)}, bf16[2,30,30,88]{3,0,2,1:T(2,128)(2,1)}, u32[]{:S(2)}) copy-start(bf16[2,30,30,88]{3,0,2,1:T(2,128)(2,1)} %param.12) | copy-start | bytes 950404
  6.9 22.2 %collective-permute-start = (bf16[4,88,1408]{2,1,0:T(8,128)(2,1)}, bf16[4,88,1408]{2,1,0:T(8,128)(2,1)}, u32[]{:S(2)}, u32[]{:S(2)}) collective-permute-start(bf16[4,88,1408]{2,1,0:T(8,128)(2,1)} %dynamic-slice_bitcast_fusion.3), channel_id=1, source_target_pairs={{0,1},{1,0},{2,3},{3,2},{4,5},{5,4},{6,7},{7,6},{8,9},{9,8},{10,11... | collective-permute-start | bytes 2973704 | tf_op jit(solution)/shard_map/ppermute | solution.py:217
  7.6 30.8 %all-to-all-start = ((s32[16,1,128]{2,1,0:T(1,128)}), s32[16,1,128]{2,1,0:T(1,128)S(1)}, u32[]{:S(2)}, u32[]{:S(2)}) async-start(s32[16,1,128]{2,1,0:T(1,128)} %broadcast_in_dim.145), calls=%async_computation | async-start | bytes 16384 | tf_op jit(solution)/shard_map/all_to_all | solution.py:301
  14.7 13.0 %collective-permute-start.14 = (bf16[2,30,30,88]{3,0,2,1:T(2,128)(2,1)S(1)}, bf16[2,30,30,88]{3,0,2,1:T(2,128)(2,1)}, u32[]{:S(2)}, u32[]{:S(2)}) collective-permute-start(bf16[2,30,30,88]{3,0,2,1:T(2,128)(2,1)S(1)} %copy-done.25), channel_id=1, source_target_pairs={{0,1},{1,0},{2,3},{3,2},{4,5},{5,4},{6,7},{7,6},{8,9},{9,8},{10,11... | collective-permute-start | bytes 950408 | tf_op jit(solution)/shard_map/ppermute | solution.py:217
  15.9 45.9 %collective-permute-start.3 = (bf16[4,88,1408]{2,1,0:T(8,128)(2,1)}, bf16[4,88,1408]{2,1,0:T(8,128)(2,1)}, u32[]{:S(2)}, u32[]{:S(2)}) collective-permute-start(bf16[4,88,1408]{2,1,0:T(8,128)(2,1)} %dynamic-slice_bitcast_fusion.2), channel_id=1, source_target_pairs={{0,1},{1,0},{2,3},{3,2},{4,5},{5,4},{6,7},{7,6},{8,9},{9,8},{10,11... | collective-permute-start | bytes 2973704 | tf_op jit(solution)/shard_map/ppermute | solution.py:217
  18.8 2.5 copy-start.5
  21.3 94.4 %collective-permute-start.2 = (bf16[4,88,2816]{2,1,0:T(8,128)(2,1)}, bf16[4,88,2816]{2,1,0:T(8,128)(2,1)}, u32[]{:S(2)}, u32[]{:S(2)}) collective-permute-start(bf16[4,88,2816]{2,1,0:T(8,128)(2,1)} %dynamic-slice_bitcast_fusion), channel_id=1, source_target_pairs={{0,1},{1,0},{2,3},{3,2},{4,5},{5,4},{6,7},{7,6},{8,9},{9,8},{10,11... | collective-permute-start | bytes 5947400 | tf_op jit(solution)/shard_map/ppermute | solution.py:217
  23.4 1.6 copy-start.9
  25.0 4.0 copy-start.14
  26.3 45.9 %collective-permute-start.1 = (bf16[4,88,2112]{2,1,0:T(8,128)(2,1)}, bf16[4,88,2112]{2,1,0:T(8,128)(2,1)}, u32[]{:S(2)}, u32[]{:S(2)}) collective-permute-start(bf16[4,88,2112]{2,1,0:T(8,128)(2,1)} %dynamic-slice_bitcast_fusion.1), channel_id=1, source_target_pairs={{0,1},{1,0},{2,3},{3,2},{4,5},{5,4},{6,7},{7,6},{8,9},{9,8},{10,11... | collective-permute-start | bytes 4460552 | tf_op jit(solution)/shard_map/ppermute | solution.py:217
  29.0 2.7 copy-start.34
  29.0 2.8 copy-start.2
  35.0 6.7 %copy-start.3 = (f32[30]{0:T(128)S(1)}, f32[30]{0:T(128)}, u32[]{:S(2)}) copy-start(f32[30]{0:T(128)} %param.13) | copy-start | bytes 364
  38.8 1.6 copy-start.32
  44.8 9.4 %copy-start.26 = (f32[8,88]{1,0:T(8,128)S(1)}, f32[8,88]{1,0:T(8,128)}, u32[]{:S(2)}) copy-start(f32[8,88]{1,0:T(8,128)} %param.14) | copy-start | bytes 8452
  44.8 10.1 %copy-start.19 = (bf16[2,30,30,88,1]{3,0,2,1,4:T(2,128)(2,1)S(1)}, bf16[2,30,30,88,1]{3,0,2,1,4:T(2,128)(2,1)}, u32[]{:S(2)}) copy-start(bf16[2,30,30,88,1]{3,0,2,1,4:T(2,128)(2,1)} %fusion.41) | copy-start | bytes 950404
  44.8 11.7 %copy-start.29 = (s32[2]{0:T(128)S(1)}, s32[2]{0:T(128)}, u32[]{:S(2)}) copy-start(s32[2]{0:T(128)} %param.19) | copy-start | bytes 28
  44.8 34.9 %collective-permute-start.4 = (bf16[4,88,1408]{2,1,0:T(8,128)(2,1)}, bf16[4,88,1408]{2,1,0:T(8,128)(2,1)}, u32[]{:S(2)}, u32[]{:S(2)}) collective-permute-start(bf16[4,88,1408]{2,1,0:T(8,128)(2,1)} %get-tuple-element.107), channel_id=1, source_target_pairs={{0,2},{2,0},{4,6},{6,4},{8,10},{10,8},{12,14},{14,12},{16,18},{18,... | collective-permute-start | bytes 2973704 | tf_op jit(solution)/shard_map/ppermute | solution.py:222
  47.4 98.4 %all-to-all-start.1 = ((bf16[16,16,3872]{2,1,0:T(8,128)(2,1)}), bf16[16,16,3872]{2,1,0:T(8,128)(2,1)S(1)}, u32[]{:S(2)}, u32[]{:S(2)}) async-start(bf16[16,16,3872]{2,1,0:T(8,128)(2,1)} %fusion.43), calls=%async_computation.1 | async-start | bytes 4063232 | tf_op jit(solution)/shard_map/all_to_all | solution.py:348
  58.9 2.9 copy-start.13
  72.2 7.6 %copy-start.22 = (bf16[4,88,1408]{2,1,0:T(8,128)(2,1)S(1)}, bf16[4,88,1408]{2,1,0:T(8,128)(2,1)}, u32[]{:S(2)}) copy-start(bf16[4,88,1408]{2,1,0:T(8,128)(2,1)} %get-tuple-element.46) | copy-start | bytes 2973700
  72.2 10.5 %copy-start.10 = (bf16[4,88,1408]{2,1,0:T(8,128)(2,1)S(1)}, bf16[4,88,1408]{2,1,0:T(8,128)(2,1)}, u32[]{:S(2)}) copy-start(bf16[4,88,1408]{2,1,0:T(8,128)(2,1)} %get-tuple-element.106) | copy-start | bytes 2973700
  79.7 33.2 %collective-permute-start.5 = (bf16[4,88,1408]{2,1,0:T(8,128)(2,1)S(1)}, bf16[4,88,1408]{2,1,0:T(8,128)(2,1)S(1)}, u32[]{:S(2)}, u32[]{:S(2)}) collective-permute-start(bf16[4,88,1408]{2,1,0:T(8,128)(2,1)S(1)} %copy-done.22), channel_id=1, source_target_pairs={{0,2},{2,0},{4,6},{6,4},{8,10},{10,8},{12,14},{14,12},{16,18},{18,... | collective-permute-start | bytes 2973704 | tf_op jit(solution)/shard_map/ppermute | solution.py:222
  86.0 26.9 %copy-start.11 = (bf16[4,88,1408]{2,1,0:T(8,128)(2,1)S(1)}, bf16[4,88,1408]{2,1,0:T(8,128)(2,1)}, u32[]{:S(2)}) copy-start(bf16[4,88,1408]{2,1,0:T(8,128)(2,1)} %get-tuple-element.104) | copy-start | bytes 2973700
  86.2 28.6 %collective-permute-start.9 = (bf16[2,2,88,1408]{3,2,1,0:T(8,128)(2,1)S(1)}, bf16[2,2,88,1408]{3,2,1,0:T(8,128)(2,1)S(1)}, u32[]{:S(2)}, u32[]{:S(2)}) collective-permute-start(bf16[2,2,88,1408]{3,2,1,0:T(8,128)(2,1)S(1)} %pad_maximum_fusion.2), channel_id=1, source_target_pairs={{0,4},{2,6},{4,0},{6,2},{8,12},{10,14},{12,8},{14,10},{16,20},{18,... | collective-permute-start | bytes 2973704 | tf_op jit(solution)/shard_map/ppermute | solution.py:222
  114.6 2.1 copy-start.6
  115.0 13.0 %collective-permute-start.10 = (bf16[2,88,1408]{2,1,0:T(8,128)(2,1)S(1)}, bf16[2,88,1408]{2,1,0:T(8,128)(2,1)S(1)}, u32[]{:S(2)}, u32[]{:S(2)}) collective-permute-start(bf16[2,88,1408]{2,1,0:T(8,128)(2,1)S(1)} %fusion.27), channel_id=1, source_target_pairs={{0,8},{2,10},{4,12},{6,14},{8,0},{10,2},{12,4},{14,6},{16,24},{18,... | collective-permute-start | bytes 1486856 | tf_op jit(solution)/shard_map/ppermute | solution.py:222
  120.5 23.5 %collective-permute-start.8 = (bf16[2,2,88,1408]{3,2,1,0:T(8,128)(2,1)S(1)}, bf16[2,2,88,1408]{3,2,1,0:T(8,128)(2,1)S(1)}, u32[]{:S(2)}, u32[]{:S(2)}) collective-permute-start(bf16[2,2,88,1408]{3,2,1,0:T(8,128)(2,1)S(1)} %pad_maximum_fusion.3), channel_id=1, source_target_pairs={{0,4},{2,6},{4,0},{6,2},{8,12},{10,14},{12,8},{14,10},{16,20},{18,... | collective-permute-start | bytes 2973704 | tf_op jit(solution)/shard_map/ppermute | solution.py:222
  121.1 47.1 %collective-permute-start.6 = (bf16[4,88,2816]{2,1,0:T(8,128)(2,1)}, bf16[4,88,2816]{2,1,0:T(8,128)(2,1)}, u32[]{:S(2)}, u32[]{:S(2)}) collective-permute-start(bf16[4,88,2816]{2,1,0:T(8,128)(2,1)} %get-tuple-element.47), channel_id=1, source_target_pairs={{0,2},{2,0},{4,6},{6,4},{8,10},{10,8},{12,14},{14,12},{16,18},{18,... | collective-permute-start | bytes 5947400 | tf_op jit(solution)/shard_map/ppermute | solution.py:222
  128.3 16.9 %copy-start.17 = (bf16[2,88,1408]{2,1,0:T(8,128)(2,1)}, bf16[2,88,1408]{2,1,0:T(8,128)(2,1)S(1)}, u32[]{:S(2)}) copy-start(bf16[2,88,1408]{2,1,0:T(8,128)(2,1)S(1)} %fusion.31) | copy-start | bytes 1486852
  128.3 1.6 collective-permute-start.11
  128.5 16.6 %copy-start.15 = (bf16[1,2,88,1408]{3,2,1,0:T(8,128)(2,1)}, bf16[1,2,88,1408]{3,2,1,0:T(8,128)(2,1)S(1)}, u32[]{:S(2)}) copy-start(bf16[1,2,88,1408]{3,2,1,0:T(8,128)(2,1)S(1)} %maximum_bitcast_fusion.10) | copy-start | bytes 1486852
  130.7 45.7 %collective-permute-start.13 = (bf16[88,1408]{1,0:T(8,128)(2,1)}, bf16[88,1408]{1,0:T(8,128)(2,1)}, u32[]{:S(2)}, u32[]{:S(2)}) collective-permute-start(bf16[88,1408]{1,0:T(8,128)(2,1)} %bitcast_select_fusion.15), channel_id=1, source_target_pairs={{0,16},{2,18},{4,20},{6,22},{8,24},{10,26},{12,28},{14,30},{16,0},... | collective-permute-start | bytes 743432 | tf_op jit(solution)/shard_map/ppermute | solution.py:222
  145.1 33.6 %collective-permute-start.16 = (bf16[2,88,1408]{2,1,0:T(8,128)(2,1)}, bf16[2,88,1408]{2,1,0:T(8,128)(2,1)}, u32[]{:S(2)}, u32[]{:S(2)}) collective-permute-start(bf16[2,88,1408]{2,1,0:T(8,128)(2,1)} %fusion.38), channel_id=1, source_target_pairs={{0,8},{2,10},{4,12},{6,14},{8,0},{10,2},{12,4},{14,6},{16,24},{18,... | collective-permute-start | bytes 1486856 | tf_op jit(solution)/shard_map/ppermute | solution.py:222
  152.7 4.6 %slice-start.1 = ((bf16[240,3872]{1,0:T(8,128)(2,1)}), bf16[160,3872]{1,0:T(8,128)(2,1)S(1)}, s32[]{:S(2)}) async-start(bf16[240,3872]{1,0:T(8,128)(2,1)} %gather_fusion.10), calls=%async_computation.4 | async-start | bytes 2539520 | tf_op jit(solution)/shard_map/slice | solution.py:386
  161.8 6.5 %copy-start.4 = (bf16[4,88,2816]{2,1,0:T(8,128)(2,1)S(1)}, bf16[4,88,2816]{2,1,0:T(8,128)(2,1)}, u32[]{:S(2)}) copy-start(bf16[4,88,2816]{2,1,0:T(8,128)(2,1)} %get-tuple-element.84) | copy-start | bytes 5947396
  172.4 2.7 copy-start.7
  174.0 43.9 %collective-permute-start.12 = (bf16[2,2,88,2816]{3,2,1,0:T(8,128)(2,1)}, bf16[2,2,88,2816]{3,2,1,0:T(8,128)(2,1)S(1)}, u32[]{:S(2)}, u32[]{:S(2)}) collective-permute-start(bf16[2,2,88,2816]{3,2,1,0:T(8,128)(2,1)} %pad_maximum_fusion), channel_id=1, source_target_pairs={{0,4},{2,6},{4,0},{6,2},{8,12},{10,14},{12,8},{14,10},{16,20},{18,... | collective-permute-start | bytes 5947400 | tf_op jit(solution)/shard_map/ppermute | solution.py:222
  174.3 46.4 %collective-permute-start.7 = (bf16[4,88,2112]{2,1,0:T(8,128)(2,1)}, bf16[4,88,2112]{2,1,0:T(8,128)(2,1)S(1)}, u32[]{:S(2)}, u32[]{:S(2)}) collective-permute-start(bf16[4,88,2112]{2,1,0:T(8,128)(2,1)} %get-tuple-element.48), channel_id=1, source_target_pairs={{0,2},{2,0},{4,6},{6,4},{8,10},{10,8},{12,14},{14,12},{16,18},{18,... | collective-permute-start | bytes 4460552 | tf_op jit(solution)/shard_map/ppermute | solution.py:222
  175.2 1.2 copy-start.24
  177.0 1.6 collective-permute-start.15
  177.1 1.6 copy-start.16
  177.1 1.6 copy-start.21
  180.1 1.6 collective-permute-start.17
  181.7 16.7 %collective-permute-start.18 = (bf16[88,1408]{1,0:T(8,128)(2,1)S(1)}, bf16[88,1408]{1,0:T(8,128)(2,1)S(1)}, u32[]{:S(2)}, u32[]{:S(2)}) collective-permute-start(bf16[88,1408]{1,0:T(8,128)(2,1)S(1)} %bitcast_select_fusion.13), channel_id=1, source_target_pairs={{0,16},{2,18},{4,20},{6,22},{8,24},{10,26},{12,28},{14,30},{16,0},... | collective-permute-start | bytes 743432 | tf_op jit(solution)/shard_map/ppermute | solution.py:222
  199.0 1.6 collective-permute-start.19
  212.7 8.0 %copy-start.8 = (bf16[4,88,2112]{2,1,0:T(8,128)(2,1)S(1)}, bf16[4,88,2112]{2,1,0:T(8,128)(2,1)}, u32[]{:S(2)}) copy-start(bf16[4,88,2112]{2,1,0:T(8,128)(2,1)} %get-tuple-element.86) | copy-start | bytes 4460548
  219.3 22.0 %collective-permute-start.21 = (bf16[2,88,2816]{2,1,0:T(8,128)(2,1)}, bf16[2,88,2816]{2,1,0:T(8,128)(2,1)}, u32[]{:S(2)}, u32[]{:S(2)}) collective-permute-start(bf16[2,88,2816]{2,1,0:T(8,128)(2,1)} %fusion.17), channel_id=1, source_target_pairs={{0,8},{2,10},{4,12},{6,14},{8,0},{10,2},{12,4},{14,6},{16,24},{18,... | collective-permute-start | bytes 2973704 | tf_op jit(solution)/shard_map/ppermute | solution.py:222
  223.9 42.3 %collective-permute-start.20 = (bf16[2,2,88,2112]{3,2,1,0:T(8,128)(2,1)}, bf16[2,2,88,2112]{3,2,1,0:T(8,128)(2,1)S(1)}, u32[]{:S(2)}, u32[]{:S(2)}) collective-permute-start(bf16[2,2,88,2112]{3,2,1,0:T(8,128)(2,1)} %pad_maximum_fusion.1), channel_id=1, source_target_pairs={{0,4},{2,6},{4,0},{6,2},{8,12},{10,14},{12,8},{14,10},{16,20},{18,... | collective-permute-start | bytes 4460552 | tf_op jit(solution)/shard_map/ppermute | solution.py:222
  242.9 1.9 collective-permute-start.22
  244.9 23.9 %collective-permute-start.24 = (bf16[88,2816]{1,0:T(8,128)(2,1)S(1)}, bf16[88,2816]{1,0:T(8,128)(2,1)S(1)}, u32[]{:S(2)}, u32[]{:S(2)}) collective-permute-start(bf16[88,2816]{1,0:T(8,128)(2,1)S(1)} %bitcast_select_fusion.9), channel_id=1, source_target_pairs={{0,16},{2,18},{4,20},{6,22},{8,24},{10,26},{12,28},{14,30},{16,0},... | collective-permute-start | bytes 1486856 | tf_op jit(solution)/shard_map/ppermute | solution.py:222
  269.5 2.6 collective-permute-start.25
  269.7 24.1 %collective-permute-start.23 = (bf16[2,88,2112]{2,1,0:T(8,128)(2,1)S(1)}, bf16[2,88,2112]{2,1,0:T(8,128)(2,1)S(1)}, u32[]{:S(2)}, u32[]{:S(2)}) collective-permute-start(bf16[2,88,2112]{2,1,0:T(8,128)(2,1)S(1)} %fusion.20), channel_id=1, source_target_pairs={{0,8},{2,10},{4,12},{6,14},{8,0},{10,2},{12,4},{14,6},{16,24},{18,... | collective-permute-start | bytes 2230280 | tf_op jit(solution)/shard_map/ppermute | solution.py:222
  294.2 1.8 collective-permute-start.26
  296.1 23.4 %collective-permute-start.27 = (bf16[88,2112]{1,0:T(8,128)(2,1)S(1)}, bf16[88,2112]{1,0:T(8,128)(2,1)S(1)}, u32[]{:S(2)}, u32[]{:S(2)}) collective-permute-start(bf16[88,2112]{1,0:T(8,128)(2,1)S(1)} %bitcast_select_fusion.10), channel_id=1, source_target_pairs={{0,16},{2,18},{4,20},{6,22},{8,24},{10,26},{12,28},{14,30},{16,0},... | collective-permute-start | bytes 1115144 | tf_op jit(solution)/shard_map/ppermute | solution.py:222
  298.8 21.4 %copy-start.33 = (s32[80]{0:T(128)S(1)}, s32[80]{0:T(128)}, u32[]{:S(2)}) copy-start(s32[80]{0:T(128)} %copy-done.32) | copy-start | bytes 964
  320.1 1.8 collective-permute-start.28
  360.1 7.8 %copy-start.28 = (s32[5]{0:T(128)S(1)}, s32[5]{0:T(128)}, u32[]{:S(2)}) copy-start(s32[5]{0:T(128)} %copy-done.27) | copy-start | bytes 64
  362.5 37.0 %all-to-all-start.2 = ((f32[16,40,484]{2,1,0:T(8,128)}), f32[16,40,484]{2,1,0:T(8,128)S(1)}, u32[]{:S(2)}, u32[]{:S(2)}) async-start(f32[16,40,484]{2,1,0:T(8,128)} %reshape.591), calls=%async_computation.2 | async-start | bytes 2621440 | tf_op jit(solution)/shard_map/all_to_all | solution.py:451
  399.7 2.8 copy-start.1
  (5 other events, 4.7 us)
